TPU v7x, 512 devices: a whole 4x8x8 slice. The times are simulated.
512 devices in a mesh: grp: 16 (over y, core), dev: 32 (over z, x).
Axes of the slice: x: 4, y: 8, z: 8, core: 2. Of those that a mesh axis runs over, the one named last changes fastest.
Arguments:
- basis_values: bfloat16 [2048, 256, 512], P(('grp', 'dev')), may hold values from -1 to 1
- stored_density_blocks: bfloat16 [256, 128, 128], P('dev'), may hold values from -0.5 to 0.5
- device_request: int32 [512, 32, 2], P(('grp', 'dev')), may hold values from -1 to 7, as said below
- batch_blocks: int32 [2048, 16], P(('grp', 'dev')), may hold values from 0 to 63, as said below
- batch_atom: int32 [2048], P(('grp', 'dev')), may hold values from 0 to 999
- point_offset: float32 [3, 2048, 256], P(None, ('grp', 'dev')), may hold values from -8 to 8
- point_weight: float32 [2048, 256], P(('grp', 'dev')), may hold values from 0.02 to 0.5
- exchange_kernel: float32 [2048, 256], P(('grp', 'dev')), may hold values from -3 to -0.3
- atom_xyz: float32 [3, 1000], replicated, may hold values from -15 to 15
Outputs:
- response_hamiltonian: bfloat16 [256, 128, 128], P('dev')
- response_density: float32 [2048, 256], P(('grp', 'dev'))
- multipoles: float32 [4, 1000], replicated
Inputs may be any that keep to these rules, and one draw needn't show every extreme that they name: `device_request`: row d belongs to device d of grp+dev in grp-major order. Each row has exactly 32 entries other than -1, distinct for one owner; in every group one owner is asked for 2 blocks by every device of the group. `batch_blocks`: every entry points to an entry of its device's request row that is not -1.
All inputs are finite; a program needn't handle non-finite values.
Results may differ from a plain program's by a relative error of at most 0.004.
Values may be sent and summed in bfloat16 or wider, within the bound.
No kernel may reach another device: no remote copies, remote signals or barrier semaphores. Data moves between devices by JAX's collectives and lax.ppermute only.
A program may use at most 64 MiB of HBM per device.

v0:
```python
import functools

import jax
import jax.numpy as jnp
from jax import lax
from jax.sharding import Mesh
from jax.sharding import PartitionSpec as P

DEV = ("dev_0", "dev_1")
GRP_DEV = ("grp_0", "grp_1", "dev_0", "dev_1")
GRP = ("grp_0", "grp_1")


HIGH = lax.Precision.HIGHEST


def by_axis(value, axes):
    return functools.reduce(lax.psum, axes, value)


def total_of_pieces(value, axis):
    pieces = lax.all_gather(value, axis)
    return pieces.sum(axis=0)


def far_field(multipoles, centre, offset, atom_xyz):
    gap = centre[:, None, None] + offset[:, :, None] - atom_xyz[:, None, :]
    inverse = lax.rsqrt(gap[0] * gap[0] + gap[1] * gap[1] + gap[2] * gap[2] + 1.0)
    cube = inverse * inverse * inverse
    dipole = multipoles[1] * gap[0] + multipoles[2] * gap[1] + multipoles[3] * gap[2]
    return jnp.sum(multipoles[0] * inverse + dipole * cube, axis=1)


def scaled_rows(values, factor):
    return (values.astype(jnp.float32) * factor[:, None]).astype(jnp.bfloat16)


def pair_terms(scaled, values, rel, tile):
    points = values.shape[0]
    return jnp.einsum(
        "rim,rjn->ijmn",
        scaled.reshape(-1, rel, tile),
        values.reshape(points, rel, tile),
        preferred_element_type=jnp.float32,
    )


def on_device(
    basis_values,
    stored_density_blocks,
    device_request,
    batch_blocks,
    batch_atom,
    point_offset,
    point_weight,
    exchange_kernel,
    atom_xyz,
):
    batches, points, width = basis_values.shape
    own, tile = (stored_density_blocks.shape[0], stored_density_blocks.shape[1])
    rel = width // tile
    wanted = device_request[0]
    owners, capacity = wanted.shape
    positions = owners * capacity
    atoms = atom_xyz.shape[1]
    picked = jnp.take(
        stored_density_blocks,
        jnp.clip(lax.all_to_all(wanted, DEV, split_axis=0, concat_axis=0, tiled=True), 0, own - 1),
        axis=0,
    )
    fetched = lax.all_to_all(picked, DEV, split_axis=0, concat_axis=0, tiled=True)
    fetched = fetched.reshape(positions, tile, tile)

    def density_one(args):
        values, needed = args
        blocks = jnp.take(fetched, needed, axis=0).reshape(rel, rel, tile, tile)
        split = values.reshape(points, rel, tile)
        left = jnp.einsum("rim,ijmn->rijn", split, blocks, preferred_element_type=jnp.float32)
        return jnp.einsum("rijn,rjn->r", left, split.astype(jnp.float32))

    density_field = lax.map(density_one, (basis_values, batch_blocks))
    weighted = density_field * point_weight
    local_parts = jnp.stack(
        [
            jnp.sum(weighted, 1),
            jnp.sum(weighted * point_offset[0], 1),
            jnp.sum(weighted * point_offset[1], 1),
            jnp.sum(weighted * point_offset[2], 1),
        ]
    )
    onehot = (batch_atom[:, None] == jnp.arange(atoms, dtype=jnp.int32)[None, :]).astype(
        jnp.float32
    )
    local_moments = jnp.dot(local_parts, onehot, precision=HIGH)
    centres = jnp.dot(atom_xyz, onehot.T, precision=HIGH)
    xc_part = point_weight * exchange_kernel * density_field
    multipoles = by_axis(local_moments, GRP_DEV)

    def potential_one(args):
        centre, offset = args
        return far_field(multipoles, centre, offset, atom_xyz)

    hartree_part = point_weight * lax.map(
        potential_one, (centres.T, jnp.moveaxis(point_offset, 1, 0))
    )

    def both_one(args):
        values, first, second = args
        stacked = jnp.concatenate([scaled_rows(values, first), scaled_rows(values, second)], axis=0)
        doubled = jnp.concatenate([values, values], axis=0)
        return pair_terms(stacked, doubled, rel, tile)

    terms = lax.map(both_one, (basis_values, xc_part, hartree_part))
    flat_terms = terms.reshape(batches * rel * rel, tile * tile)
    summed = jax.ops.segment_sum(flat_terms, batch_blocks.reshape(-1), num_segments=positions)
    outgoing = summed.astype(jnp.bfloat16).reshape(owners, capacity, tile, tile)
    received, received_ids = (
        lax.all_to_all(outgoing, DEV, split_axis=0, concat_axis=0, tiled=True),
        lax.all_to_all(wanted, DEV, split_axis=0, concat_axis=0, tiled=True),
    )
    owner_onehot = (
        jnp.arange(own, dtype=jnp.int32)[:, None] == received_ids.reshape(1, positions)
    ).astype(jnp.bfloat16)
    owned = jnp.dot(
        owner_onehot, received.reshape(positions, tile * tile), preferred_element_type=jnp.float32
    )
    total = total_of_pieces(owned, GRP)
    hamiltonian = total.astype(jnp.bfloat16).reshape(own, tile, tile)
    return (hamiltonian, density_field, multipoles)


def solution(mesh):
    finer = Mesh(mesh.devices.reshape(8, 2, 8, 4), ("grp_0", "grp_1", "dev_0", "dev_1"))
    placed = (
        P(GRP_DEV, None, None),
        P(DEV, None, None),
        P(GRP_DEV, None, None),
        P(GRP_DEV, None),
        P(GRP_DEV),
        P(None, GRP_DEV, None),
        P(GRP_DEV, None),
        P(GRP_DEV, None),
        P(),
    )
    return jax.shard_map(
        on_device,
        mesh=finer,
        in_specs=placed,
        out_specs=(P(DEV, None, None), P(GRP_DEV, None), P()),
        check_vma=False,
    )
```

profile of v0, /device:TPU:1, one launch (start us, length us, event | category | flops | bytes accessed | tf_op | source)
XLA Modules:
  0.0 323.0 jit_solution(13030260249354573462)
XLA Ops:
  8.0 22.1 %all_to_all.20 = s32[32,1,2]{2,1,0:T(1,128)S(1)} all-to-all(s32[32,1,2]{2,1,0:T(1,128)S(1)} %copy.70), channel_id=1, replica_groups=mesh['grp_0'=8,'grp_1'=2,'dev_0'=8,'dev_1'=4] {'dev_0','dev_1'}, dimensions={0} | all-to-all | bytes 512 | tf_op jit(solution)/shard_map/all_to_all | solution.py:119
  30.5 1.0 gather_fusion.1
  31.5 1.6 broadcast_select_fusion
  33.1 4.9 %all-to-all-start.1 = ((bf16[32,2,128,128]{3,2,1,0:T(8,128)(2,1)}), bf16[32,2,128,128]{3,2,1,0:T(8,128)(2,1)}, u32[]{:S(2)}, u32[]{:S(2)}) async-start(bf16[32,2,128,128]{3,2,1,0:T(8,128)(2,1)} %broadcast_select_fusion), calls=%async_computation.1 | async-start | bytes 4194304 | tf_op jit(solution)/shard_map/all_to_all | solution.py:71
  38.9 46.0 %all-to-all-done.1 = bf16[32,2,128,128]{3,2,1,0:T(8,128)(2,1)} async-done(((bf16[32,2,128,128]{3,2,1,0:T(8,128)(2,1)}), bf16[32,2,128,128]{3,2,1,0:T(8,128)(2,1)}, u32[]{:S(2)}, u32[]{:S(2)}) %all-to-all-start.1) | async-done | bytes 2097184 | tf_op jit(solution)/shard_map/all_to_all | solution.py:71
  84.9 12.6 %while.30 = (s32[]{:T(128)}, f32[4,256]{1,0:T(4,128)S(1)}, bf16[4,256,512]{1,2,0:T(8,128)(2,1)S(1)}, s32[4,16]{1,0:T(4,128)S(1)}, bf16[64,128,128]{2,1,0:T(8,128)(2,1)}, /*index=5*/s32[]{:T(128)}, s32[]{:T(128)}) while((s32[]{:T(128)}, f32[4,256]{1,0:T(4,128)S(1)}, bf16[4,256,512]{1,2,0:T(8,128)(2,1)S(1)}, s32[4,16]{1,0:T(4,128)S(1)}, ...), condition=%wide.region_1.2_spmd, body=%wide.region_0.1_spmd.sunk | while | flops 134874000 | bytes 2629349 | solution.py:81
  85.1 2.2 gather_fusion
  88.3 2.2 gather_fusion
  91.4 2.2 gather_fusion
  94.6 2.2 gather_fusion
  97.8 23.3 %psum.28 = f32[4,1000]{1,0:T(4,128)S(1)} all-reduce(f32[4,1000]{1,0:T(4,128)S(1)} %fusion.25), channel_id=1, replica_groups=mesh['grp_0'=8,'grp_1'=2,'dev_0'=8,'dev_1'=4] {'grp_0'}, use_global_device_ids=true, to_apply=%region_6.7 | all-reduce | flops 4000 | bytes 32000 | tf_op jit(solution)/shard_map/psum | solution.py:18
  121.1 15.2 %psum.29 = f32[4,1000]{1,0:T(4,128)S(1)} all-reduce(f32[4,1000]{1,0:T(4,128)S(1)} %psum.28), channel_id=1, replica_groups=mesh['grp_0'=8,'grp_1'=2,'dev_0'=8,'dev_1'=4] {'grp_1'}, use_global_device_ids=true, to_apply=%region_7.8 | all-reduce | flops 4000 | bytes 32000 | tf_op jit(solution)/shard_map/psum | solution.py:18
  136.3 20.2 %psum.30 = f32[4,1000]{1,0:T(4,128)S(1)} all-reduce(f32[4,1000]{1,0:T(4,128)S(1)} %psum.29), channel_id=1, replica_groups=mesh['grp_0'=8,'grp_1'=2,'dev_0'=8,'dev_1'=4] {'dev_0'}, use_global_device_ids=true, to_apply=%region_8.9 | all-reduce | flops 4000 | bytes 32000 | tf_op jit(solution)/shard_map/psum | solution.py:18
  156.5 13.1 %psum.31 = f32[4,1000]{1,0:T(4,128)S(1)} all-reduce(f32[4,1000]{1,0:T(4,128)S(1)} %psum.30), channel_id=1, replica_groups=mesh['grp_0'=8,'grp_1'=2,'dev_0'=8,'dev_1'=4] {'dev_1'}, use_global_device_ids=true, to_apply=%region_9.10 | all-reduce | flops 4000 | bytes 32000 | tf_op jit(solution)/shard_map/psum | solution.py:18
  169.6 5.8 %while.31 = (s32[]{:T(128)}, f32[4,256]{1,0:T(4,128)S(1)}, f32[4,1000]{1,0:T(4,128)S(1)}, f32[4,3]{1,0:T(4,128)S(1)}, f32[4,3,256]{2,1,0:T(4,128)S(1)}, /*index=5*/f32[3,1000]{1,0:T(4,128)S(1)}, s32[]{:T(128)}, s32[]{:T(128)}) while((s32[]{:T(128)}, f32[4,256]{1,0:T(4,128)S(1)}, f32[4,1000]{1,0:T(4,128)S(1)}, f32[4,3]{1,0:T(4,128)S(1)}, ...), condition=%wide.region_12.13_spmd, body=%wide.region_10.12_spmd.sunk | while | flops 5120514 | bytes 6216429 | solution.py:103
  170.2 0.8 fusion.56
  171.7 0.8 fusion.56
  173.1 0.8 fusion.56
  174.6 0.8 fusion.56
  176.1 9.0 %while.32 = (s32[]{:T(128)}, f32[4,4,4,128,128]{4,3,2,1,0:T(8,128)}, bf16[4,256,512]{1,2,0:T(8,128)(2,1)S(1)}, f32[4,256]{1,0:T(4,128)S(1)}, f32[4,256]{1,0:T(4,128)S(1)}, /*index=5*/s32[]{:T(128)}) while((s32[]{:T(128)}, f32[4,4,4,128,128]{4,3,2,1,0:T(8,128)}, bf16[4,256,512]{1,2,0:T(8,128)(2,1)S(1)}, f32[4,256]{1,0:T(4,128)S(1)}, ...), condition=%wide.region_14.15_spmd, body=%wide.region_13.14_spmd.sunk | while | flops 271187968 | bytes 7870553 | solution.py:113
  177.2 1.1 constant_dynamic-update-slice_fusion.2
  179.5 1.1 constant_dynamic-update-slice_fusion.2
  181.8 1.1 constant_dynamic-update-slice_fusion.2
  184.0 1.1 constant_dynamic-update-slice_fusion.2
  185.1 11.4 %scatter_custom_fusion = f32[64,16384]{1,0:T(8,128)} fusion(s32[64]{0:T(128)S(1)} %reshape.177, f32[8,8,128,128]{3,2,1,0:T(8,128)} %bitcast.161, f32[]{:T(128)} %constant.70.clone.1), kind=kCustom, calls=%fused_computation.45 | custom fusion | flops 1048576 | bytes 8388612 | tf_op jit(solution)/shard_map/scatter-add | solution.py:115
  196.5 2.5 convert_bitcast_fusion
  199.0 1.9 copy.96
  201.0 4.6 %all-to-all-start.2 = ((bf16[32,2,128,128]{3,2,1,0:T(8,128)(2,1)}), bf16[32,2,128,128]{3,2,1,0:T(8,128)(2,1)S(1)}, u32[]{:S(2)}, u32[]{:S(2)}) async-start(bf16[32,2,128,128]{3,2,1,0:T(8,128)(2,1)} %bitcast.158), calls=%async_computation.2 | async-start | bytes 4194304 | tf_op jit(solution)/shard_map/all_to_all | solution.py:118
  207.0 36.5 %all-to-all-done.2 = bf16[32,2,128,128]{3,2,1,0:T(8,128)(2,1)S(1)} async-done(((bf16[32,2,128,128]{3,2,1,0:T(8,128)(2,1)}), bf16[32,2,128,128]{3,2,1,0:T(8,128)(2,1)S(1)}, u32[]{:S(2)}, u32[]{:S(2)}) %all-to-all-start.2) | async-done | bytes 2097184 | tf_op jit(solution)/shard_map/all_to_all | solution.py:118
  243.5 2.1 fusion.20
  245.6 66.0 %all-gather.3.cloned.1.call-done = f32[128,16384]{1,0:T(8,128)} async-done(((f32[8,16384]{1,0:T(8,128)}), f32[128,16384]{1,0:T(8,128)}) %all-gather.3.cloned.1.call-update) | async-done | bytes 8388624 | tf_op jit(solution)/shard_map/all_gather | solution.py:22
  311.6 3.8 %bitcast_reduce_fusion = bf16[8,16384]{1,0:T(8,128)(2,1)S(1)} fusion(f32[128,16384]{1,0:T(8,128)} %all-gather.3.cloned.1.call-done), kind=kLoop, calls=%fused_computation.44 | loop fusion | flops 1966080 | bytes 8650752 | tf_op jit(solution)/shard_map/reduce_sum | solution.py:23
  (125 shorter events, 15.5 us)
Async XLA Ops:
  7.2 23.3 %copy-start = (bf16[8,128,128]{2,1,0:T(8,128)(2,1)S(1)}, bf16[8,128,128]{2,1,0:T(8,128)(2,1)}, u32[]{:S(2)}) copy-start(bf16[8,128,128]{2,1,0:T(8,128)(2,1)} %param.16) | copy-start | bytes 786436
  31.5 6.6 %copy-start.8 = (s32[4,16]{1,0:T(4,128)S(1)}, s32[4,16]{1,0:T(4,128)}, u32[]{:S(2)}) copy-start(s32[4,16]{1,0:T(4,128)} %param.18) | copy-start | bytes 772
  31.5 6.6 %copy-start.4 = (f32[3,4,256]{2,1,0:T(4,128)S(1)}, f32[3,4,256]{2,1,0:T(4,128)}, u32[]{:S(2)}) copy-start(f32[3,4,256]{2,1,0:T(4,128)} %param.20) | copy-start | bytes 36868
  33.1 5.0 %copy-start.1 = (bf16[4,256,512]{2,1,0:T(8,128)(2,1)S(1)}, bf16[4,256,512]{2,1,0:T(8,128)(2,1)}, u32[]{:S(2)}) copy-start(bf16[4,256,512]{2,1,0:T(8,128)(2,1)} %param.15) | copy-start | bytes 3145732
  33.1 5.6 %copy-start.3 = (f32[3,1000]{1,0:T(4,128)S(1)}, f32[3,1000]{1,0:T(4,128)}, u32[]{:S(2)}) copy-start(f32[3,1000]{1,0:T(4,128)} %param.23) | copy-start | bytes 36004
  33.1 5.6 %copy-start.9 = (s32[4]{0:T(128)S(1)}, s32[4]{0:T(128)}, u32[]{:S(2)}) copy-start(s32[4]{0:T(128)} %param.19) | copy-start | bytes 52
  33.1 51.8 %all-to-all-start.1 = ((bf16[32,2,128,128]{3,2,1,0:T(8,128)(2,1)}), bf16[32,2,128,128]{3,2,1,0:T(8,128)(2,1)}, u32[]{:S(2)}, u32[]{:S(2)}) async-start(bf16[32,2,128,128]{3,2,1,0:T(8,128)(2,1)} %broadcast_select_fusion), calls=%async_computation.1 | async-start | bytes 4194304 | tf_op jit(solution)/shard_map/all_to_all | solution.py:71
  84.9 12.6 %copy-start.5 = (f32[4,256]{1,0:T(4,128)S(1)}, f32[4,256]{1,0:T(4,128)}, u32[]{:S(2)}) copy-start(f32[4,256]{1,0:T(4,128)} %param.21) | copy-start | bytes 12292
  84.9 12.6 %copy-start.7 = (f32[4,256]{1,0:T(4,128)S(1)}, f32[4,256]{1,0:T(4,128)}, u32[]{:S(2)}) copy-start(f32[4,256]{1,0:T(4,128)} %param.22) | copy-start | bytes 12292
  97.4 72.2 %copy-start.6 = (f32[4,256]{1,0:T(4,128)}, f32[4,256]{1,0:T(4,128)S(1)}, u32[]{:S(2)}) copy-start(f32[4,256]{1,0:T(4,128)S(1)} %get-tuple-element.87) | copy-start | bytes 12292
  175.5 0.6 copy-start.2
  201.0 42.6 %all-to-all-start.2 = ((bf16[32,2,128,128]{3,2,1,0:T(8,128)(2,1)}), bf16[32,2,128,128]{3,2,1,0:T(8,128)(2,1)S(1)}, u32[]{:S(2)}, u32[]{:S(2)}) async-start(bf16[32,2,128,128]{3,2,1,0:T(8,128)(2,1)} %bitcast.158), calls=%async_computation.2 | async-start | bytes 4194304 | tf_op jit(solution)/shard_map/all_to_all | solution.py:118
  205.6 106.0 %all-gather.3.cloned.1.call-start = ((), (), s32[]{:S(2)}) async-start(), calls=%async_computation.3 | async-start | bytes 8912896 | tf_op jit(solution)/shard_map/all_gather | solution.py:22
Sparse Core Ops, SparseCore 0:
  245.7 65.8 all-gather.2
where the time goes:
time: 324 us; the launch traced here: 323 us
  waiting for transfers between devices  149 us (46%)
  blocking collectives  93.9 us (29%)
  other arithmetic  26.5 us (8%)
  local copies, waits for them, and re-layouts  23.4 us (7%)
  between operations  14.2 us (4%)
  starting transfers between devices  9.6 us (3%)
  matrix products  6.43 us (2%)
    psum x4, blocking collectives, by_axis(): return functools.reduce(lax.psum, axes, value)  71.8 us
    all_gather x1, waiting for transfers between devices, total_of_pieces(): pieces = lax.all_gather(value, axis)  66 us
    all_to_all x1, waiting for transfers between devices, on_device(): lax.all_to_all(picked, DEV, split_axis=0, concat_axis=0, tiled=True)  46 us
    all_to_all x1, waiting for transfers between devices, on_device(): lax.all_to_all(outgoing, DEV, split_axis=0, concat_axis=0, tiled=True)  36.5 us
    all_to_all x1, blocking collectives, on_device(): lax.all_to_all(wanted, DEV, split_axis=0, concat_axis=0, tiled=True)  22.1 us
    scatter-add x1, other arithmetic, on_device(): jax.ops.segment_sum(flat_terms, batch_blocks.reshape(-1), num_segments=po...  11.4 us
    gather x4, local copies, waits for them, and re-layouts, density_one(): blocks = jnp.take(fetched, needed, axis=0).reshape(rel, rel, tile, tile)  8.95 us
  transfers between devices with their start and end apart: 3, of which 3 were waited for; matrix products, arithmetic and copies ran while one was open for 1% of the time, Pallas kernels for 0%

commit v1 on v0

v1 whole, which is shorter than its diff:
```python
import functools

import jax
import jax.numpy as jnp
from jax import lax
from jax.experimental import pallas as pl
from jax.experimental.pallas import tpu as pltpu
from jax.sharding import Mesh
from jax.sharding import PartitionSpec as P

GRP = ("y4", "y2", "c")
DEV = ("z4", "z2", "x")
GRP_DEV = GRP + DEV
SERVE = ("c", "z2", "x")
COLLECT = ("y2", "c", "z2", "x")
SETTLE = ("y4", "z4")

F32 = jnp.float32
BF16 = jnp.bfloat16
MIB = 1024 * 1024
VALUES = 8


def exchange(value, axes):
    return lax.all_to_all(value, axes, split_axis=0, concat_axis=0, tiled=True)


def vmem(count):
    return [pl.BlockSpec(memory_space=pltpu.VMEM)] * count


def smem(count):
    return [pl.BlockSpec(memory_space=pltpu.SMEM)] * count


def place_of(position):
    return (position >> 1) & 7, (position >> 4) * 2 + (position & 1)


def serve_kernel(ids, z4, own, one, two, three, out, held):
    for shift, piece in enumerate((own, one, two, three)):
        held[(z4[0] - shift) & 3] = piece[...]

    def serve_one(n, _):
        for k in range(8):
            block = jnp.maximum(ids[n * 8 + k], 0)
            out[n, k] = held[k // 2, block]
        return 0

    lax.fori_loop(0, out.shape[0], serve_one, 0)


def density_kernel(needed, atom, phi, blocks, weight, offset, rho_out, share_out, wide):
    batches, points, width = phi.shape
    rel = width // 128
    half = blocks.shape[2]
    lane = lax.broadcasted_iota(jnp.int32, (points, 128), 1)
    columns = jnp.zeros((points, 128), F32)
    for b in range(batches):
        for p in range(rel * rel):
            w, k = place_of(needed[b * rel * rel + p])
            i, j = p // rel, p % rel
            for c in range(2):
                wide[b % 2, pl.ds(i * 128 + c * half, half), pl.ds(j * 128, 128)] = blocks[c * 8 + w, k]
        values = phi[b]
        product = jnp.dot(values, wide[b % 2], preferred_element_type=F32) * values.astype(F32)
        folded = product[:, :128]
        for j in range(1, rel):
            folded = folded + product[:, j * 128 : (j + 1) * 128]
        columns = jnp.where(lane == b, jnp.sum(folded, axis=1, keepdims=True), columns)
    rho = columns.T[:batches]
    rho_out[...] = rho
    weighted = rho * weight[...]
    moments = [weighted] + [weighted * offset[k] for k in range(3)]
    spot = lax.broadcasted_iota(jnp.int32, (batches, 128), 1)
    row = lax.broadcasted_iota(jnp.int32, (batches, 128), 0)
    tile = jnp.zeros((batches, 128), F32)
    for k, moment in enumerate(moments):
        tile = jnp.where(spot % VALUES == k, jnp.sum(moment, axis=1, keepdims=True), tile)
    for b in range(batches):
        tile = jnp.where((spot % VALUES == 4) & (row == b), atom[b].astype(F32), tile)
    tile = jnp.where(spot // VALUES == row, tile, 0.0)
    flat = jnp.sum(tile, axis=0, keepdims=True)[:, : batches * VALUES]
    share_out[...] = jnp.broadcast_to(flat, share_out.shape)


def term_kernel(
    needed,
    atom,
    places,
    shares,
    phi,
    rho,
    weight,
    exchange_part,
    offset,
    xyz,
    multipoles_out,
    out,
    rows,
    spread,
    points_at,
    potential,
    total,
):
    batches, points, width = phi.shape
    rel = width // 128
    devices, lanes = rows.shape
    group = devices // shares.shape[0]
    each = batches * VALUES
    atoms = xyz.shape[1]

    rows[...] = jnp.zeros_like(rows)
    for g in range(group):
        rows[g * shares.shape[0] : (g + 1) * shares.shape[0], :each] = shares[:, g * each : (g + 1) * each]
    table = rows[...]
    turned = table.T
    atom_at = lax.broadcasted_iota(jnp.int32, (devices, atoms), 1).astype(F32)
    summed = jnp.zeros((VALUES * 3, atoms), F32)
    for b in range(batches):
        member = table[:, b * VALUES + 4 : b * VALUES + 5] == atom_at
        member = jnp.where(member, 1.0, 0.0).astype(BF16)
        exact = turned[b * VALUES : (b + 1) * VALUES]
        high = exact.astype(BF16)
        rest = exact - high.astype(F32)
        middle = rest.astype(BF16)
        low = (rest - middle.astype(F32)).astype(BF16)
        three = jnp.concatenate([high.astype(F32), middle.astype(F32), low.astype(F32)], axis=0)
        summed = summed + jnp.dot(three.astype(BF16), member, preferred_element_type=F32)
    multipoles = summed[:VALUES] + (summed[VALUES : 2 * VALUES] + summed[2 * VALUES :])
    multipoles_out[...] = multipoles

    chunks = atoms // 128
    for h in range(chunks):
        at = slice(h * 128, (h + 1) * 128)
        for k in range(3):
            spread[k * chunks + h] = jnp.broadcast_to(xyz[k : k + 1, at], (8, 128))
        for k in range(4):
            spread[(3 + k) * chunks + h] = jnp.broadcast_to(multipoles[k : k + 1, at], (8, 128))

    rho_now = rho[...]
    filler = jnp.zeros((128 - 6 * batches, points), F32)
    features = jnp.concatenate(
        [weight[...], exchange_part[...] * rho_now, offset[0], offset[1], offset[2], rho_now, filler], axis=0
    )
    features = features.T
    for b in range(batches):
        for k in range(3):
            at = (2 + k) * batches + b
            spot = features[:, at : at + 1] + places[k, atom[b]]
            points_at[k, b * points // 8 : (b + 1) * points // 8] = jnp.broadcast_to(
                spot, (points, 128)
            ).reshape(points // 8, 8, 128)

    def potential_of(step, _):
        at = pl.ds(step * 8, 8)
        px, py, pz = points_at[0, at], points_at[1, at], points_at[2, at]
        acc = jnp.zeros((8, 8, 128), F32)
        for h in range(chunks):
            gx = px - spread[h][None]
            gy = py - spread[chunks + h][None]
            gz = pz - spread[2 * chunks + h][None]
            inverse = lax.rsqrt(gx * gx + gy * gy + gz * gz + 1.0)
            dipole = (
                spread[4 * chunks + h][None] * gx
                + spread[5 * chunks + h][None] * gy
                + spread[6 * chunks + h][None] * gz
            )
            acc = acc + inverse * (spread[3 * chunks + h][None] + dipole * (inverse * inverse))
        potential[at] = acc
        return 0

    lax.fori_loop(0, batches * points // 64, potential_of, 0)

    total[...] = jnp.zeros_like(total)
    for b in range(batches):
        field = potential[b * points // 8 : (b + 1) * points // 8].reshape(points, 128)
        hartree = jnp.sum(field, axis=1, keepdims=True)
        factor = features[:, b : b + 1] * (features[:, batches + b : batches + b + 1] + hartree)
        values = phi[b]
        scaled = (values.astype(F32) * factor).astype(BF16)
        for i in range(rel):
            term = lax.dot_general(
                scaled[:, i * 128 : (i + 1) * 128],
                values,
                (((0,), (0,)), ((), ())),
                preferred_element_type=F32,
            )
            for j in range(rel):
                q = needed[b * rel * rel + i * rel + j]
                total[q] += term[:, j * 128 : (j + 1) * 128]

    for q in range(total.shape[0]):
        w, k = place_of(q)
        for c in range(2):
            for y2 in range(2):
                first = c * 64 + y2 * 32
                out[(y2 * 2 + c) * 8 + w, k] = total[q, first : first + 32].astype(BF16)


def collect_kernel(ids, y2, received, out, total):
    total[...] = jnp.zeros_like(total)

    def add_one(n, _):
        near = ((n >> 4) ^ y2[0]) * 128 + (n & 15) * 8
        for k in range(8):
            block = jnp.maximum(ids[near + k], 0)
            total[(k // 2) * 8 + block] += received[n, k].astype(F32)
        return 0

    lax.fori_loop(0, received.shape[0], add_one, 0)
    for y4 in range(4):
        for z4 in range(4):
            for h in range(4):
                pair = jnp.concatenate(
                    [total[z4 * 8 + 2 * h + e, y4 * 8 : (y4 + 1) * 8] for e in range(2)], axis=0
                )
                out[y4 * 4 + z4, h * 16 : (h + 1) * 16] = pair.astype(BF16)


def on_device(
    basis_values,
    stored_density_blocks,
    device_request,
    batch_blocks,
    batch_atom,
    point_offset,
    point_weight,
    exchange_kernel,
    atom_xyz,
):
    batches, points, width = basis_values.shape
    own, tile = stored_density_blocks.shape[0], stored_density_blocks.shape[1]
    atoms = atom_xyz.shape[1]
    rel = width // tile
    padded = -(-atoms // 128) * 128
    c, y2, z4 = (lax.axis_index(a) for a in ("c", "y2", "z4"))
    half = tile // 2
    params = pltpu.CompilerParams(vmem_limit_bytes=40 * MIB)

    slab = lax.dynamic_slice_in_dim(stored_density_blocks, c * half, half, axis=1)
    pieces = [slab] + [lax.ppermute(slab, "z4", [(i, (i + s) % 4) for i in range(4)]) for s in (1, 2, 3)]
    wanted = device_request[0].reshape(4, 2, 4, 2).transpose(1, 2, 0, 3).reshape(1, 8, 8)
    wanted = jnp.broadcast_to(wanted, (2, 8, 8)).reshape(16, 8)
    ids = exchange(wanted, SERVE).reshape(-1)
    served = pl.pallas_call(
        serve_kernel,
        name="serve",
        out_shape=jax.ShapeDtypeStruct((16, 8, half, tile), BF16),
        in_specs=smem(2) + vmem(4),
        out_specs=vmem(1)[0],
        scratch_shapes=[pltpu.VMEM((4, own, half, tile), BF16)],
        compiler_params=params,
    )(ids, z4.reshape(1), *pieces)
    blocks = exchange(served, SERVE)
    near_ids = lax.ppermute(ids, "y2", [(0, 1), (1, 0)])
    both_ids = jnp.concatenate([ids, near_ids])

    needed = batch_blocks.reshape(-1)
    each = batches * VALUES
    density, share = pl.pallas_call(
        density_kernel,
        name="density",
        out_shape=(
            jax.ShapeDtypeStruct((batches, points), F32),
            jax.ShapeDtypeStruct((16, each), F32),
        ),
        in_specs=smem(2) + vmem(4),
        out_specs=tuple(vmem(2)),
        scratch_shapes=[pltpu.VMEM((2, width, width), BF16)],
        compiler_params=params,
    )(needed, batch_atom, basis_values, blocks, point_weight, point_offset)

    shares = exchange(share, GRP).reshape(1, 16 * each)
    shares = exchange(jnp.broadcast_to(shares, (32, 16 * each)), DEV)
    far = jnp.pad(atom_xyz, ((0, 0), (0, padded - atoms)))
    multipoles, outgoing = pl.pallas_call(
        term_kernel,
        name="terms",
        out_shape=(
            jax.ShapeDtypeStruct((VALUES, padded), F32),
            jax.ShapeDtypeStruct((32, 8, 32, tile), BF16),
        ),
        in_specs=smem(3) + vmem(7),
        out_specs=tuple(vmem(2)),
        scratch_shapes=[
            pltpu.VMEM((512, 128), F32),
            pltpu.VMEM((7 * padded // 128, 8, 128), F32),
            pltpu.VMEM((3, batches * points // 8, 8, 128), F32),
            pltpu.VMEM((batches * points // 8, 8, 128), F32),
            pltpu.VMEM((64, tile, tile), F32),
        ],
        compiler_params=params,
    )(
        needed,
        batch_atom,
        atom_xyz,
        shares,
        basis_values,
        density,
        point_weight,
        exchange_kernel,
        point_offset,
        far,
    )

    received = exchange(outgoing, COLLECT)
    partial = pl.pallas_call(
        collect_kernel,
        name="collect",
        out_shape=jax.ShapeDtypeStruct((16, own * 8, tile), BF16),
        in_specs=smem(2) + vmem(1),
        out_specs=vmem(1)[0],
        scratch_shapes=[pltpu.VMEM((4 * own, 32, tile), F32)],
        compiler_params=params,
    )(both_ids, y2.reshape(1), received)
    settled = exchange(partial, SETTLE).astype(F32).sum(axis=0).astype(BF16)
    rows = exchange(jnp.broadcast_to(settled[None], (16, own * 8, tile)), GRP)
    rows = rows.reshape(4, 2, 2, own, 8, tile).transpose(3, 2, 1, 0, 4, 5)
    return (rows.reshape(own, tile, tile), density, multipoles[:4, :atoms])


def solution(mesh):
    finer = Mesh(mesh.devices.reshape(4, 2, 2, 4, 2, 4), GRP_DEV)
    placed = (
        P(GRP_DEV, None, None),
        P(DEV, None, None),
        P(GRP_DEV, None, None),
        P(GRP_DEV, None),
        P(GRP_DEV),
        P(None, GRP_DEV, None),
        P(GRP_DEV, None),
        P(GRP_DEV, None),
        P(),
    )
    return jax.shard_map(
        on_device,
        mesh=finer,
        in_specs=placed,
        out_specs=(P(DEV, None, None), P(GRP_DEV, None), P()),
        check_vma=False,
    )
```

time: 324 us -> 182 us (0.56)
  waiting for transfers between devices: 149 us -> 76.5 us
  blocking collectives: 93.9 us -> 28.6 us
  starting transfers between devices: 9.6 us -> 51.9 us
  other arithmetic: 26.5 us -> 1.39 us
  local copies, waits for them, and re-layouts: 23.4 us -> 9.93 us
  between operations: 14.2 us -> 0.87 us
  Pallas kernels: 0 us -> 11.8 us
  matrix products: 6.43 us -> 0 us
    psum x4 -> x0, blocking collectives: 71.8 us -> none  [by_axis(): return functools.reduce(lax.psum, axes, value)]
    all_gather x1 -> x0, waiting for transfers between devices: 66 us -> none  [total_of_pieces(): pieces = lax.all_gather(value, axis)]
    all_to_all x2 -> x5, waiting for transfers between devices: 82.5 us -> 55 us  [exchange(): return lax.all_to_all(value, axes, split_axis=0, concat_axis=0, tiled=True)]
    ppermute x0 -> x4, starting transfers between devices: none -> 22.2 us  [the longest x3 18.9 us: on_device(): lax.ppermute(slab, 'z4', [(i, (i + s) % 4) for i in range(4)])]
    ppermute x0 -> x4, waiting for transfers between devices: none -> 21.5 us  [the longest x1 21.5 us: on_device(): near_ids = lax.ppermute(ids, 'y2', [(0, 1), (1, 0)])]
    all_to_all x2 -> x5, starting transfers between devices: 9.56 us -> 29.7 us  [exchange(): return lax.all_to_all(value, axes, split_axis=0, concat_axis=0, tiled=True)]
    pallas_call x0 -> x4, Pallas kernels: none -> 11.8 us  [the longest x1 6.83 us: on_device(): pl.pallas_call(term_kernel, name='terms', out_shape=(jax.ShapeDtypeStruct...]
    scatter-add x1 -> x0, other arithmetic: 11.4 us -> none  [on_device(): jax.ops.segment_sum(flat_terms, batch_blocks.reshape(-1), num_segments=po...]
  transfers between devices with their start and end apart: 3 -> 9, of which waited for: 3 -> 6; matrix products, arithmetic and copies ran while one was open for 1% -> 2% of each run, Pallas kernels for 0% -> 0%
where the time goes in v1:
time: 182 us; the launch traced here: 181 us
  waiting for transfers between devices  76.5 us (42%)
  starting transfers between devices  51.9 us (29%)
  blocking collectives  28.6 us (16%)
  Pallas kernels  11.8 us (6%)
  local copies, waits for them, and re-layouts  9.93 us (5%)
    all_to_all x5, waiting for transfers between devices, exchange(): return lax.all_to_all(value, axes, split_axis=0, concat_axis=0, tiled=True)  55 us
    all_to_all x5, starting transfers between devices, exchange(): return lax.all_to_all(value, axes, split_axis=0, concat_axis=0, tiled=True)  29.7 us
    all_to_all x2, blocking collectives, exchange(): return lax.all_to_all(value, axes, split_axis=0, concat_axis=0, tiled=True)  28.6 us
    ppermute x1, waiting for transfers between devices, on_device(): near_ids = lax.ppermute(ids, 'y2', [(0, 1), (1, 0)])  21.5 us
    ppermute x3, starting transfers between devices, on_device(): lax.ppermute(slab, 'z4', [(i, (i + s) % 4) for i in range(4)])  18.9 us
    pallas_call x1, Pallas kernels, on_device(): pl.pallas_call(term_kernel, name='terms', out_shape=(jax.ShapeDtypeStruct...  6.83 us
    unnamed x24, local copies, waits for them, and re-layouts  4.4 us
  transfers between devices with their start and end apart: 9, of which 6 were waited for; matrix products, arithmetic and copies ran while one was open for 2% of the time, Pallas kernels for 0%

profile of v1, /device:TPU:1, one launch (start us, length us, event | category | flops | bytes accessed | tf_op | source)
XLA Modules:
  0.0 181.0 jit_solution(4558892736299659108)
XLA Ops:
  0.7 0.9 copy-done
  1.6 6.6 %collective-permute-start.1 = (bf16[8,64,128]{2,1,0:T(8,128)(2,1)S(1)}, bf16[8,64,128]{2,1,0:T(8,128)(2,1)S(1)}, u32[]{:S(2)}, u32[]{:S(2)}) collective-permute-start(bf16[8,64,128]{2,1,0:T(8,128)(2,1)S(1)} %constant_dynamic-slice_fusion.own), channel_id=1, source_target_pairs={{0,8},{8,16},{16,24},{24,0},{1,9},{9,17},{17,25},{25,1},{2,10},{10... | collective-permute-start | bytes 393224 | tf_op jit(solution)/shard_map/ppermute | solution.py:242
  8.2 8.8 %collective-permute-start.2 = (bf16[8,64,128]{2,1,0:T(8,128)(2,1)S(1)}, bf16[8,64,128]{2,1,0:T(8,128)(2,1)S(1)}, u32[]{:S(2)}, u32[]{:S(2)}) collective-permute-start(bf16[8,64,128]{2,1,0:T(8,128)(2,1)S(1)} %constant_dynamic-slice_fusion.own), channel_id=1, source_target_pairs={{0,16},{8,24},{16,0},{24,8},{1,17},{9,25},{17,1},{25,9},{2,18},{10... | collective-permute-start | bytes 393224 | tf_op jit(solution)/shard_map/ppermute | solution.py:242
  17.1 3.4 %collective-permute-start.3 = (bf16[8,64,128]{2,1,0:T(8,128)(2,1)S(1)}, bf16[8,64,128]{2,1,0:T(8,128)(2,1)S(1)}, u32[]{:S(2)}, u32[]{:S(2)}) collective-permute-start(bf16[8,64,128]{2,1,0:T(8,128)(2,1)S(1)} %constant_dynamic-slice_fusion.own), channel_id=1, source_target_pairs={{0,24},{8,0},{16,8},{24,16},{1,25},{9,1},{17,9},{25,17},{2,26},{10... | collective-permute-start | bytes 393224 | tf_op jit(solution)/shard_map/ppermute | solution.py:242
  20.5 0.8 reshape_squeeze.3
  22.0 6.7 %all-to-all-start = ((s32[16,1,8]{2,1,0:T(1,128)}), s32[16,1,8]{2,1,0:T(1,128)S(1)}, u32[]{:S(2)}, u32[]{:S(2)}) async-start(s32[16,1,8]{2,1,0:T(1,128)} %bitcast.1), calls=%async_computation | async-start | bytes 16384 | tf_op jit(solution)/shard_map/all_to_all | solution.py:25
  28.8 5.4 %all-to-all-done = s32[16,1,8]{2,1,0:T(1,128)S(1)} async-done(((s32[16,1,8]{2,1,0:T(1,128)}), s32[16,1,8]{2,1,0:T(1,128)S(1)}, u32[]{:S(2)}, u32[]{:S(2)}) %all-to-all-start) | async-done | bytes 544 | tf_op jit(solution)/shard_map/all_to_all | solution.py:25
  34.7 0.7 reduce.7
  35.5 0.9 serve.1
  36.4 1.3 copy-done.1
  37.7 4.4 %all-to-all-start.1 = ((bf16[16,8,64,128]{3,2,1,0:T(8,128)(2,1)}), bf16[16,8,64,128]{3,2,1,0:T(8,128)(2,1)S(1)}, u32[]{:S(2)}, u32[]{:S(2)}) async-start(bf16[16,8,64,128]{3,2,1,0:T(8,128)(2,1)} %copy-done.1), calls=%async_computation.1 | async-start | bytes 4194304 | tf_op jit(solution)/shard_map/all_to_all | solution.py:25
  42.2 27.4 %all-to-all-done.1.blocks = bf16[16,8,64,128]{3,2,1,0:T(8,128)(2,1)S(1)} async-done(((bf16[16,8,64,128]{3,2,1,0:T(8,128)(2,1)}), bf16[16,8,64,128]{3,2,1,0:T(8,128)(2,1)S(1)}, u32[]{:S(2)}, u32[]{:S(2)}) %all-to-all-start.1) | async-done | bytes 2097184 | tf_op jit(solution)/shard_map/all_to_all | solution.py:25
  69.6 2.3 %density.1 = (f32[4,256]{1,0:T(4,128)}, f32[16,32]{1,0:T(8,128)S(1)}) custom-call(s32[64]{0:T(128)S(1)} %reshape.46.needed, s32[4]{0:T(128)S(1)} %copy-done.9, bf16[4,256,512]{2,1,0:T(8,128)(2,1)S(1)} %copy-done.2, bf16[16,8,64,128]{3,2,1,0:T(8,128)(2,1)S(1)} %all-to-all-done.1.blocks, f32[4,256]{1,0:T(4,128)S(1)} %copy-done.6, f32[3,4,256]{2,1,0:T(4,128)S(1)} %copy-done.5), custom_call_target="tpu_custom_call" | custom-call | tf_op jit(solution)/shard_map/density/pallas_call | solution.py:261
  71.9 14.2 %all_to_all.46 = f32[16,1,32]{2,1,0:T(1,128)S(1)} all-to-all(f32[16,1,32]{2,1,0:T(1,128)S(1)} %bitcast.19), channel_id=1, replica_groups=mesh['y4'=4,'y2'=2,'c'=2,'z4'=4,'z2'=2,'x'=4] {'y4','y2','c'}, dimensions={0} | all-to-all | bytes 4096 | tf_op jit(solution)/shard_map/all_to_all | solution.py:25
  86.6 0.7 reduce.8
  87.3 0.7 broadcast_in_dim.23
  88.0 5.2 %all-to-all-start.3 = ((f32[32,1,512]{2,1,0:T(1,128)}), f32[32,1,512]{2,1,0:T(1,128)S(1)}, u32[]{:S(2)}, u32[]{:S(2)}) async-start(f32[32,1,512]{2,1,0:T(1,128)} %broadcast_in_dim.23), calls=%async_computation.3 | async-start | bytes 131072 | tf_op jit(solution)/shard_map/all_to_all | solution.py:25
  93.3 8.8 %all-to-all-done.3 = f32[32,1,512]{2,1,0:T(1,128)S(1)} async-done(((f32[32,1,512]{2,1,0:T(1,128)}), f32[32,1,512]{2,1,0:T(1,128)S(1)}, u32[]{:S(2)}, u32[]{:S(2)}) %all-to-all-start.3) | async-done | bytes 65568 | tf_op jit(solution)/shard_map/all_to_all | solution.py:25
  102.1 0.7 copy-done.8
  102.7 6.8 %terms.1 = (f32[8,1024]{1,0:T(8,128)S(1)}, bf16[32,8,32,128]{3,2,1,0:T(8,128)(2,1)S(1)}) custom-call(s32[64]{0:T(128)S(1)} %reshape.46.needed, s32[4]{0:T(128)S(1)} %copy-done.9, f32[3,1000]{1,0:T(4,128)S(1)} %copy-done.4, f32[32,512]{1,0:T(8,128)S(1)} %bitcast.18, bf16[4,256,512]{2,1,0:T(8,128)(2,1)S(1)} %copy-done.2, f32[4,256]{1,0:T(4,128)S(1)} %copy-done.8, ...), custom_call_target="tpu_custom_call" | custom-call | tf_op jit(solution)/shard_map/terms/pallas_call | solution.py:277
  109.6 1.3 copy-done.3
  110.9 5.8 %all-to-all-start.4 = ((bf16[32,8,32,128]{3,2,1,0:T(8,128)(2,1)}), bf16[32,8,32,128]{3,2,1,0:T(8,128)(2,1)S(1)}, u32[]{:S(2)}, u32[]{:S(2)}) async-start(bf16[32,8,32,128]{3,2,1,0:T(8,128)(2,1)} %copy-done.3), calls=%async_computation.4 | async-start | bytes 4194304 | tf_op jit(solution)/shard_map/all_to_all | solution.py:25
  116.7 3.4 %collective-permute-start = (s32[128]{0:T(128)S(1)}, s32[128]{0:T(128)S(1)}, u32[]{:S(2)}, u32[]{:S(2)}) collective-permute-start(s32[128]{0:T(128)S(1)} %reshape.44.ids), channel_id=1, source_target_pairs={{0,64},{64,0},{1,65},{65,1},{2,66},{66,2},{3,67},{67,3},{4,68},{68... | collective-permute-start | bytes 1544 | tf_op jit(solution)/shard_map/ppermute | solution.py:256
  120.1 21.5 %collective-permute-done = s32[128]{0:T(128)S(1)} collective-permute-done((s32[128]{0:T(128)S(1)}, s32[128]{0:T(128)S(1)}, u32[]{:S(2)}, u32[]{:S(2)}) %collective-permute-start) | collective-permute-done | bytes 544 | tf_op jit(solution)/shard_map/ppermute | solution.py:256
  141.6 2.3 %all-to-all-done.4.received = bf16[32,8,32,128]{3,2,1,0:T(8,128)(2,1)S(1)} async-done(((bf16[32,8,32,128]{3,2,1,0:T(8,128)(2,1)}), bf16[32,8,32,128]{3,2,1,0:T(8,128)(2,1)S(1)}, u32[]{:S(2)}, u32[]{:S(2)}) %all-to-all-start.4) | async-done | bytes 2097184 | tf_op jit(solution)/shard_map/all_to_all | solution.py:25
  143.9 1.9 %collect.1 = bf16[16,64,128]{2,1,0:T(8,128)(2,1)S(1)} custom-call(s32[256]{0:T(256)S(1)} %pad_add_fusion.ids, s32[1]{0:T(128)} %bitcast.2.y2, bf16[32,8,32,128]{3,2,1,0:T(8,128)(2,1)S(1)} %all-to-all-done.4.received), custom_call_target="tpu_custom_call" | custom-call | tf_op jit(solution)/shard_map/collect/pallas_call | solution.py:308
  145.7 14.5 %all_to_all.47 = bf16[16,64,128]{2,1,0:T(8,128)(2,1)S(1)} all-to-all(bf16[16,64,128]{2,1,0:T(8,128)(2,1)S(1)} %collect.1), channel_id=1, replica_groups=mesh['y4'=4,'y2'=2,'c'=2,'z4'=4,'z2'=2,'x'=4] {'y4','z4'}, dimensions={0} | all-to-all | bytes 524288 | tf_op jit(solution)/shard_map/all_to_all | solution.py:25
  160.3 0.8 broadcast_in_dim.24
  161.0 7.5 %all-to-all-start.6 = ((bf16[16,64,128]{2,1,0:T(8,128)(2,1)}), bf16[16,64,128]{2,1,0:T(8,128)(2,1)S(1)}, u32[]{:S(2)}, u32[]{:S(2)}) async-start(bf16[16,64,128]{2,1,0:T(8,128)(2,1)} %broadcast_in_dim.24), calls=%async_computation.6 | async-start | bytes 524288 | tf_op jit(solution)/shard_map/all_to_all | solution.py:25
  168.6 0.6 slice.3
  169.2 11.1 %all-to-all-done.6 = bf16[16,64,128]{2,1,0:T(8,128)(2,1)S(1)} async-done(((bf16[16,64,128]{2,1,0:T(8,128)(2,1)}), bf16[16,64,128]{2,1,0:T(8,128)(2,1)S(1)}, u32[]{:S(2)}, u32[]{:S(2)}) %all-to-all-start.6) | async-done | bytes 262176 | tf_op jit(solution)/shard_map/all_to_all | solution.py:25
  180.3 0.8 copy.22
  (35 shorter events, 2.2 us)
Async XLA Ops:
  0.6 1.0 copy-start
  1.6 33.9 %collective-permute-start.1 = (bf16[8,64,128]{2,1,0:T(8,128)(2,1)S(1)}, bf16[8,64,128]{2,1,0:T(8,128)(2,1)S(1)}, u32[]{:S(2)}, u32[]{:S(2)}) collective-permute-start(bf16[8,64,128]{2,1,0:T(8,128)(2,1)S(1)} %constant_dynamic-slice_fusion.own), channel_id=1, source_target_pairs={{0,8},{8,16},{16,24},{24,0},{1,9},{9,17},{17,25},{25,1},{2,10},{10... | collective-permute-start | bytes 393224 | tf_op jit(solution)/shard_map/ppermute | solution.py:242
  8.2 27.2 %collective-permute-start.2 = (bf16[8,64,128]{2,1,0:T(8,128)(2,1)S(1)}, bf16[8,64,128]{2,1,0:T(8,128)(2,1)S(1)}, u32[]{:S(2)}, u32[]{:S(2)}) collective-permute-start(bf16[8,64,128]{2,1,0:T(8,128)(2,1)S(1)} %constant_dynamic-slice_fusion.own), channel_id=1, source_target_pairs={{0,16},{8,24},{16,0},{24,8},{1,17},{9,25},{17,1},{25,9},{2,18},{10... | collective-permute-start | bytes 393224 | tf_op jit(solution)/shard_map/ppermute | solution.py:242
  17.1 18.4 %collective-permute-start.3 = (bf16[8,64,128]{2,1,0:T(8,128)(2,1)S(1)}, bf16[8,64,128]{2,1,0:T(8,128)(2,1)S(1)}, u32[]{:S(2)}, u32[]{:S(2)}) collective-permute-start(bf16[8,64,128]{2,1,0:T(8,128)(2,1)S(1)} %constant_dynamic-slice_fusion.own), channel_id=1, source_target_pairs={{0,24},{8,0},{16,8},{24,16},{1,25},{9,1},{17,9},{25,17},{2,26},{10... | collective-permute-start | bytes 393224 | tf_op jit(solution)/shard_map/ppermute | solution.py:242
  22.0 12.2 %all-to-all-start = ((s32[16,1,8]{2,1,0:T(1,128)}), s32[16,1,8]{2,1,0:T(1,128)S(1)}, u32[]{:S(2)}, u32[]{:S(2)}) async-start(s32[16,1,8]{2,1,0:T(1,128)} %bitcast.1), calls=%async_computation | async-start | bytes 16384 | tf_op jit(solution)/shard_map/all_to_all | solution.py:25
  36.3 1.3 copy-start.1
  37.7 4.4 %copy-start.10 = (s32[4,16]{1,0:T(4,128)S(1)}, s32[4,16]{1,0:T(4,128)}, u32[]{:S(2)}) copy-start(s32[4,16]{1,0:T(4,128)} %param.12) | copy-start | bytes 772
  37.7 31.9 %copy-start.2 = (bf16[4,256,512]{2,1,0:T(8,128)(2,1)S(1)}, bf16[4,256,512]{2,1,0:T(8,128)(2,1)}, u32[]{:S(2)}) copy-start(bf16[4,256,512]{2,1,0:T(8,128)(2,1)} %phi.3) | copy-start | bytes 3145732
  37.7 31.9 %copy-start.5 = (f32[3,4,256]{2,1,0:T(4,128)S(1)}, f32[3,4,256]{2,1,0:T(4,128)}, u32[]{:S(2)}) copy-start(f32[3,4,256]{2,1,0:T(4,128)} %offset.3) | copy-start | bytes 36868
  37.7 31.9 %copy-start.6 = (f32[4,256]{1,0:T(4,128)S(1)}, f32[4,256]{1,0:T(4,128)}, u32[]{:S(2)}) copy-start(f32[4,256]{1,0:T(4,128)} %weight.3) | copy-start | bytes 12292
  37.7 31.9 %copy-start.9 = (s32[4]{0:T(128)S(1)}, s32[4]{0:T(128)}, u32[]{:S(2)}) copy-start(s32[4]{0:T(128)} %atom.3) | copy-start | bytes 52
  37.7 31.9 %all-to-all-start.1 = ((bf16[16,8,64,128]{3,2,1,0:T(8,128)(2,1)}), bf16[16,8,64,128]{3,2,1,0:T(8,128)(2,1)S(1)}, u32[]{:S(2)}, u32[]{:S(2)}) async-start(bf16[16,8,64,128]{3,2,1,0:T(8,128)(2,1)} %copy-done.1), calls=%async_computation.1 | async-start | bytes 4194304 | tf_op jit(solution)/shard_map/all_to_all | solution.py:25
  42.1 51.2 %copy-start.4 = (f32[3,1000]{1,0:T(4,128)S(1)}, f32[3,1000]{1,0:T(4,128)}, u32[]{:S(2)}) copy-start(f32[3,1000]{1,0:T(4,128)} %places.1) | copy-start | bytes 36004
  42.1 60.0 %copy-start.7 = (f32[4,256]{1,0:T(4,128)S(1)}, f32[4,256]{1,0:T(4,128)}, u32[]{:S(2)}) copy-start(f32[4,256]{1,0:T(4,128)} %exchange_part.1) | copy-start | bytes 12292
  88.0 14.1 %all-to-all-start.3 = ((f32[32,1,512]{2,1,0:T(1,128)}), f32[32,1,512]{2,1,0:T(1,128)S(1)}, u32[]{:S(2)}, u32[]{:S(2)}) async-start(f32[32,1,512]{2,1,0:T(1,128)} %broadcast_in_dim.23), calls=%async_computation.3 | async-start | bytes 131072 | tf_op jit(solution)/shard_map/all_to_all | solution.py:25
  102.1 0.7 copy-start.8
  109.6 1.3 copy-start.3
  110.9 32.9 %all-to-all-start.4 = ((bf16[32,8,32,128]{3,2,1,0:T(8,128)(2,1)}), bf16[32,8,32,128]{3,2,1,0:T(8,128)(2,1)S(1)}, u32[]{:S(2)}, u32[]{:S(2)}) async-start(bf16[32,8,32,128]{3,2,1,0:T(8,128)(2,1)} %copy-done.3), calls=%async_computation.4 | async-start | bytes 4194304 | tf_op jit(solution)/shard_map/all_to_all | solution.py:25
  116.7 24.9 %collective-permute-start = (s32[128]{0:T(128)S(1)}, s32[128]{0:T(128)S(1)}, u32[]{:S(2)}, u32[]{:S(2)}) collective-permute-start(s32[128]{0:T(128)S(1)} %reshape.44.ids), channel_id=1, source_target_pairs={{0,64},{64,0},{1,65},{65,1},{2,66},{66,2},{3,67},{67,3},{4,68},{68... | collective-permute-start | bytes 1544 | tf_op jit(solution)/shard_map/ppermute | solution.py:256
  161.0 19.2 %all-to-all-start.6 = ((bf16[16,64,128]{2,1,0:T(8,128)(2,1)}), bf16[16,64,128]{2,1,0:T(8,128)(2,1)S(1)}, u32[]{:S(2)}, u32[]{:S(2)}) async-start(bf16[16,64,128]{2,1,0:T(8,128)(2,1)} %broadcast_in_dim.24), calls=%async_computation.6 | async-start | bytes 524288 | tf_op jit(solution)/shard_map/all_to_all | solution.py:25

commit v2 on v1

v2 whole, which is shorter than its diff:
```python
import functools

import jax
import jax.numpy as jnp
from jax import lax
from jax.experimental import pallas as pl
from jax.experimental.pallas import tpu as pltpu
from jax.sharding import Mesh
from jax.sharding import PartitionSpec as P

GRP = ("y4", "y2", "c")
DEV = ("z4", "z2", "x")
GRP_DEV = GRP + DEV
SERVE = ("c", "z2", "x")
COLLECT = ("y2", "c", "z2", "x")
SETTLE = ("y4", "z4")

F32 = jnp.float32
BF16 = jnp.bfloat16
MIB = 1024 * 1024
VALUES = 8


def exchange(value, axes):
    return lax.all_to_all(value, axes, split_axis=0, concat_axis=0, tiled=True)


def vmem(count):
    return [pl.BlockSpec(memory_space=pltpu.VMEM)] * count


def smem(count):
    return [pl.BlockSpec(memory_space=pltpu.SMEM)] * count


def place_of(position):
    return (position >> 1) & 7, (position >> 4) * 2 + (position & 1)


def prepare_kernel(request, stored, message, slab, staged, sems):
    half = slab.shape[1]
    own = stored.at[:, pl.ds(pl.multiple_of(lax.axis_index("c") * half, half), half)]
    load = pltpu.make_async_copy(own, slab, sems.at[0])
    load.start()
    owners, slots = request.shape[1], request.shape[2]
    wide = jnp.pad(request[0], ((0, 128 - owners), (0, 128 - slots))).T
    flat = jnp.concatenate([wide[k : k + 1, :owners] for k in range(slots)], axis=1)
    flat = jnp.concatenate([flat, jnp.zeros((1, staged.shape[2] - owners * slots), jnp.int32)], axis=1)
    for n in range(staged.shape[0]):
        staged[n] = flat
    save = pltpu.make_async_copy(staged, message, sems.at[1])
    save.start()
    save.wait()
    load.wait()


def asked_at(asked, n, w, k):
    return jnp.maximum(asked[n, 0, (k % 2) * 32 + (k // 2) * 8 + w], 0)


def serve_kernel(message, own, one, two, three, out, kept, asked, held, ready, load_sems, sems):
    few = message.at[:, :, pl.ds(0, 128)]
    loads = [pltpu.make_async_copy(few, target, load_sems.at[n]) for n, target in enumerate((asked, kept))]
    for load in loads:
        load.start()
    z4 = lax.axis_index("z4")
    w = lax.axis_index("z2") * 4 + lax.axis_index("x")
    for shift, piece in enumerate((own, one, two, three)):
        held[(z4 - shift) & 3] = piece[...]
    for load in loads:
        load.wait()
    copies = []
    for n in range(ready.shape[0]):
        for k in range(8):
            ready[n, k] = held[k // 2, asked_at(asked, n, w, k)]
        copies.append(pltpu.make_async_copy(ready.at[n], out.at[n], sems.at[n]))
        copies[-1].start()
    for copy in copies:
        copy.wait()


def geometry_kernel(atom, places, offset, xyz, points_far, inverse_far, points_out, inverse_out, sems):
    batches, points = offset.shape[1], offset.shape[2]
    chunks = xyz.shape[1]
    filler = jnp.zeros((128 - 3 * batches, points), F32)
    features = jnp.concatenate([offset[0], offset[1], offset[2], filler], axis=0).T
    for b in range(batches):
        for k in range(3):
            spot = features[:, k * batches + b : k * batches + b + 1] + places[k, atom[b]]
            spot = jnp.broadcast_to(spot, (points, 128)).reshape(points // 8, 8, 128)
            points_out[k, b * points // 8 : (b + 1) * points // 8] = spot

    def inverse_of(step, _):
        at = pl.ds(step * 8, 8)
        px, py, pz = points_out[0, at], points_out[1, at], points_out[2, at]
        for h in range(chunks):
            gx = px - xyz[0, h : h + 1][None]
            gy = py - xyz[1, h : h + 1][None]
            gz = pz - xyz[2, h : h + 1][None]
            inverse_out[h, at] = lax.rsqrt(gx * gx + gy * gy + gz * gz + 1.0)
        return 0

    first = pltpu.make_async_copy(points_out, points_far, sems.at[0])
    first.start()
    lax.fori_loop(0, batches * points // 64, inverse_of, 0)
    second = pltpu.make_async_copy(inverse_out, inverse_far, sems.at[1])
    second.start()
    first.wait()
    second.wait()


def density_kernel(needed, atom, phi, blocks, weight, offset, rho_out, rho_again, share_out, wide):
    batches, points, width = phi.shape
    rel = width // 128
    half = blocks.shape[2]
    lane = lax.broadcasted_iota(jnp.int32, (points, 128), 1)
    columns = jnp.zeros((points, 128), F32)
    for b in range(batches):
        for p in range(rel * rel):
            w, k = place_of(needed[b * rel * rel + p])
            i, j = p // rel, p % rel
            for c in range(2):
                wide[b % 2, pl.ds(i * 128 + c * half, half), pl.ds(j * 128, 128)] = blocks[c * 8 + w, k]
        values = phi[b]
        product = jnp.dot(values, wide[b % 2], preferred_element_type=F32) * values.astype(F32)
        folded = product[:, :128]
        for j in range(1, rel):
            folded = folded + product[:, j * 128 : (j + 1) * 128]
        columns = jnp.where(lane == b, jnp.sum(folded, axis=1, keepdims=True), columns)
    rho = columns.T[:batches]
    rho_out[...] = rho
    rho_again[...] = rho
    weighted = rho * weight[...]
    moments = [weighted] + [weighted * offset[k] for k in range(3)]
    spot = lax.broadcasted_iota(jnp.int32, (batches, 128), 1)
    row = lax.broadcasted_iota(jnp.int32, (batches, 128), 0)
    tile = jnp.zeros((batches, 128), F32)
    for k, moment in enumerate(moments):
        tile = jnp.where(spot % VALUES == k, jnp.sum(moment, axis=1, keepdims=True), tile)
    for b in range(batches):
        mine = row == b
        tile = jnp.where((spot % VALUES == 4) & mine, (atom[b] & 127).astype(F32), tile)
        tile = jnp.where((spot % VALUES == 5) & mine, (atom[b] >> 7).astype(F32), tile)
    tile = jnp.where(spot // VALUES == row, tile, 0.0)
    flat = jnp.sum(tile, axis=0, keepdims=True)[:, : batches * VALUES]
    for n in range(share_out.shape[0]):
        share_out[n] = flat


def relay_kernel(near, out):
    row = jnp.concatenate([near[n] for n in range(near.shape[0])], axis=1)
    for n in range(out.shape[0]):
        out[n] = row


def term_kernel(
    needed,
    shares,
    rho,
    weight,
    exchange_part,
    xyz,
    points_from,
    inverse_from,
    phi_from,
    multipoles_out,
    out,
    points_at,
    inverse,
    phi,
    rows,
    spread,
    potential,
    total,
    ready,
    load_sems,
    sems,
):
    loads = [
        pltpu.make_async_copy(source, target, load_sems.at[n])
        for n, (source, target) in enumerate(((points_from, points_at), (inverse_from, inverse), (phi_from, phi)))
    ]
    for load in loads:
        load.start()
    batches, points, width = phi.shape
    rel = width // 128
    devices = rows.shape[0]
    sources = shares.shape[0]
    each = batches * VALUES
    chunks = xyz.shape[1]

    rows[...] = jnp.zeros_like(rows)
    near = shares[...].reshape(sources, shares.shape[2])
    for g in range(devices // sources):
        rows[g * sources : (g + 1) * sources, :each] = near[:, g * each : (g + 1) * each]
    table = rows[...]
    turned = table.T
    low_at = lax.broadcasted_iota(jnp.int32, (devices, 128), 1).astype(F32)
    high_at = lax.broadcasted_iota(jnp.int32, (chunks, devices), 0).astype(F32)
    summed = jnp.zeros((12 * chunks, 128), F32)
    for b in range(batches):
        low = jnp.where(table[:, b * VALUES + 4 : b * VALUES + 5] == low_at, 1.0, 0.0).astype(BF16)
        high = jnp.where(turned[b * VALUES + 5 : b * VALUES + 6] == high_at, 1.0, 0.0)
        rest = turned[b * VALUES : (b + 1) * VALUES]
        stacked = []
        for _ in range(3):
            part = rest.astype(BF16).astype(F32)
            rest = rest - part
            stacked += [high * part[k : k + 1] for k in range(4)]
        stacked = jnp.concatenate(stacked, axis=0).astype(BF16)
        summed = summed + jnp.dot(stacked, low, preferred_element_type=F32)
    multipoles = [
        summed[k * chunks : (k + 1) * chunks]
        + (summed[(4 + k) * chunks : (5 + k) * chunks] + summed[(8 + k) * chunks : (9 + k) * chunks])
        for k in range(4)
    ]
    for k in range(4):
        multipoles_out[k * chunks : (k + 1) * chunks] = multipoles[k]
    shift = multipoles[1] * xyz[0] + multipoles[2] * xyz[1] + multipoles[3] * xyz[2]
    for k, value in enumerate(multipoles + [shift]):
        for h in range(chunks):
            spread[k * chunks + h] = jnp.broadcast_to(value[h : h + 1], (8, 128))

    loads[0].wait()
    loads[1].wait()

    def potential_of(step, _):
        at = pl.ds(step * 8, 8)
        px, py, pz = points_at[0, at], points_at[1, at], points_at[2, at]
        acc = jnp.zeros((8, 8, 128), F32)
        for h in range(chunks):
            dipole = (
                spread[chunks + h][None] * px
                + spread[2 * chunks + h][None] * py
                + spread[3 * chunks + h][None] * pz
                - spread[4 * chunks + h][None]
            )
            s = inverse[h, at]
            acc = acc + s * (spread[h][None] + dipole * (s * s))
        potential[at] = acc
        return 0

    lax.fori_loop(0, batches * points // 64, potential_of, 0)

    filler = jnp.zeros((128 - 2 * batches, points), F32)
    features = jnp.concatenate([weight[...], exchange_part[...] * rho[...], filler], axis=0).T
    total[...] = jnp.zeros_like(total)
    loads[2].wait()
    for b in range(batches):
        field = potential[b * points // 8 : (b + 1) * points // 8].reshape(points, 128)
        hartree = jnp.sum(field, axis=1, keepdims=True)
        factor = features[:, b : b + 1] * (features[:, batches + b : batches + b + 1] + hartree)
        values = phi[b]
        scaled = (values.astype(F32) * factor).astype(BF16)
        for i in range(rel):
            term = lax.dot_general(
                scaled[:, i * 128 : (i + 1) * 128],
                values,
                (((0,), (0,)), ((), ())),
                preferred_element_type=F32,
            )
            for j in range(rel):
                q = needed[b * rel * rel + i * rel + j]
                total[q] += term[:, j * 128 : (j + 1) * 128]

    copies = []
    for w in range(8):
        for k in range(8):
            q = (k // 2) * 16 + w * 2 + k % 2
            for c in range(2):
                for y2 in range(2):
                    first = c * 64 + y2 * 32
                    ready[(y2 * 2 + c) * 8 + w, k] = total[q, first : first + 32].astype(BF16)
        for d in range(w, 32, 8):
            copies.append(pltpu.make_async_copy(ready.at[d], out.at[d], sems.at[d]))
            copies[-1].start()
    for copy in copies:
        copy.wait()


def collect_kernel(asked, asked_near, received, out, total):
    total[...] = jnp.zeros_like(total)
    w = lax.axis_index("z2") * 4 + lax.axis_index("x")
    y2 = lax.axis_index("y2")

    def add_one(n, _):
        mine = (n >> 4) == y2
        for k in range(8):
            block = jnp.where(mine, asked_at(asked, n & 15, w, k), asked_at(asked_near, n & 15, w, k))
            total[(k // 2) * 8 + block] += received[n, k].astype(F32)
        return 0

    lax.fori_loop(0, received.shape[0], add_one, 0)
    for y4 in range(4):
        for z4 in range(4):
            for h in range(4):
                pair = jnp.concatenate(
                    [total[z4 * 8 + 2 * h + e, y4 * 8 : (y4 + 1) * 8] for e in range(2)], axis=0
                )
                out[y4 * 4 + z4, h * 16 : (h + 1) * 16] = pair.astype(BF16)


def on_device(
    basis_values,
    stored_density_blocks,
    device_request,
    batch_blocks,
    batch_atom,
    point_offset,
    point_weight,
    exchange_kernel,
    atom_xyz,
):
    batches, points, width = basis_values.shape
    own, tile = stored_density_blocks.shape[0], stored_density_blocks.shape[1]
    atoms = atom_xyz.shape[1]
    padded = -(-atoms // 128) * 128
    half = tile // 2
    chunks = padded // 128
    each = batches * VALUES
    groups = batches * points // 8
    params = pltpu.CompilerParams(vmem_limit_bytes=32 * MIB)
    hbm = pl.BlockSpec(memory_space=pltpu.HBM)
    far_away = pl.BlockSpec(memory_space=pl.ANY)

    far = jnp.pad(atom_xyz, ((0, 0), (0, padded - atoms))).reshape(3, chunks, 128)
    points_at, inverse = pl.pallas_call(
        geometry_kernel,
        name="geometry",
        out_shape=(
            pltpu.HBM((3, groups, 8, 128), F32),
            pltpu.HBM((chunks, groups, 8, 128), F32),
        ),
        in_specs=smem(2) + vmem(2),
        out_specs=(hbm, hbm),
        scratch_shapes=[
            pltpu.VMEM((3, groups, 8, 128), F32),
            pltpu.VMEM((chunks, groups, 8, 128), F32),
            pltpu.SemaphoreType.DMA((2,)),
        ],
        compiler_params=params,
        cost_estimate=pl.CostEstimate(flops=2 * 10**7, bytes_accessed=6 * MIB, transcendentals=10**6),
    )(batch_atom, atom_xyz, point_offset, far)

    message, slab = pl.pallas_call(
        prepare_kernel,
        name="prepare",
        out_shape=(pltpu.HBM((16, 1, 2048), jnp.int32), jax.ShapeDtypeStruct((own, half, tile), BF16)),
        in_specs=vmem(1) + [hbm],
        out_specs=(hbm, vmem(1)[0]),
        scratch_shapes=[pltpu.VMEM((16, 1, 2048), jnp.int32), pltpu.SemaphoreType.DMA((2,))],
        compiler_params=params,
    )(device_request, pltpu.with_memory_space_constraint(stored_density_blocks, pltpu.HBM))
    message = exchange(message, SERVE)
    pieces = [slab] + [lax.ppermute(slab, "z4", [(i, (i + s) % 4) for i in range(4)]) for s in (1, 2, 3)]
    served, asked = pl.pallas_call(
        serve_kernel,
        name="serve",
        out_shape=(pltpu.HBM((16, 8, half, tile), BF16), jax.ShapeDtypeStruct((16, 1, 128), jnp.int32)),
        in_specs=[far_away] + vmem(4),
        out_specs=(hbm, vmem(1)[0]),
        scratch_shapes=[
            pltpu.SMEM((16, 1, 128), jnp.int32),
            pltpu.VMEM((4, own, half, tile), BF16),
            pltpu.VMEM((16, 8, half, tile), BF16),
            pltpu.SemaphoreType.DMA((2,)),
            pltpu.SemaphoreType.DMA((16,)),
        ],
        compiler_params=params,
    )(message, *pieces)
    blocks = exchange(served, SERVE)
    asked_near = lax.ppermute(asked, "y2", [(0, 1), (1, 0)])

    needed = batch_blocks.reshape(-1)
    density, density_again, share = pl.pallas_call(
        density_kernel,
        name="density",
        out_shape=(
            jax.ShapeDtypeStruct((batches, points), F32),
            jax.ShapeDtypeStruct((batches, points), F32),
            jax.ShapeDtypeStruct((16, 1, each), F32),
        ),
        in_specs=smem(2) + vmem(4),
        out_specs=tuple(vmem(3)),
        scratch_shapes=[pltpu.VMEM((2, width, width), BF16)],
        compiler_params=params,
    )(needed, batch_atom, basis_values, blocks, point_weight, point_offset)

    shares = pl.pallas_call(
        relay_kernel,
        name="relay",
        out_shape=jax.ShapeDtypeStruct((32, 1, 16 * each), F32),
        in_specs=vmem(1),
        out_specs=vmem(1)[0],
        compiler_params=params,
    )(exchange(share, GRP))
    multipoles, outgoing = pl.pallas_call(
        term_kernel,
        name="terms",
        out_shape=(
            jax.ShapeDtypeStruct((4 * chunks, 128), F32),
            pltpu.HBM((32, 8, 32, tile), BF16),
        ),
        in_specs=smem(1) + vmem(5) + [hbm, hbm, far_away],
        out_specs=(vmem(1)[0], hbm),
        scratch_shapes=[
            pltpu.VMEM(points_at.shape, F32),
            pltpu.VMEM(inverse.shape, F32),
            pltpu.VMEM(basis_values.shape, BF16),
            pltpu.VMEM((512, 128), F32),
            pltpu.VMEM((5 * chunks, 8, 128), F32),
            pltpu.VMEM((groups, 8, 128), F32),
            pltpu.VMEM((64, tile, tile), F32),
            pltpu.VMEM((32, 8, 32, tile), BF16),
            pltpu.SemaphoreType.DMA((3,)),
            pltpu.SemaphoreType.DMA((32,)),
        ],
        compiler_params=params,
    )(
        needed,
        exchange(shares, DEV),
        density_again,
        point_weight,
        exchange_kernel,
        far,
        pltpu.with_memory_space_constraint(points_at, pltpu.HBM),
        pltpu.with_memory_space_constraint(inverse, pltpu.HBM),
        basis_values,
    )

    received = exchange(outgoing, COLLECT)
    partial = pl.pallas_call(
        collect_kernel,
        name="collect",
        out_shape=jax.ShapeDtypeStruct((16, own * 8, tile), BF16),
        in_specs=smem(2) + vmem(1),
        out_specs=vmem(1)[0],
        scratch_shapes=[pltpu.VMEM((4 * own, 32, tile), F32)],
        compiler_params=params,
    )(asked, asked_near, received)
    settled = exchange(partial, SETTLE).astype(F32).sum(axis=0).astype(BF16)
    rows = exchange(jnp.broadcast_to(settled[None], (16, own * 8, tile)), GRP)
    rows = rows.reshape(4, 2, 2, own, 8, tile).transpose(3, 2, 1, 0, 4, 5)
    return (rows.reshape(own, tile, tile), density, multipoles.reshape(4, padded)[:, :atoms])


def solution(mesh):
    finer = Mesh(mesh.devices.reshape(4, 2, 2, 4, 2, 4), GRP_DEV)
    placed = (
        P(GRP_DEV, None, None),
        P(DEV, None, None),
        P(GRP_DEV, None, None),
        P(GRP_DEV, None),
        P(GRP_DEV),
        P(None, GRP_DEV, None),
        P(GRP_DEV, None),
        P(GRP_DEV, None),
        P(),
    )
    return jax.shard_map(
        on_device,
        mesh=finer,
        in_specs=placed,
        out_specs=(P(DEV, None, None), P(GRP_DEV, None), P()),
        check_vma=False,
    )
```

time: 182 us -> 185 us (1.016)
  Pallas kernels: 11.8 us -> 21.6 us
  local copies, waits for them, and re-layouts: 9.93 us -> 3.04 us
    all_to_all x5, waiting for transfers between devices: 55 us -> 44.6 us  [exchange(): return lax.all_to_all(value, axes, split_axis=0, concat_axis=0, tiled=True)]
    ppermute x3, waiting for transfers between devices: 0.01 us -> 10.1 us  [on_device(): lax.ppermute(slab, 'z4', [(i, (i + s) % 4) for i in range(4)])]
    pallas_call x1 -> x4, Pallas kernels: 0.86 us -> 8.69 us  [the longest x1 4.85 us: on_device(): pl.pallas_call(geometry_kernel, name='geometry', out_shape=(pltpu.HBM((3,...]
    all_to_all x5, starting transfers between devices: 29.7 us -> 35.6 us  [exchange(): return lax.all_to_all(value, axes, split_axis=0, concat_axis=0, tiled=True)]
    ppermute x3, starting transfers between devices: 18.9 us -> 14.5 us  [on_device(): lax.ppermute(slab, 'z4', [(i, (i + s) % 4) for i in range(4)])]
    unnamed x24 -> x17, local copies, waits for them, and re-layouts: 4.4 us -> 0.81 us
  transfers between devices with their start and end apart: 9 -> 9, of which waited for: 6 -> 7; matrix products, arithmetic and copies ran while one was open for 2% -> 0% of each run, Pallas kernels for 0% -> 3%
where the time goes in v2:
time: 185 us; the launch traced here: 184 us
  waiting for transfers between devices  76.3 us (41%)
  starting transfers between devices  53.6 us (29%)
  blocking collectives  29 us (16%)
  Pallas kernels  21.6 us (12%)
  local copies, waits for them, and re-layouts  3.04 us (2%)
    all_to_all x5, waiting for transfers between devices, exchange(): return lax.all_to_all(value, axes, split_axis=0, concat_axis=0, tiled=True)  44.6 us
    all_to_all x5, starting transfers between devices, exchange(): return lax.all_to_all(value, axes, split_axis=0, concat_axis=0, tiled=True)  35.6 us
    all_to_all x2, blocking collectives, exchange(): return lax.all_to_all(value, axes, split_axis=0, concat_axis=0, tiled=True)  29 us
    ppermute x1, waiting for transfers between devices, on_device(): asked_near = lax.ppermute(asked, 'y2', [(0, 1), (1, 0)])  21.7 us
    ppermute x3, starting transfers between devices, on_device(): lax.ppermute(slab, 'z4', [(i, (i + s) % 4) for i in range(4)])  14.5 us
    ppermute x3, waiting for transfers between devices, on_device(): lax.ppermute(slab, 'z4', [(i, (i + s) % 4) for i in range(4)])  10.1 us
    pallas_call x1, Pallas kernels, on_device(): pl.pallas_call(term_kernel, name='terms', out_shape=(jax.ShapeDtypeStruct...  8.29 us
    pallas_call x1, Pallas kernels, on_device(): pl.pallas_call(geometry_kernel, name='geometry', out_shape=(pltpu.HBM((3,...  4.85 us
  transfers between devices with their start and end apart: 9, of which 7 were waited for; matrix products, arithmetic and copies ran while one was open for 0% of the time, Pallas kernels for 3%

profile of v2, /device:TPU:1, one launch (start us, length us, event | category | flops | bytes accessed | tf_op | source)
XLA Modules:
  0.0 184.4 jit_solution(8533206691126697803)
XLA Ops:
  0.6 0.8 copy.14.request
  1.4 0.9 prepare.1
  2.3 10.2 %all-to-all-start = ((s32[16,1,2048]{2,1,0:T(1,128)}), s32[16,1,2048]{2,1,0:T(1,128)S(1)}, u32[]{:S(2)}, u32[]{:S(2)}) async-start(s32[16,1,2048]{2,1,0:T(1,128)} %get-tuple-element.14), calls=%async_computation | async-start | bytes 262144 | tf_op jit(solution)/shard_map/all_to_all | solution.py:25
  12.6 3.2 %collective-permute-start = (bf16[8,64,128]{2,1,0:T(8,128)(2,1)S(1)}, bf16[8,64,128]{2,1,0:T(8,128)(2,1)S(1)}, u32[]{:S(2)}, u32[]{:S(2)}) collective-permute-start(bf16[8,64,128]{2,1,0:T(8,128)(2,1)S(1)} %get-tuple-element.15.own), channel_id=1, source_target_pairs={{0,8},{8,16},{16,24},{24,0},{1,9},{9,17},{17,25},{25,1},{2,10},{10... | collective-permute-start | bytes 393224 | tf_op jit(solution)/shard_map/ppermute | solution.py:355
  15.8 7.9 %collective-permute-start.1 = (bf16[8,64,128]{2,1,0:T(8,128)(2,1)S(1)}, bf16[8,64,128]{2,1,0:T(8,128)(2,1)S(1)}, u32[]{:S(2)}, u32[]{:S(2)}) collective-permute-start(bf16[8,64,128]{2,1,0:T(8,128)(2,1)S(1)} %get-tuple-element.15.own), channel_id=1, source_target_pairs={{0,16},{8,24},{16,0},{24,8},{1,17},{9,25},{17,1},{25,9},{2,18},{10... | collective-permute-start | bytes 393224 | tf_op jit(solution)/shard_map/ppermute | solution.py:355
  23.8 3.4 %collective-permute-start.2 = (bf16[8,64,128]{2,1,0:T(8,128)(2,1)S(1)}, bf16[8,64,128]{2,1,0:T(8,128)(2,1)S(1)}, u32[]{:S(2)}, u32[]{:S(2)}) collective-permute-start(bf16[8,64,128]{2,1,0:T(8,128)(2,1)S(1)} %get-tuple-element.15.own), channel_id=1, source_target_pairs={{0,24},{8,0},{16,8},{24,16},{1,25},{9,1},{17,9},{25,17},{2,26},{10... | collective-permute-start | bytes 393224 | tf_op jit(solution)/shard_map/ppermute | solution.py:355
  27.2 5.5 %collective-permute-done.1.two = bf16[8,64,128]{2,1,0:T(8,128)(2,1)S(1)} collective-permute-done((bf16[8,64,128]{2,1,0:T(8,128)(2,1)S(1)}, bf16[8,64,128]{2,1,0:T(8,128)(2,1)S(1)}, u32[]{:S(2)}, u32[]{:S(2)}) %collective-permute-start.1) | collective-permute-done | bytes 131104 | tf_op jit(solution)/shard_map/ppermute | solution.py:355
  32.7 4.6 %collective-permute-done.2.three = bf16[8,64,128]{2,1,0:T(8,128)(2,1)S(1)} collective-permute-done((bf16[8,64,128]{2,1,0:T(8,128)(2,1)S(1)}, bf16[8,64,128]{2,1,0:T(8,128)(2,1)S(1)}, u32[]{:S(2)}, u32[]{:S(2)}) %collective-permute-start.2) | collective-permute-done | bytes 131104 | tf_op jit(solution)/shard_map/ppermute | solution.py:355
  37.2 2.2 %serve.1 = (bf16[16,8,64,128]{3,2,1,0:T(8,128)(2,1)}, s32[16,1,128]{2,1,0:T(1,128)S(1)}) custom-call(s32[16,1,2048]{2,1,0:T(1,128)S(1)} %all-to-all-done.message, bf16[8,64,128]{2,1,0:T(8,128)(2,1)S(1)} %get-tuple-element.15.own, bf16[8,64,128]{2,1,0:T(8,128)(2,1)S(1)} %collective-permute-done.one, bf16[8,64,128]{2,1,0:T(8,128)(2,1)S(1)} %collective-permute-done.1.two, ...), custom_call_target="tpu_custom_call" | custom-call | tf_op jit(solution)/shard_map/serve/pallas_call | solution.py:356
  39.4 0.0 copy-start.6
  39.5 0.0 copy-start
  39.5 4.9 %all-to-all-start.1 = ((bf16[16,8,64,128]{3,2,1,0:T(8,128)(2,1)}), bf16[16,8,64,128]{3,2,1,0:T(8,128)(2,1)S(1)}, u32[]{:S(2)}, u32[]{:S(2)}) async-start(bf16[16,8,64,128]{3,2,1,0:T(8,128)(2,1)} %get-tuple-element.17), calls=%async_computation.1 | async-start | bytes 4194304 | tf_op jit(solution)/shard_map/all_to_all | solution.py:25
  44.4 0.1 reshape.22.needed
  44.5 27.4 %all-to-all-done.1.blocks = bf16[16,8,64,128]{3,2,1,0:T(8,128)(2,1)S(1)} async-done(((bf16[16,8,64,128]{3,2,1,0:T(8,128)(2,1)}), bf16[16,8,64,128]{3,2,1,0:T(8,128)(2,1)S(1)}, u32[]{:S(2)}, u32[]{:S(2)}) %all-to-all-start.1) | async-done | bytes 2097184 | tf_op jit(solution)/shard_map/all_to_all | solution.py:25
  72.0 2.3 %density.1 = (f32[4,256]{1,0:T(4,128)}, f32[4,256]{1,0:T(4,128)S(1)}, f32[16,1,32]{2,1,0:T(1,128)S(1)}) custom-call(s32[64]{0:T(128)S(1)} %reshape.22.needed, s32[4]{0:T(128)S(1)} %copy-done.5, bf16[4,256,512]{2,1,0:T(8,128)(2,1)S(1)} %copy-done, bf16[16,8,64,128]{3,2,1,0:T(8,128)(2,1)S(1)} %all-to-all-done.1.blocks, f32[4,256]{1,0:T(4,128)S(1)} %copy-done.2, ...), custom_call_target="tpu_custom_call" | custom-call | tf_op jit(solution)/shard_map/density/pallas_call | solution.py:375
  74.3 14.1 %all_to_all.35.near = f32[16,1,32]{2,1,0:T(1,128)S(1)} all-to-all(f32[16,1,32]{2,1,0:T(1,128)S(1)} %get-tuple-element.18), channel_id=1, replica_groups=mesh['y4'=4,'y2'=2,'c'=2,'z4'=4,'z2'=2,'x'=4] {'y4','y2','c'}, dimensions={0} | all-to-all | bytes 4096 | tf_op jit(solution)/shard_map/all_to_all | solution.py:25
  88.4 0.7 relay.1
  89.1 7.1 %all-to-all-start.3 = ((f32[32,1,512]{2,1,0:T(1,128)}), f32[32,1,512]{2,1,0:T(1,128)S(1)}, u32[]{:S(2)}, u32[]{:S(2)}) async-start(f32[32,1,512]{2,1,0:T(1,128)} %relay.1), calls=%async_computation.3 | async-start | bytes 131072 | tf_op jit(solution)/shard_map/all_to_all | solution.py:25
  96.3 4.9 %geometry.1 = (f32[3,128,8,128]{3,2,1,0:T(8,128)}, f32[8,128,8,128]{3,2,1,0:T(8,128)}) custom-call(s32[4]{0:T(128)S(1)} %copy-done.5, f32[3,1000]{1,0:T(4,128)S(1)} %copy-done.1, f32[3,4,256]{2,1,0:T(4,128)S(1)} %copy-done.3, f32[3,8,128]{2,1,0:T(8,128)S(1)} %bitcast.10), custom_call_target="tpu_custom_call" | custom-call | flops 20000000 | bytes 6291456 | tf_op jit(solution)/shard_map/geometry/pallas_call | solution.py:327
  101.1 3.9 %all-to-all-done.3.shares = f32[32,1,512]{2,1,0:T(1,128)S(1)} async-done(((f32[32,1,512]{2,1,0:T(1,128)}), f32[32,1,512]{2,1,0:T(1,128)S(1)}, u32[]{:S(2)}, u32[]{:S(2)}) %all-to-all-start.3) | async-done | bytes 65568 | tf_op jit(solution)/shard_map/all_to_all | solution.py:25
  105.0 8.3 %terms.1 = (f32[32,128]{1,0:T(8,128)S(1)}, bf16[32,8,32,128]{3,2,1,0:T(8,128)(2,1)}) custom-call(s32[64]{0:T(128)S(1)} %reshape.22.needed, f32[32,1,512]{2,1,0:T(1,128)S(1)} %all-to-all-done.3.shares, f32[4,256]{1,0:T(4,128)S(1)} %get-tuple-element.19.rho, f32[4,256]{1,0:T(4,128)S(1)} %copy-done.2, f32[4,256]{1,0:T(4,128)S(1)} %copy-done.4, ...), custom_call_target="tpu_custom_call" | custom-call | tf_op jit(solution)/shard_map/terms/pallas_call | solution.py:397
  113.3 5.8 %all-to-all-start.4 = ((bf16[32,8,32,128]{3,2,1,0:T(8,128)(2,1)}), bf16[32,8,32,128]{3,2,1,0:T(8,128)(2,1)S(1)}, u32[]{:S(2)}, u32[]{:S(2)}) async-start(bf16[32,8,32,128]{3,2,1,0:T(8,128)(2,1)} %get-tuple-element.22), calls=%async_computation.4 | async-start | bytes 4194304 | tf_op jit(solution)/shard_map/all_to_all | solution.py:25
  119.2 3.4 %collective-permute-start.3 = (s32[16,1,128]{2,1,0:T(1,128)S(1)}, s32[16,1,128]{2,1,0:T(1,128)S(1)}, u32[]{:S(2)}, u32[]{:S(2)}) collective-permute-start(s32[16,1,128]{2,1,0:T(1,128)S(1)} %get-tuple-element.16.asked), channel_id=1, source_target_pairs={{0,64},{64,0},{1,65},{65,1},{2,66},{66,2},{3,67},{67,3},{4,68},{68... | collective-permute-start | bytes 24584 | tf_op jit(solution)/shard_map/ppermute | solution.py:372
  122.6 21.7 %collective-permute-done.3.asked_near = s32[16,1,128]{2,1,0:T(1,128)S(1)} collective-permute-done((s32[16,1,128]{2,1,0:T(1,128)S(1)}, s32[16,1,128]{2,1,0:T(1,128)S(1)}, u32[]{:S(2)}, u32[]{:S(2)}) %collective-permute-start.3) | collective-permute-done | bytes 8224 | tf_op jit(solution)/shard_map/ppermute | solution.py:372
  144.2 2.1 %all-to-all-done.4.received = bf16[32,8,32,128]{3,2,1,0:T(8,128)(2,1)S(1)} async-done(((bf16[32,8,32,128]{3,2,1,0:T(8,128)(2,1)}), bf16[32,8,32,128]{3,2,1,0:T(8,128)(2,1)S(1)}, u32[]{:S(2)}, u32[]{:S(2)}) %all-to-all-start.4) | async-done | bytes 2097184 | tf_op jit(solution)/shard_map/all_to_all | solution.py:25
  146.3 2.3 %collect.1 = bf16[16,64,128]{2,1,0:T(8,128)(2,1)S(1)} custom-call(s32[16,1,128]{2,1,0:T(1,128)S(1)} %get-tuple-element.16.asked, s32[16,1,128]{2,1,0:T(1,128)S(1)} %collective-permute-done.3.asked_near, bf16[32,8,32,128]{3,2,1,0:T(8,128)(2,1)S(1)} %all-to-all-done.4.received), custom_call_target="tpu_custom_call" | custom-call | tf_op jit(solution)/shard_map/collect/pallas_call | solution.py:432
  148.6 14.9 %all_to_all.36 = bf16[16,64,128]{2,1,0:T(8,128)(2,1)S(1)} all-to-all(bf16[16,64,128]{2,1,0:T(8,128)(2,1)S(1)} %collect.1), channel_id=1, replica_groups=mesh['y4'=4,'y2'=2,'c'=2,'z4'=4,'z2'=2,'x'=4] {'y4','z4'}, dimensions={0} | all-to-all | bytes 524288 | tf_op jit(solution)/shard_map/all_to_all | solution.py:25
  163.6 0.8 broadcast_in_dim.2
  164.3 7.6 %all-to-all-start.6 = ((bf16[16,64,128]{2,1,0:T(8,128)(2,1)}), bf16[16,64,128]{2,1,0:T(8,128)(2,1)S(1)}, u32[]{:S(2)}, u32[]{:S(2)}) async-start(bf16[16,64,128]{2,1,0:T(8,128)(2,1)} %broadcast_in_dim.2), calls=%async_computation.6 | async-start | bytes 524288 | tf_op jit(solution)/shard_map/all_to_all | solution.py:25
  171.9 0.6 reshape.26
  172.5 11.1 %all-to-all-done.6 = bf16[16,64,128]{2,1,0:T(8,128)(2,1)S(1)} async-done(((bf16[16,64,128]{2,1,0:T(8,128)(2,1)}), bf16[16,64,128]{2,1,0:T(8,128)(2,1)S(1)}, u32[]{:S(2)}, u32[]{:S(2)}) %all-to-all-start.6) | async-done | bytes 262176 | tf_op jit(solution)/shard_map/all_to_all | solution.py:25
  183.6 0.8 copy.15
  (17 shorter events, 0.1 us)
Async XLA Ops:
  2.3 34.9 %all-to-all-start = ((s32[16,1,2048]{2,1,0:T(1,128)}), s32[16,1,2048]{2,1,0:T(1,128)S(1)}, u32[]{:S(2)}, u32[]{:S(2)}) async-start(s32[16,1,2048]{2,1,0:T(1,128)} %get-tuple-element.14), calls=%async_computation | async-start | bytes 262144 | tf_op jit(solution)/shard_map/all_to_all | solution.py:25
  12.6 14.6 %collective-permute-start = (bf16[8,64,128]{2,1,0:T(8,128)(2,1)S(1)}, bf16[8,64,128]{2,1,0:T(8,128)(2,1)S(1)}, u32[]{:S(2)}, u32[]{:S(2)}) collective-permute-start(bf16[8,64,128]{2,1,0:T(8,128)(2,1)S(1)} %get-tuple-element.15.own), channel_id=1, source_target_pairs={{0,8},{8,16},{16,24},{24,0},{1,9},{9,17},{17,25},{25,1},{2,10},{10... | collective-permute-start | bytes 393224 | tf_op jit(solution)/shard_map/ppermute | solution.py:355
  15.8 16.9 %collective-permute-start.1 = (bf16[8,64,128]{2,1,0:T(8,128)(2,1)S(1)}, bf16[8,64,128]{2,1,0:T(8,128)(2,1)S(1)}, u32[]{:S(2)}, u32[]{:S(2)}) collective-permute-start(bf16[8,64,128]{2,1,0:T(8,128)(2,1)S(1)} %get-tuple-element.15.own), channel_id=1, source_target_pairs={{0,16},{8,24},{16,0},{24,8},{1,17},{9,25},{17,1},{25,9},{2,18},{10... | collective-permute-start | bytes 393224 | tf_op jit(solution)/shard_map/ppermute | solution.py:355
  23.8 13.5 %collective-permute-start.2 = (bf16[8,64,128]{2,1,0:T(8,128)(2,1)S(1)}, bf16[8,64,128]{2,1,0:T(8,128)(2,1)S(1)}, u32[]{:S(2)}, u32[]{:S(2)}) collective-permute-start(bf16[8,64,128]{2,1,0:T(8,128)(2,1)S(1)} %get-tuple-element.15.own), channel_id=1, source_target_pairs={{0,24},{8,0},{16,8},{24,16},{1,25},{9,1},{17,9},{25,17},{2,26},{10... | collective-permute-start | bytes 393224 | tf_op jit(solution)/shard_map/ppermute | solution.py:355
  39.4 5.0 %copy-start.6 = (s32[4,16]{1,0:T(4,128)S(1)}, s32[4,16]{1,0:T(4,128)}, u32[]{:S(2)}) copy-start(s32[4,16]{1,0:T(4,128)} %param.12) | copy-start | bytes 772
  39.5 32.5 %copy-start = (bf16[4,256,512]{2,1,0:T(8,128)(2,1)S(1)}, bf16[4,256,512]{2,1,0:T(8,128)(2,1)}, u32[]{:S(2)}) copy-start(bf16[4,256,512]{2,1,0:T(8,128)(2,1)} %phi_from.1) | copy-start | bytes 3145732
  39.5 32.5 %copy-start.2 = (f32[4,256]{1,0:T(4,128)S(1)}, f32[4,256]{1,0:T(4,128)}, u32[]{:S(2)}) copy-start(f32[4,256]{1,0:T(4,128)} %weight.3) | copy-start | bytes 12292
  39.5 32.5 %copy-start.3 = (f32[3,4,256]{2,1,0:T(4,128)S(1)}, f32[3,4,256]{2,1,0:T(4,128)}, u32[]{:S(2)}) copy-start(f32[3,4,256]{2,1,0:T(4,128)} %offset.3) | copy-start | bytes 36868
  39.5 32.5 %copy-start.5 = (s32[4]{0:T(128)S(1)}, s32[4]{0:T(128)}, u32[]{:S(2)}) copy-start(s32[4]{0:T(128)} %atom.3) | copy-start | bytes 52
  39.5 32.4 %all-to-all-start.1 = ((bf16[16,8,64,128]{3,2,1,0:T(8,128)(2,1)}), bf16[16,8,64,128]{3,2,1,0:T(8,128)(2,1)S(1)}, u32[]{:S(2)}, u32[]{:S(2)}) async-start(bf16[16,8,64,128]{3,2,1,0:T(8,128)(2,1)} %get-tuple-element.17), calls=%async_computation.1 | async-start | bytes 4194304 | tf_op jit(solution)/shard_map/all_to_all | solution.py:25
  44.4 51.8 %copy-start.1 = (f32[3,1000]{1,0:T(4,128)S(1)}, f32[3,1000]{1,0:T(4,128)}, u32[]{:S(2)}) copy-start(f32[3,1000]{1,0:T(4,128)} %places.1) | copy-start | bytes 36004
  44.5 60.5 %copy-start.4 = (f32[4,256]{1,0:T(4,128)S(1)}, f32[4,256]{1,0:T(4,128)}, u32[]{:S(2)}) copy-start(f32[4,256]{1,0:T(4,128)} %exchange_part.1) | copy-start | bytes 12292
  89.1 15.9 %all-to-all-start.3 = ((f32[32,1,512]{2,1,0:T(1,128)}), f32[32,1,512]{2,1,0:T(1,128)S(1)}, u32[]{:S(2)}, u32[]{:S(2)}) async-start(f32[32,1,512]{2,1,0:T(1,128)} %relay.1), calls=%async_computation.3 | async-start | bytes 131072 | tf_op jit(solution)/shard_map/all_to_all | solution.py:25
  113.3 33.0 %all-to-all-start.4 = ((bf16[32,8,32,128]{3,2,1,0:T(8,128)(2,1)}), bf16[32,8,32,128]{3,2,1,0:T(8,128)(2,1)S(1)}, u32[]{:S(2)}, u32[]{:S(2)}) async-start(bf16[32,8,32,128]{3,2,1,0:T(8,128)(2,1)} %get-tuple-element.22), calls=%async_computation.4 | async-start | bytes 4194304 | tf_op jit(solution)/shard_map/all_to_all | solution.py:25
  119.2 25.0 %collective-permute-start.3 = (s32[16,1,128]{2,1,0:T(1,128)S(1)}, s32[16,1,128]{2,1,0:T(1,128)S(1)}, u32[]{:S(2)}, u32[]{:S(2)}) collective-permute-start(s32[16,1,128]{2,1,0:T(1,128)S(1)} %get-tuple-element.16.asked), channel_id=1, source_target_pairs={{0,64},{64,0},{1,65},{65,1},{2,66},{66,2},{3,67},{67,3},{4,68},{68... | collective-permute-start | bytes 24584 | tf_op jit(solution)/shard_map/ppermute | solution.py:372
  164.3 19.3 %all-to-all-start.6 = ((bf16[16,64,128]{2,1,0:T(8,128)(2,1)}), bf16[16,64,128]{2,1,0:T(8,128)(2,1)S(1)}, u32[]{:S(2)}, u32[]{:S(2)}) async-start(bf16[16,64,128]{2,1,0:T(8,128)(2,1)} %broadcast_in_dim.2), calls=%async_computation.6 | async-start | bytes 524288 | tf_op jit(solution)/shard_map/all_to_all | solution.py:25

commit v3 on v2

--- a/solution.py
+++ b/solution.py
@@ -11,7 +11,6 @@
 GRP = ("y4", "y2", "c")
 DEV = ("z4", "z2", "x")
 GRP_DEV = GRP + DEV
-SERVE = ("c", "z2", "x")
 COLLECT = ("y2", "c", "z2", "x")
 SETTLE = ("y4", "z4")
 
@@ -38,8 +37,9 @@
 
 
 def prepare_kernel(request, stored, message, slab, staged, sems):
-    half = slab.shape[1]
-    own = stored.at[:, pl.ds(pl.multiple_of(lax.axis_index("c") * half, half), half)]
+    part = slab.shape[1]
+    at = (lax.axis_index("c") * 2 + lax.axis_index("y2")) * part
+    own = stored.at[:, pl.ds(pl.multiple_of(at, part), part)]
     load = pltpu.make_async_copy(own, slab, sems.at[0])
     load.start()
     owners, slots = request.shape[1], request.shape[2]
@@ -79,40 +79,39 @@
         copy.wait()
 
 
-def geometry_kernel(atom, places, offset, xyz, points_far, inverse_far, points_out, inverse_out, sems):
+def geometry_kernel(atom, places, offset, xyz, points_out, inverse_far, inverse, sems):
     batches, points = offset.shape[1], offset.shape[2]
     chunks = xyz.shape[1]
+    rows = points // 8
     filler = jnp.zeros((128 - 3 * batches, points), F32)
     features = jnp.concatenate([offset[0], offset[1], offset[2], filler], axis=0).T
+    copies = []
     for b in range(batches):
         for k in range(3):
             spot = features[:, k * batches + b : k * batches + b + 1] + places[k, atom[b]]
-            spot = jnp.broadcast_to(spot, (points, 128)).reshape(points // 8, 8, 128)
-            points_out[k, b * points // 8 : (b + 1) * points // 8] = spot
-
-    def inverse_of(step, _):
-        at = pl.ds(step * 8, 8)
-        px, py, pz = points_out[0, at], points_out[1, at], points_out[2, at]
-        for h in range(chunks):
-            gx = px - xyz[0, h : h + 1][None]
-            gy = py - xyz[1, h : h + 1][None]
-            gz = pz - xyz[2, h : h + 1][None]
-            inverse_out[h, at] = lax.rsqrt(gx * gx + gy * gy + gz * gz + 1.0)
-        return 0
-
-    first = pltpu.make_async_copy(points_out, points_far, sems.at[0])
-    first.start()
-    lax.fori_loop(0, batches * points // 64, inverse_of, 0)
-    second = pltpu.make_async_copy(inverse_out, inverse_far, sems.at[1])
-    second.start()
-    first.wait()
-    second.wait()
+            points_out[k, b * rows : (b + 1) * rows] = jnp.broadcast_to(spot, (points, 128)).reshape(rows, 8, 128)
+
+        def inverse_of(step, _, b=b):
+            at = pl.ds(step * 8, 8)
+            px, py, pz = (points_out[k, pl.ds(b * rows + step * 8, 8)] for k in range(3))
+            for h in range(chunks):
+                gx = px - xyz[0, h : h + 1][None]
+                gy = py - xyz[1, h : h + 1][None]
+                gz = pz - xyz[2, h : h + 1][None]
+                inverse[b, h, at] = lax.rsqrt(gx * gx + gy * gy + gz * gz + 1.0)
+            return 0
+
+        lax.fori_loop(0, rows // 8, inverse_of, 0)
+        copies.append(pltpu.make_async_copy(inverse.at[b], inverse_far.at[b], sems.at[b]))
+        copies[-1].start()
+    for copy in copies:
+        copy.wait()
 
 
 def density_kernel(needed, atom, phi, blocks, weight, offset, rho_out, rho_again, share_out, wide):
     batches, points, width = phi.shape
     rel = width // 128
-    half = blocks.shape[2]
+    part = blocks.shape[2]
     lane = lax.broadcasted_iota(jnp.int32, (points, 128), 1)
     columns = jnp.zeros((points, 128), F32)
     for b in range(batches):
@@ -120,7 +119,9 @@
             w, k = place_of(needed[b * rel * rel + p])
             i, j = p // rel, p % rel
             for c in range(2):
-                wide[b % 2, pl.ds(i * 128 + c * half, half), pl.ds(j * 128, 128)] = blocks[c * 8 + w, k]
+                for y2 in range(2):
+                    at = i * 128 + (c * 2 + y2) * part
+                    wide[b % 2, pl.ds(at, part), pl.ds(j * 128, 128)] = blocks[(y2 * 2 + c) * 8 + w, k]
         values = phi[b]
         product = jnp.dot(values, wide[b % 2], preferred_element_type=F32) * values.astype(F32)
         folded = product[:, :128]
@@ -160,26 +161,19 @@
     weight,
     exchange_part,
     xyz,
-    points_from,
-    inverse_from,
-    phi_from,
+    points_at,
+    phi,
+    inverse_far,
     multipoles_out,
     out,
-    points_at,
     inverse,
-    phi,
     rows,
     spread,
     potential,
     total,
-    ready,
     load_sems,
-    sems,
 ):
-    loads = [
-        pltpu.make_async_copy(source, target, load_sems.at[n])
-        for n, (source, target) in enumerate(((points_from, points_at), (inverse_from, inverse), (phi_from, phi)))
-    ]
+    loads = [pltpu.make_async_copy(inverse_far.at[b], inverse.at[b], load_sems.at[b]) for b in range(phi.shape[0])]
     for load in loads:
         load.start()
     batches, points, width = phi.shape
@@ -221,34 +215,31 @@
         for h in range(chunks):
             spread[k * chunks + h] = jnp.broadcast_to(value[h : h + 1], (8, 128))
 
-    loads[0].wait()
-    loads[1].wait()
-
-    def potential_of(step, _):
-        at = pl.ds(step * 8, 8)
-        px, py, pz = points_at[0, at], points_at[1, at], points_at[2, at]
-        acc = jnp.zeros((8, 8, 128), F32)
-        for h in range(chunks):
-            dipole = (
-                spread[chunks + h][None] * px
-                + spread[2 * chunks + h][None] * py
-                + spread[3 * chunks + h][None] * pz
-                - spread[4 * chunks + h][None]
-            )
-            s = inverse[h, at]
-            acc = acc + s * (spread[h][None] + dipole * (s * s))
-        potential[at] = acc
-        return 0
-
-    lax.fori_loop(0, batches * points // 64, potential_of, 0)
-
     filler = jnp.zeros((128 - 2 * batches, points), F32)
     features = jnp.concatenate([weight[...], exchange_part[...] * rho[...], filler], axis=0).T
     total[...] = jnp.zeros_like(total)
-    loads[2].wait()
+    rows_each = points // 8
     for b in range(batches):
-        field = potential[b * points // 8 : (b + 1) * points // 8].reshape(points, 128)
-        hartree = jnp.sum(field, axis=1, keepdims=True)
+        loads[b].wait()
+
+        def potential_of(step, _, b=b):
+            at = pl.ds(step * 8, 8)
+            px, py, pz = (points_at[k, pl.ds(b * rows_each + step * 8, 8)] for k in range(3))
+            acc = jnp.zeros((8, 8, 128), F32)
+            for h in range(chunks):
+                dipole = (
+                    spread[chunks + h][None] * px
+                    + spread[2 * chunks + h][None] * py
+                    + spread[3 * chunks + h][None] * pz
+                    - spread[4 * chunks + h][None]
+                )
+                s = inverse[b, h, at]
+                acc = acc + s * (spread[h][None] + dipole * (s * s))
+            potential[at] = acc
+            return 0
+
+        lax.fori_loop(0, rows_each // 8, potential_of, 0)
+        hartree = jnp.sum(potential[...].reshape(points, 128), axis=1, keepdims=True)
         factor = features[:, b : b + 1] * (features[:, batches + b : batches + b + 1] + hartree)
         values = phi[b]
         scaled = (values.astype(F32) * factor).astype(BF16)
@@ -263,31 +254,22 @@
                 q = needed[b * rel * rel + i * rel + j]
                 total[q] += term[:, j * 128 : (j + 1) * 128]
 
-    copies = []
     for w in range(8):
         for k in range(8):
             q = (k // 2) * 16 + w * 2 + k % 2
             for c in range(2):
                 for y2 in range(2):
                     first = c * 64 + y2 * 32
-                    ready[(y2 * 2 + c) * 8 + w, k] = total[q, first : first + 32].astype(BF16)
-        for d in range(w, 32, 8):
-            copies.append(pltpu.make_async_copy(ready.at[d], out.at[d], sems.at[d]))
-            copies[-1].start()
-    for copy in copies:
-        copy.wait()
-
-
-def collect_kernel(asked, asked_near, received, out, total):
+                    out[(y2 * 2 + c) * 8 + w, k] = total[q, first : first + 32].astype(BF16)
+
+
+def collect_kernel(asked, received, out, total):
     total[...] = jnp.zeros_like(total)
     w = lax.axis_index("z2") * 4 + lax.axis_index("x")
-    y2 = lax.axis_index("y2")
 
     def add_one(n, _):
-        mine = (n >> 4) == y2
         for k in range(8):
-            block = jnp.where(mine, asked_at(asked, n & 15, w, k), asked_at(asked_near, n & 15, w, k))
-            total[(k // 2) * 8 + block] += received[n, k].astype(F32)
+            total[(k // 2) * 8 + asked_at(asked, n, w, k)] += received[n, k].astype(F32)
         return 0
 
     lax.fori_loop(0, received.shape[0], add_one, 0)
@@ -315,7 +297,7 @@
     own, tile = stored_density_blocks.shape[0], stored_density_blocks.shape[1]
     atoms = atom_xyz.shape[1]
     padded = -(-atoms // 128) * 128
-    half = tile // 2
+    part = tile // 4
     chunks = padded // 128
     each = batches * VALUES
     groups = batches * points // 8
@@ -328,15 +310,14 @@
         geometry_kernel,
         name="geometry",
         out_shape=(
-            pltpu.HBM((3, groups, 8, 128), F32),
-            pltpu.HBM((chunks, groups, 8, 128), F32),
+            pltpu.VMEM((3, groups, 8, 128), F32),
+            pltpu.HBM((batches, chunks, points // 8, 8, 128), F32),
         ),
         in_specs=smem(2) + vmem(2),
-        out_specs=(hbm, hbm),
+        out_specs=(vmem(1)[0], hbm),
         scratch_shapes=[
-            pltpu.VMEM((3, groups, 8, 128), F32),
-            pltpu.VMEM((chunks, groups, 8, 128), F32),
-            pltpu.SemaphoreType.DMA((2,)),
+            pltpu.VMEM((batches, chunks, points // 8, 8, 128), F32),
+            pltpu.SemaphoreType.DMA((batches,)),
         ],
         compiler_params=params,
         cost_estimate=pl.CostEstimate(flops=2 * 10**7, bytes_accessed=6 * MIB, transcendentals=10**6),
@@ -345,31 +326,30 @@
     message, slab = pl.pallas_call(
         prepare_kernel,
         name="prepare",
-        out_shape=(pltpu.HBM((16, 1, 2048), jnp.int32), jax.ShapeDtypeStruct((own, half, tile), BF16)),
+        out_shape=(pltpu.HBM((32, 1, 1024), jnp.int32), jax.ShapeDtypeStruct((own, part, tile), BF16)),
         in_specs=vmem(1) + [hbm],
         out_specs=(hbm, vmem(1)[0]),
-        scratch_shapes=[pltpu.VMEM((16, 1, 2048), jnp.int32), pltpu.SemaphoreType.DMA((2,))],
+        scratch_shapes=[pltpu.VMEM((32, 1, 1024), jnp.int32), pltpu.SemaphoreType.DMA((2,))],
         compiler_params=params,
     )(device_request, pltpu.with_memory_space_constraint(stored_density_blocks, pltpu.HBM))
-    message = exchange(message, SERVE)
+    message = exchange(message, COLLECT)
     pieces = [slab] + [lax.ppermute(slab, "z4", [(i, (i + s) % 4) for i in range(4)]) for s in (1, 2, 3)]
     served, asked = pl.pallas_call(
         serve_kernel,
         name="serve",
-        out_shape=(pltpu.HBM((16, 8, half, tile), BF16), jax.ShapeDtypeStruct((16, 1, 128), jnp.int32)),
+        out_shape=(pltpu.HBM((32, 8, part, tile), BF16), jax.ShapeDtypeStruct((32, 1, 128), jnp.int32)),
         in_specs=[far_away] + vmem(4),
         out_specs=(hbm, vmem(1)[0]),
         scratch_shapes=[
-            pltpu.SMEM((16, 1, 128), jnp.int32),
-            pltpu.VMEM((4, own, half, tile), BF16),
-            pltpu.VMEM((16, 8, half, tile), BF16),
+            pltpu.SMEM((32, 1, 128), jnp.int32),
+            pltpu.VMEM((4, own, part, tile), BF16),
+            pltpu.VMEM((32, 8, part, tile), BF16),
             pltpu.SemaphoreType.DMA((2,)),
-            pltpu.SemaphoreType.DMA((16,)),
+            pltpu.SemaphoreType.DMA((32,)),
         ],
         compiler_params=params,
     )(message, *pieces)
-    blocks = exchange(served, SERVE)
-    asked_near = lax.ppermute(asked, "y2", [(0, 1), (1, 0)])
+    blocks = exchange(served, COLLECT)
 
     needed = batch_blocks.reshape(-1)
     density, density_again, share = pl.pallas_call(
@@ -378,7 +358,7 @@
         out_shape=(
             jax.ShapeDtypeStruct((batches, points), F32),
             jax.ShapeDtypeStruct((batches, points), F32),
-            jax.ShapeDtypeStruct((16, 1, each), F32),
+            jax.ShapeDtypeStruct((32, 1, each), F32),
         ),
         in_specs=smem(2) + vmem(4),
         out_specs=tuple(vmem(3)),
@@ -389,43 +369,39 @@
     shares = pl.pallas_call(
         relay_kernel,
         name="relay",
-        out_shape=jax.ShapeDtypeStruct((32, 1, 16 * each), F32),
+        out_shape=jax.ShapeDtypeStruct((16, 1, 32 * each), F32),
         in_specs=vmem(1),
         out_specs=vmem(1)[0],
         compiler_params=params,
-    )(exchange(share, GRP))
+    )(exchange(share, COLLECT))
     multipoles, outgoing = pl.pallas_call(
         term_kernel,
         name="terms",
         out_shape=(
             jax.ShapeDtypeStruct((4 * chunks, 128), F32),
-            pltpu.HBM((32, 8, 32, tile), BF16),
+            jax.ShapeDtypeStruct((32, 8, 32, tile), BF16),
         ),
-        in_specs=smem(1) + vmem(5) + [hbm, hbm, far_away],
-        out_specs=(vmem(1)[0], hbm),
+        in_specs=smem(1) + vmem(7) + [hbm],
+        out_specs=tuple(vmem(2)),
         scratch_shapes=[
-            pltpu.VMEM(points_at.shape, F32),
             pltpu.VMEM(inverse.shape, F32),
-            pltpu.VMEM(basis_values.shape, BF16),
             pltpu.VMEM((512, 128), F32),
             pltpu.VMEM((5 * chunks, 8, 128), F32),
-            pltpu.VMEM((groups, 8, 128), F32),
+            pltpu.VMEM((points // 8, 8, 128), F32),
             pltpu.VMEM((64, tile, tile), F32),
-            pltpu.VMEM((32, 8, 32, tile), BF16),
-            pltpu.SemaphoreType.DMA((3,)),
-            pltpu.SemaphoreType.DMA((32,)),
+            pltpu.SemaphoreType.DMA((batches,)),
         ],
         compiler_params=params,
     )(
         needed,
-        exchange(shares, DEV),
+        exchange(shares, SETTLE),
         density_again,
         point_weight,
         exchange_kernel,
         far,
-        pltpu.with_memory_space_constraint(points_at, pltpu.HBM),
+        pltpu.with_memory_space_constraint(points_at, pltpu.VMEM),
+        basis_values,
         pltpu.with_memory_space_constraint(inverse, pltpu.HBM),
-        basis_values,
     )
 
     received = exchange(outgoing, COLLECT)
@@ -433,11 +409,11 @@
         collect_kernel,
         name="collect",
         out_shape=jax.ShapeDtypeStruct((16, own * 8, tile), BF16),
-        in_specs=smem(2) + vmem(1),
+        in_specs=smem(1) + vmem(1),
         out_specs=vmem(1)[0],
         scratch_shapes=[pltpu.VMEM((4 * own, 32, tile), F32)],
         compiler_params=params,
-    )(asked, asked_near, received)
+    )(asked, received)
     settled = exchange(partial, SETTLE).astype(F32).sum(axis=0).astype(BF16)
     rows = exchange(jnp.broadcast_to(settled[None], (16, own * 8, tile)), GRP)
     rows = rows.reshape(4, 2, 2, own, 8, tile).transpose(3, 2, 1, 0, 4, 5)

time: 185 us -> 183 us (0.989)
  blocking collectives: 29 us -> 59.9 us
  waiting for transfers between devices: 76.3 us -> 49.7 us
  starting transfers between devices: 53.6 us -> 49.7 us
  Pallas kernels: 21.6 us -> 19.6 us
    all_to_all x2 -> x3, blocking collectives: 29 us -> 59.9 us  [exchange(): return lax.all_to_all(value, axes, split_axis=0, concat_axis=0, tiled=True)]
    ppermute x1 -> x0, waiting for transfers between devices: 21.7 us -> none  [on_device(): asked_near = lax.ppermute(asked, 'y2', [(0, 1), (1, 0)])]
    ppermute x3, waiting for transfers between devices: 10.1 us -> 4.5 us  [on_device(): lax.ppermute(slab, 'z4', [(i, (i + s) % 4) for i in range(4)])]
    ppermute x1 -> x0, starting transfers between devices: 3.37 us -> none  [on_device(): asked_near = lax.ppermute(asked, 'y2', [(0, 1), (1, 0)])]
    all_to_all x5 -> x4, waiting for transfers between devices: 44.6 us -> 45.2 us  [exchange(): return lax.all_to_all(value, axes, split_axis=0, concat_axis=0, tiled=True)]
    all_to_all x5 -> x4, starting transfers between devices: 35.6 us -> 35.4 us  [exchange(): return lax.all_to_all(value, axes, split_axis=0, concat_axis=0, tiled=True)]
  transfers between devices with their start and end apart: 9 -> 7, of which waited for: 7 -> 4; matrix products, arithmetic and copies ran while one was open for 0% -> 0% of each run, Pallas kernels for 3% -> 2%
where the time goes in v3:
time: 183 us
  blocking collectives  59.9 us (33%)
  starting transfers between devices  49.7 us (27%)
  waiting for transfers between devices  49.7 us (27%)
  Pallas kernels  19.6 us (11%)
  local copies, waits for them, and re-layouts  3.04 us (2%)
    all_to_all x3, blocking collectives, exchange(): return lax.all_to_all(value, axes, split_axis=0, concat_axis=0, tiled=True)  59.9 us
    all_to_all x4, waiting for transfers between devices, exchange(): return lax.all_to_all(value, axes, split_axis=0, concat_axis=0, tiled=True)  45.2 us
    all_to_all x4, starting transfers between devices, exchange(): return lax.all_to_all(value, axes, split_axis=0, concat_axis=0, tiled=True)  35.4 us
    ppermute x3, starting transfers between devices, on_device(): lax.ppermute(slab, 'z4', [(i, (i + s) % 4) for i in range(4)])  14.3 us
    pallas_call x1, Pallas kernels, on_device(): pl.pallas_call(term_kernel, name='terms', out_shape=(jax.ShapeDtypeStruct...  7 us
    ppermute x3, waiting for transfers between devices, on_device(): lax.ppermute(slab, 'z4', [(i, (i + s) % 4) for i in range(4)])  4.5 us
    pallas_call x1, Pallas kernels, on_device(): pl.pallas_call(geometry_kernel, name='geometry', out_shape=(pltpu.VMEM((3...  4.1 us
  transfers between devices with their start and end apart: 7, of which 4 were waited for; matrix products, arithmetic and copies ran while one was open for 0% of the time, Pallas kernels for 2%

profile of v3, /device:TPU:1, one launch (start us, length us, event | category | flops | bytes accessed | tf_op | source)
XLA Modules:
  0.0 182.8 jit_solution(16493914578394029076)
XLA Ops:
  0.6 0.8 copy.14.request
  1.4 0.9 prepare.1
  2.3 10.5 %all-to-all-start = ((s32[32,1,1024]{2,1,0:T(1,128)}), s32[32,1,1024]{2,1,0:T(1,128)S(1)}, u32[]{:S(2)}, u32[]{:S(2)}) async-start(s32[32,1,1024]{2,1,0:T(1,128)} %get-tuple-element.14), calls=%async_computation | async-start | bytes 262144 | tf_op jit(solution)/shard_map/all_to_all | solution.py:24
  12.7 8.1 %collective-permute-start.2 = (bf16[8,32,128]{2,1,0:T(8,128)(2,1)S(1)}, bf16[8,32,128]{2,1,0:T(8,128)(2,1)S(1)}, u32[]{:S(2)}, u32[]{:S(2)}) collective-permute-start(bf16[8,32,128]{2,1,0:T(8,128)(2,1)S(1)} %get-tuple-element.15.own), channel_id=1, source_target_pairs={{0,24},{8,0},{16,8},{24,16},{1,25},{9,1},{17,9},{25,17},{2,26},{10... | collective-permute-start | bytes 196616 | tf_op jit(solution)/shard_map/ppermute | solution.py:336
  20.8 1.9 %collective-permute-start.1 = (bf16[8,32,128]{2,1,0:T(8,128)(2,1)S(1)}, bf16[8,32,128]{2,1,0:T(8,128)(2,1)S(1)}, u32[]{:S(2)}, u32[]{:S(2)}) collective-permute-start(bf16[8,32,128]{2,1,0:T(8,128)(2,1)S(1)} %get-tuple-element.15.own), channel_id=1, source_target_pairs={{0,16},{8,24},{16,0},{24,8},{1,17},{9,25},{17,1},{25,9},{2,18},{10... | collective-permute-start | bytes 196616 | tf_op jit(solution)/shard_map/ppermute | solution.py:336
  22.8 4.2 %collective-permute-start = (bf16[8,32,128]{2,1,0:T(8,128)(2,1)S(1)}, bf16[8,32,128]{2,1,0:T(8,128)(2,1)S(1)}, u32[]{:S(2)}, u32[]{:S(2)}) collective-permute-start(bf16[8,32,128]{2,1,0:T(8,128)(2,1)S(1)} %get-tuple-element.15.own), channel_id=1, source_target_pairs={{0,8},{8,16},{16,24},{24,0},{1,9},{9,17},{17,25},{25,1},{2,10},{10... | collective-permute-start | bytes 196616 | tf_op jit(solution)/shard_map/ppermute | solution.py:336
  27.0 4.5 %collective-permute-done.1.two = bf16[8,32,128]{2,1,0:T(8,128)(2,1)S(1)} collective-permute-done((bf16[8,32,128]{2,1,0:T(8,128)(2,1)S(1)}, bf16[8,32,128]{2,1,0:T(8,128)(2,1)S(1)}, u32[]{:S(2)}, u32[]{:S(2)}) %collective-permute-start.1) | collective-permute-done | bytes 65568 | tf_op jit(solution)/shard_map/ppermute | solution.py:336
  31.5 2.5 %serve.1 = (bf16[32,8,32,128]{3,2,1,0:T(8,128)(2,1)}, s32[32,1,128]{2,1,0:T(1,128)S(1)}) custom-call(s32[32,1,1024]{2,1,0:T(1,128)S(1)} %all-to-all-done.message, bf16[8,32,128]{2,1,0:T(8,128)(2,1)S(1)} %get-tuple-element.15.own, bf16[8,32,128]{2,1,0:T(8,128)(2,1)S(1)} %collective-permute-done.one, bf16[8,32,128]{2,1,0:T(8,128)(2,1)S(1)} %collective-permute-done.1.two, ...), custom_call_target="tpu_custom_call" | custom-call | tf_op jit(solution)/shard_map/serve/pallas_call | solution.py:337
  34.0 0.0 copy-start.6
  34.0 0.0 copy-start
  34.0 0.0 copy-start.2
  34.1 0.0 copy-start.3
  34.1 0.0 copy-start.5
  34.1 9.0 %all-to-all-start.1 = ((bf16[32,8,32,128]{3,2,1,0:T(8,128)(2,1)}), bf16[32,8,32,128]{3,2,1,0:T(8,128)(2,1)S(1)}, u32[]{:S(2)}, u32[]{:S(2)}) async-start(bf16[32,8,32,128]{3,2,1,0:T(8,128)(2,1)} %get-tuple-element.17), calls=%async_computation.1 | async-start | bytes 4194304 | tf_op jit(solution)/shard_map/all_to_all | solution.py:24
  43.1 0.0 copy-start.1
  43.1 0.1 reshape.22.needed
  43.2 26.9 %all-to-all-done.1.blocks = bf16[32,8,32,128]{3,2,1,0:T(8,128)(2,1)S(1)} async-done(((bf16[32,8,32,128]{3,2,1,0:T(8,128)(2,1)}), bf16[32,8,32,128]{3,2,1,0:T(8,128)(2,1)S(1)}, u32[]{:S(2)}, u32[]{:S(2)}) %all-to-all-start.1) | async-done | bytes 2097184 | tf_op jit(solution)/shard_map/all_to_all | solution.py:24
  70.2 2.3 %density.1 = (f32[4,256]{1,0:T(4,128)}, f32[4,256]{1,0:T(4,128)S(1)}, f32[32,1,32]{2,1,0:T(1,128)S(1)}) custom-call(s32[64]{0:T(128)S(1)} %reshape.22.needed, s32[4]{0:T(128)S(1)} %copy-done.5, bf16[4,256,512]{2,1,0:T(8,128)(2,1)S(1)} %copy-done, bf16[32,8,32,128]{3,2,1,0:T(8,128)(2,1)S(1)} %all-to-all-done.1.blocks, f32[4,256]{1,0:T(4,128)S(1)} %copy-done.2, ...), custom_call_target="tpu_custom_call" | custom-call | tf_op jit(solution)/shard_map/density/pallas_call | solution.py:355
  72.5 12.0 %all_to_all.35.near = f32[32,1,32]{2,1,0:T(1,128)S(1)} all-to-all(f32[32,1,32]{2,1,0:T(1,128)S(1)} %get-tuple-element.18), channel_id=1, replica_groups=mesh['y4'=4,'y2'=2,'c'=2,'z4'=4,'z2'=2,'x'=4] {'y2','c','z2','x'}, dimensions={0} | all-to-all | bytes 8192 | tf_op jit(solution)/shard_map/all_to_all | solution.py:24
  84.4 0.7 relay.1
  85.2 9.8 %all-to-all-start.3 = ((f32[16,1,1024]{2,1,0:T(1,128)}), f32[16,1,1024]{2,1,0:T(1,128)S(1)}, u32[]{:S(2)}, u32[]{:S(2)}) async-start(f32[16,1,1024]{2,1,0:T(1,128)} %relay.1), calls=%async_computation.3 | async-start | bytes 131072 | tf_op jit(solution)/shard_map/all_to_all | solution.py:24
  95.0 4.1 %geometry.1 = (f32[3,128,8,128]{3,2,1,0:T(8,128)S(1)}, f32[4,8,32,8,128]{4,3,2,1,0:T(8,128)}) custom-call(s32[4]{0:T(128)S(1)} %copy-done.5, f32[3,1000]{1,0:T(4,128)S(1)} %copy-done.1, f32[3,4,256]{2,1,0:T(4,128)S(1)} %copy-done.3, f32[3,8,128]{2,1,0:T(8,128)S(1)} %bitcast.10), custom_call_target="tpu_custom_call" | custom-call | flops 20000000 | bytes 6291456 | tf_op jit(solution)/shard_map/geometry/pallas_call | solution.py:309
  99.1 7.2 %all-to-all-done.3.shares = f32[16,1,1024]{2,1,0:T(1,128)S(1)} async-done(((f32[16,1,1024]{2,1,0:T(1,128)}), f32[16,1,1024]{2,1,0:T(1,128)S(1)}, u32[]{:S(2)}, u32[]{:S(2)}) %all-to-all-start.3) | async-done | bytes 65568 | tf_op jit(solution)/shard_map/all_to_all | solution.py:24
  106.3 7.0 %terms.1 = (f32[32,128]{1,0:T(8,128)S(1)}, bf16[32,8,32,128]{3,2,1,0:T(8,128)(2,1)S(1)}) custom-call(s32[64]{0:T(128)S(1)} %reshape.22.needed, f32[16,1,1024]{2,1,0:T(1,128)S(1)} %all-to-all-done.3.shares, f32[4,256]{1,0:T(4,128)S(1)} %get-tuple-element.19.rho, f32[4,256]{1,0:T(4,128)S(1)} %copy-done.2, f32[4,256]{1,0:T(4,128)S(1)} %copy-done.4, ...), custom_call_target="tpu_custom_call" | custom-call | tf_op jit(solution)/shard_map/terms/pallas_call | solution.py:377
  113.3 31.6 %all_to_all.36.received = bf16[32,8,32,128]{3,2,1,0:T(8,128)(2,1)S(1)} all-to-all(bf16[32,8,32,128]{3,2,1,0:T(8,128)(2,1)S(1)} %get-tuple-element.22), channel_id=1, replica_groups=mesh['y4'=4,'y2'=2,'c'=2,'z4'=4,'z2'=2,'x'=4] {'y2','c','z2','x'}, dimensions={0} | all-to-all | bytes 4194304 | tf_op jit(solution)/shard_map/all_to_all | solution.py:24
  144.9 2.1 %collect.1 = bf16[16,64,128]{2,1,0:T(8,128)(2,1)S(1)} custom-call(s32[32,1,128]{2,1,0:T(1,128)S(1)} %get-tuple-element.16.asked, bf16[32,8,32,128]{3,2,1,0:T(8,128)(2,1)S(1)} %all_to_all.36.received), custom_call_target="tpu_custom_call" | custom-call | tf_op jit(solution)/shard_map/collect/pallas_call | solution.py:408
  147.1 16.3 %all_to_all.37 = bf16[16,64,128]{2,1,0:T(8,128)(2,1)S(1)} all-to-all(bf16[16,64,128]{2,1,0:T(8,128)(2,1)S(1)} %collect.1), channel_id=1, replica_groups=mesh['y4'=4,'y2'=2,'c'=2,'z4'=4,'z2'=2,'x'=4] {'y4','z4'}, dimensions={0} | all-to-all | bytes 524288 | tf_op jit(solution)/shard_map/all_to_all | solution.py:24
  163.4 0.8 broadcast_in_dim.2
  164.2 6.1 %all-to-all-start.6 = ((bf16[16,64,128]{2,1,0:T(8,128)(2,1)}), bf16[16,64,128]{2,1,0:T(8,128)(2,1)S(1)}, u32[]{:S(2)}, u32[]{:S(2)}) async-start(bf16[16,64,128]{2,1,0:T(8,128)(2,1)} %broadcast_in_dim.2), calls=%async_computation.6 | async-start | bytes 524288 | tf_op jit(solution)/shard_map/all_to_all | solution.py:24
  170.3 0.6 reshape.26
  170.9 11.1 %all-to-all-done.6 = bf16[16,64,128]{2,1,0:T(8,128)(2,1)S(1)} async-done(((bf16[16,64,128]{2,1,0:T(8,128)(2,1)}), bf16[16,64,128]{2,1,0:T(8,128)(2,1)S(1)}, u32[]{:S(2)}, u32[]{:S(2)}) %all-to-all-start.6) | async-done | bytes 262176 | tf_op jit(solution)/shard_map/all_to_all | solution.py:24
  182.0 0.8 copy.15
  (14 shorter events, 0.1 us)
Async XLA Ops:
  2.3 29.3 %all-to-all-start = ((s32[32,1,1024]{2,1,0:T(1,128)}), s32[32,1,1024]{2,1,0:T(1,128)S(1)}, u32[]{:S(2)}, u32[]{:S(2)}) async-start(s32[32,1,1024]{2,1,0:T(1,128)} %get-tuple-element.14), calls=%async_computation | async-start | bytes 262144 | tf_op jit(solution)/shard_map/all_to_all | solution.py:24
  12.7 14.3 %collective-permute-start.2 = (bf16[8,32,128]{2,1,0:T(8,128)(2,1)S(1)}, bf16[8,32,128]{2,1,0:T(8,128)(2,1)S(1)}, u32[]{:S(2)}, u32[]{:S(2)}) collective-permute-start(bf16[8,32,128]{2,1,0:T(8,128)(2,1)S(1)} %get-tuple-element.15.own), channel_id=1, source_target_pairs={{0,24},{8,0},{16,8},{24,16},{1,25},{9,1},{17,9},{25,17},{2,26},{10... | collective-permute-start | bytes 196616 | tf_op jit(solution)/shard_map/ppermute | solution.py:336
  20.8 10.7 %collective-permute-start.1 = (bf16[8,32,128]{2,1,0:T(8,128)(2,1)S(1)}, bf16[8,32,128]{2,1,0:T(8,128)(2,1)S(1)}, u32[]{:S(2)}, u32[]{:S(2)}) collective-permute-start(bf16[8,32,128]{2,1,0:T(8,128)(2,1)S(1)} %get-tuple-element.15.own), channel_id=1, source_target_pairs={{0,16},{8,24},{16,0},{24,8},{1,17},{9,25},{17,1},{25,9},{2,18},{10... | collective-permute-start | bytes 196616 | tf_op jit(solution)/shard_map/ppermute | solution.py:336
  22.8 8.8 %collective-permute-start = (bf16[8,32,128]{2,1,0:T(8,128)(2,1)S(1)}, bf16[8,32,128]{2,1,0:T(8,128)(2,1)S(1)}, u32[]{:S(2)}, u32[]{:S(2)}) collective-permute-start(bf16[8,32,128]{2,1,0:T(8,128)(2,1)S(1)} %get-tuple-element.15.own), channel_id=1, source_target_pairs={{0,8},{8,16},{16,24},{24,0},{1,9},{9,17},{17,25},{25,1},{2,10},{10... | collective-permute-start | bytes 196616 | tf_op jit(solution)/shard_map/ppermute | solution.py:336
  34.0 9.1 %copy-start.6 = (s32[4,16]{1,0:T(4,128)S(1)}, s32[4,16]{1,0:T(4,128)}, u32[]{:S(2)}) copy-start(s32[4,16]{1,0:T(4,128)} %param.12) | copy-start | bytes 772
  34.0 36.1 %copy-start = (bf16[4,256,512]{2,1,0:T(8,128)(2,1)S(1)}, bf16[4,256,512]{2,1,0:T(8,128)(2,1)}, u32[]{:S(2)}) copy-start(bf16[4,256,512]{2,1,0:T(8,128)(2,1)} %phi.3) | copy-start | bytes 3145732
  34.0 36.1 %copy-start.2 = (f32[4,256]{1,0:T(4,128)S(1)}, f32[4,256]{1,0:T(4,128)}, u32[]{:S(2)}) copy-start(f32[4,256]{1,0:T(4,128)} %weight.3) | copy-start | bytes 12292
  34.1 36.1 %copy-start.3 = (f32[3,4,256]{2,1,0:T(4,128)S(1)}, f32[3,4,256]{2,1,0:T(4,128)}, u32[]{:S(2)}) copy-start(f32[3,4,256]{2,1,0:T(4,128)} %offset.3) | copy-start | bytes 36868
  34.1 36.1 %copy-start.5 = (s32[4]{0:T(128)S(1)}, s32[4]{0:T(128)}, u32[]{:S(2)}) copy-start(s32[4]{0:T(128)} %atom.3) | copy-start | bytes 52
  34.1 36.1 %all-to-all-start.1 = ((bf16[32,8,32,128]{3,2,1,0:T(8,128)(2,1)}), bf16[32,8,32,128]{3,2,1,0:T(8,128)(2,1)S(1)}, u32[]{:S(2)}, u32[]{:S(2)}) async-start(bf16[32,8,32,128]{3,2,1,0:T(8,128)(2,1)} %get-tuple-element.17), calls=%async_computation.1 | async-start | bytes 4194304 | tf_op jit(solution)/shard_map/all_to_all | solution.py:24
  43.1 51.9 %copy-start.1 = (f32[3,1000]{1,0:T(4,128)S(1)}, f32[3,1000]{1,0:T(4,128)}, u32[]{:S(2)}) copy-start(f32[3,1000]{1,0:T(4,128)} %places.1) | copy-start | bytes 36004
  43.2 63.1 %copy-start.4 = (f32[4,256]{1,0:T(4,128)S(1)}, f32[4,256]{1,0:T(4,128)}, u32[]{:S(2)}) copy-start(f32[4,256]{1,0:T(4,128)} %exchange_part.1) | copy-start | bytes 12292
  85.2 21.2 %all-to-all-start.3 = ((f32[16,1,1024]{2,1,0:T(1,128)}), f32[16,1,1024]{2,1,0:T(1,128)S(1)}, u32[]{:S(2)}, u32[]{:S(2)}) async-start(f32[16,1,1024]{2,1,0:T(1,128)} %relay.1), calls=%async_computation.3 | async-start | bytes 131072 | tf_op jit(solution)/shard_map/all_to_all | solution.py:24
  164.2 17.8 %all-to-all-start.6 = ((bf16[16,64,128]{2,1,0:T(8,128)(2,1)}), bf16[16,64,128]{2,1,0:T(8,128)(2,1)S(1)}, u32[]{:S(2)}, u32[]{:S(2)}) async-start(bf16[16,64,128]{2,1,0:T(8,128)(2,1)} %broadcast_in_dim.2), calls=%async_computation.6 | async-start | bytes 524288 | tf_op jit(solution)/shard_map/all_to_all | solution.py:24

commit v4 on v3

--- a/solution.py
+++ b/solution.py
@@ -36,15 +36,17 @@
     return (position >> 1) & 7, (position >> 4) * 2 + (position & 1)
 
 
-def prepare_kernel(request, stored, message, slab, staged, sems):
+def prepare_kernel(request_far, stored, message, slab, request, staged, sems):
+    ask = pltpu.make_async_copy(request_far, request, sems.at[2])
+    ask.start()
     part = slab.shape[1]
     at = (lax.axis_index("c") * 2 + lax.axis_index("y2")) * part
     own = stored.at[:, pl.ds(pl.multiple_of(at, part), part)]
     load = pltpu.make_async_copy(own, slab, sems.at[0])
     load.start()
-    owners, slots = request.shape[1], request.shape[2]
-    wide = jnp.pad(request[0], ((0, 128 - owners), (0, 128 - slots))).T
-    flat = jnp.concatenate([wide[k : k + 1, :owners] for k in range(slots)], axis=1)
+    slots, owners = request.shape[1], request.shape[2]
+    ask.wait()
+    flat = jnp.concatenate([request[0, k : k + 1] for k in range(slots)], axis=1)
     flat = jnp.concatenate([flat, jnp.zeros((1, staged.shape[2] - owners * slots), jnp.int32)], axis=1)
     for n in range(staged.shape[0]):
         staged[n] = flat
@@ -58,7 +60,7 @@
     return jnp.maximum(asked[n, 0, (k % 2) * 32 + (k // 2) * 8 + w], 0)
 
 
-def serve_kernel(message, own, one, two, three, out, kept, asked, held, ready, load_sems, sems):
+def serve_kernel(message, own, one, two, three, out, kept, asked, held, load_sems):
     few = message.at[:, :, pl.ds(0, 128)]
     loads = [pltpu.make_async_copy(few, target, load_sems.at[n]) for n, target in enumerate((asked, kept))]
     for load in loads:
@@ -69,14 +71,9 @@
         held[(z4 - shift) & 3] = piece[...]
     for load in loads:
         load.wait()
-    copies = []
-    for n in range(ready.shape[0]):
+    for n in range(out.shape[0]):
         for k in range(8):
-            ready[n, k] = held[k // 2, asked_at(asked, n, w, k)]
-        copies.append(pltpu.make_async_copy(ready.at[n], out.at[n], sems.at[n]))
-        copies[-1].start()
-    for copy in copies:
-        copy.wait()
+            out[n, k] = held[k // 2, asked_at(asked, n, w, k)]
 
 
 def geometry_kernel(atom, places, offset, xyz, points_out, inverse_far, inverse, sems):
@@ -116,7 +113,7 @@
     columns = jnp.zeros((points, 128), F32)
     for b in range(batches):
         for p in range(rel * rel):
-            w, k = place_of(needed[b * rel * rel + p])
+            w, k = place_of(needed[b, p])
             i, j = p // rel, p % rel
             for c in range(2):
                 for y2 in range(2):
@@ -251,7 +248,7 @@
                 preferred_element_type=F32,
             )
             for j in range(rel):
-                q = needed[b * rel * rel + i * rel + j]
+                q = needed[b, i * rel + j]
                 total[q] += term[:, j * 128 : (j + 1) * 128]
 
     for w in range(8):
@@ -263,22 +260,22 @@
                     out[(y2 * 2 + c) * 8 + w, k] = total[q, first : first + 32].astype(BF16)
 
 
-def collect_kernel(asked, received, out, total):
-    total[...] = jnp.zeros_like(total)
+def collect_kernel(asked, received, out, *totals):
+    for total in totals:
+        total[...] = jnp.zeros_like(total)
     w = lax.axis_index("z2") * 4 + lax.axis_index("x")
 
     def add_one(n, _):
-        for k in range(8):
-            total[(k // 2) * 8 + asked_at(asked, n, w, k)] += received[n, k].astype(F32)
+        for k, total in enumerate(totals):
+            total[asked_at(asked, n, w, k)] += received[n, k].astype(F32)
         return 0
 
     lax.fori_loop(0, received.shape[0], add_one, 0)
-    for y4 in range(4):
-        for z4 in range(4):
-            for h in range(4):
-                pair = jnp.concatenate(
-                    [total[z4 * 8 + 2 * h + e, y4 * 8 : (y4 + 1) * 8] for e in range(2)], axis=0
-                )
+    for z4 in range(4):
+        for h in range(4):
+            two = [totals[2 * z4][2 * h + e] + totals[2 * z4 + 1][2 * h + e] for e in range(2)]
+            for y4 in range(4):
+                pair = jnp.concatenate([value[y4 * 8 : (y4 + 1) * 8] for value in two], axis=0)
                 out[y4 * 4 + z4, h * 16 : (h + 1) * 16] = pair.astype(BF16)
 
 
@@ -327,53 +324,57 @@
         prepare_kernel,
         name="prepare",
         out_shape=(pltpu.HBM((32, 1, 1024), jnp.int32), jax.ShapeDtypeStruct((own, part, tile), BF16)),
-        in_specs=vmem(1) + [hbm],
+        in_specs=[hbm, hbm],
         out_specs=(hbm, vmem(1)[0]),
-        scratch_shapes=[pltpu.VMEM((32, 1, 1024), jnp.int32), pltpu.SemaphoreType.DMA((2,))],
-        compiler_params=params,
-    )(device_request, pltpu.with_memory_space_constraint(stored_density_blocks, pltpu.HBM))
+        scratch_shapes=[
+            pltpu.VMEM((1, 2, 32), jnp.int32),
+            pltpu.VMEM((32, 1, 1024), jnp.int32),
+            pltpu.SemaphoreType.DMA((3,)),
+        ],
+        compiler_params=params,
+    )(
+        pltpu.with_memory_space_constraint(device_request.transpose(0, 2, 1), pltpu.HBM),
+        pltpu.with_memory_space_constraint(stored_density_blocks, pltpu.HBM),
+    )
     message = exchange(message, COLLECT)
     pieces = [slab] + [lax.ppermute(slab, "z4", [(i, (i + s) % 4) for i in range(4)]) for s in (1, 2, 3)]
     served, asked = pl.pallas_call(
         serve_kernel,
         name="serve",
-        out_shape=(pltpu.HBM((32, 8, part, tile), BF16), jax.ShapeDtypeStruct((32, 1, 128), jnp.int32)),
+        out_shape=(jax.ShapeDtypeStruct((32, 8, part, tile), BF16), jax.ShapeDtypeStruct((32, 1, 128), jnp.int32)),
         in_specs=[far_away] + vmem(4),
-        out_specs=(hbm, vmem(1)[0]),
+        out_specs=tuple(vmem(2)),
         scratch_shapes=[
             pltpu.SMEM((32, 1, 128), jnp.int32),
             pltpu.VMEM((4, own, part, tile), BF16),
-            pltpu.VMEM((32, 8, part, tile), BF16),
             pltpu.SemaphoreType.DMA((2,)),
-            pltpu.SemaphoreType.DMA((32,)),
         ],
         compiler_params=params,
     )(message, *pieces)
     blocks = exchange(served, COLLECT)
 
-    needed = batch_blocks.reshape(-1)
     density, density_again, share = pl.pallas_call(
         density_kernel,
         name="density",
         out_shape=(
             jax.ShapeDtypeStruct((batches, points), F32),
             jax.ShapeDtypeStruct((batches, points), F32),
-            jax.ShapeDtypeStruct((32, 1, each), F32),
+            jax.ShapeDtypeStruct((16, 1, each), F32),
         ),
         in_specs=smem(2) + vmem(4),
         out_specs=tuple(vmem(3)),
         scratch_shapes=[pltpu.VMEM((2, width, width), BF16)],
         compiler_params=params,
-    )(needed, batch_atom, basis_values, blocks, point_weight, point_offset)
+    )(batch_blocks, batch_atom, basis_values, blocks, point_weight, point_offset)
 
     shares = pl.pallas_call(
         relay_kernel,
         name="relay",
-        out_shape=jax.ShapeDtypeStruct((16, 1, 32 * each), F32),
+        out_shape=jax.ShapeDtypeStruct((32, 1, 16 * each), F32),
         in_specs=vmem(1),
         out_specs=vmem(1)[0],
         compiler_params=params,
-    )(exchange(share, COLLECT))
+    )(exchange(share, GRP))
     multipoles, outgoing = pl.pallas_call(
         term_kernel,
         name="terms",
@@ -393,8 +394,8 @@
         ],
         compiler_params=params,
     )(
-        needed,
-        exchange(shares, SETTLE),
+        batch_blocks,
+        exchange(shares, DEV),
         density_again,
         point_weight,
         exchange_kernel,
@@ -411,7 +412,7 @@
         out_shape=jax.ShapeDtypeStruct((16, own * 8, tile), BF16),
         in_specs=smem(1) + vmem(1),
         out_specs=vmem(1)[0],
-        scratch_shapes=[pltpu.VMEM((4 * own, 32, tile), F32)],
+        scratch_shapes=[pltpu.VMEM((own, 32, tile), F32)] * 8,
         compiler_params=params,
     )(asked, received)
     settled = exchange(partial, SETTLE).astype(F32).sum(axis=0).astype(BF16)

time: 183 us -> 178 us (0.973)
  blocking collectives: 59.9 us -> 97.1 us
  waiting for transfers between devices: 49.7 us -> 20.3 us
  starting transfers between devices: 49.7 us -> 37.8 us
    all_to_all x3 -> x4, blocking collectives: 59.9 us -> 97.1 us  [exchange(): return lax.all_to_all(value, axes, split_axis=0, concat_axis=0, tiled=True)]
    all_to_all x4 -> x3, waiting for transfers between devices: 45.2 us -> 15.8 us  [exchange(): return lax.all_to_all(value, axes, split_axis=0, concat_axis=0, tiled=True)]
    all_to_all x4 -> x3, starting transfers between devices: 35.4 us -> 23.6 us  [exchange(): return lax.all_to_all(value, axes, split_axis=0, concat_axis=0, tiled=True)]
  transfers between devices with their start and end apart: 7 -> 6, of which waited for: 4 -> 3; matrix products, arithmetic and copies ran while one was open for 0% -> 0% of each run, Pallas kernels for 2% -> 2%
where the time goes in v4:
time: 178 us; the launch traced here: 177 us
  blocking collectives  97.1 us (55%)
  starting transfers between devices  37.8 us (21%)
  waiting for transfers between devices  20.3 us (11%)
  Pallas kernels  18.8 us (11%)
  local copies, waits for them, and re-layouts  2.2 us (1%)
    all_to_all x4, blocking collectives, exchange(): return lax.all_to_all(value, axes, split_axis=0, concat_axis=0, tiled=True)  97.1 us
    all_to_all x3, starting transfers between devices, exchange(): return lax.all_to_all(value, axes, split_axis=0, concat_axis=0, tiled=True)  23.6 us
    all_to_all x3, waiting for transfers between devices, exchange(): return lax.all_to_all(value, axes, split_axis=0, concat_axis=0, tiled=True)  15.8 us
    ppermute x3, starting transfers between devices, on_device(): lax.ppermute(slab, 'z4', [(i, (i + s) % 4) for i in range(4)])  14.3 us
    pallas_call x1, Pallas kernels, on_device(): pl.pallas_call(term_kernel, name='terms', out_shape=(jax.ShapeDtypeStruct...  6.96 us
    ppermute x3, waiting for transfers between devices, on_device(): lax.ppermute(slab, 'z4', [(i, (i + s) % 4) for i in range(4)])  4.5 us
    pallas_call x1, Pallas kernels, on_device(): pl.pallas_call(geometry_kernel, name='geometry', out_shape=(pltpu.VMEM((3...  4.1 us
  transfers between devices with their start and end apart: 6, of which 3 were waited for; matrix products, arithmetic and copies ran while one was open for 0% of the time, Pallas kernels for 2%

profile of v4, /device:TPU:1, one launch (start us, length us, event | category | flops | bytes accessed | tf_op | source)
XLA Modules:
  0.0 177.0 jit_solution(15182787127534861714)
XLA Ops:
  0.6 1.4 prepare.1
  2.1 10.4 %all-to-all-start = ((s32[32,1,1024]{2,1,0:T(1,128)}), s32[32,1,1024]{2,1,0:T(1,128)S(1)}, u32[]{:S(2)}, u32[]{:S(2)}) async-start(s32[32,1,1024]{2,1,0:T(1,128)} %get-tuple-element.14), calls=%async_computation | async-start | bytes 262144 | tf_op jit(solution)/shard_map/all_to_all | solution.py:24
  12.5 8.1 %collective-permute-start.2 = (bf16[8,32,128]{2,1,0:T(8,128)(2,1)S(1)}, bf16[8,32,128]{2,1,0:T(8,128)(2,1)S(1)}, u32[]{:S(2)}, u32[]{:S(2)}) collective-permute-start(bf16[8,32,128]{2,1,0:T(8,128)(2,1)S(1)} %get-tuple-element.15.own), channel_id=1, source_target_pairs={{0,24},{8,0},{16,8},{24,16},{1,25},{9,1},{17,9},{25,17},{2,26},{10... | collective-permute-start | bytes 196616 | tf_op jit(solution)/shard_map/ppermute | solution.py:340
  20.6 1.9 %collective-permute-start.1 = (bf16[8,32,128]{2,1,0:T(8,128)(2,1)S(1)}, bf16[8,32,128]{2,1,0:T(8,128)(2,1)S(1)}, u32[]{:S(2)}, u32[]{:S(2)}) collective-permute-start(bf16[8,32,128]{2,1,0:T(8,128)(2,1)S(1)} %get-tuple-element.15.own), channel_id=1, source_target_pairs={{0,16},{8,24},{16,0},{24,8},{1,17},{9,25},{17,1},{25,9},{2,18},{10... | collective-permute-start | bytes 196616 | tf_op jit(solution)/shard_map/ppermute | solution.py:340
  22.6 4.2 %collective-permute-start = (bf16[8,32,128]{2,1,0:T(8,128)(2,1)S(1)}, bf16[8,32,128]{2,1,0:T(8,128)(2,1)S(1)}, u32[]{:S(2)}, u32[]{:S(2)}) collective-permute-start(bf16[8,32,128]{2,1,0:T(8,128)(2,1)S(1)} %get-tuple-element.15.own), channel_id=1, source_target_pairs={{0,8},{8,16},{16,24},{24,0},{1,9},{9,17},{17,25},{25,1},{2,10},{10... | collective-permute-start | bytes 196616 | tf_op jit(solution)/shard_map/ppermute | solution.py:340
  26.8 0.0 collective-permute-done.2.three
  26.8 4.5 %collective-permute-done.1.two = bf16[8,32,128]{2,1,0:T(8,128)(2,1)S(1)} collective-permute-done((bf16[8,32,128]{2,1,0:T(8,128)(2,1)S(1)}, bf16[8,32,128]{2,1,0:T(8,128)(2,1)S(1)}, u32[]{:S(2)}, u32[]{:S(2)}) %collective-permute-start.1) | collective-permute-done | bytes 65568 | tf_op jit(solution)/shard_map/ppermute | solution.py:340
  31.3 0.0 collective-permute-done.one
  31.3 1.3 serve.1
  32.7 0.0 copy-start
  32.7 0.0 copy-start.1
  32.7 0.0 copy-start.3
  32.7 0.0 copy-start.4
  32.7 0.0 copy-start.6
  32.7 35.5 %all_to_all.35.blocks = bf16[32,8,32,128]{3,2,1,0:T(8,128)(2,1)S(1)} all-to-all(bf16[32,8,32,128]{3,2,1,0:T(8,128)(2,1)S(1)} %get-tuple-element.17), channel_id=1, replica_groups=mesh['y4'=4,'y2'=2,'c'=2,'z4'=4,'z2'=2,'x'=4] {'y2','c','z2','x'}, dimensions={0} | all-to-all | bytes 4194304 | tf_op jit(solution)/shard_map/all_to_all | solution.py:24
  68.3 0.0 copy-start.2
  68.3 0.0 copy-start.5
  68.3 2.3 %density.1 = (f32[4,256]{1,0:T(4,128)}, f32[4,256]{1,0:T(4,128)S(1)}, f32[16,1,32]{2,1,0:T(1,128)S(1)}) custom-call(s32[4,16]{1,0:T(4,128)S(1)} %copy-done.4, s32[4]{0:T(128)S(1)} %copy-done.6, bf16[4,256,512]{2,1,0:T(8,128)(2,1)S(1)} %copy-done, bf16[32,8,32,128]{3,2,1,0:T(8,128)(2,1)S(1)} %all_to_all.35.blocks, f32[4,256]{1,0:T(4,128)S(1)} %copy-done.1, ...), custom_call_target="tpu_custom_call" | custom-call | tf_op jit(solution)/shard_map/density/pallas_call | solution.py:356
  70.6 14.0 %all_to_all.36.near = f32[16,1,32]{2,1,0:T(1,128)S(1)} all-to-all(f32[16,1,32]{2,1,0:T(1,128)S(1)} %get-tuple-element.18), channel_id=1, replica_groups=mesh['y4'=4,'y2'=2,'c'=2,'z4'=4,'z2'=2,'x'=4] {'y4','y2','c'}, dimensions={0} | all-to-all | bytes 4096 | tf_op jit(solution)/shard_map/all_to_all | solution.py:24
  84.6 0.7 relay.1
  85.4 6.6 %all-to-all-start.3 = ((f32[32,1,512]{2,1,0:T(1,128)}), f32[32,1,512]{2,1,0:T(1,128)S(1)}, u32[]{:S(2)}, u32[]{:S(2)}) async-start(f32[32,1,512]{2,1,0:T(1,128)} %relay.1), calls=%async_computation.3 | async-start | bytes 131072 | tf_op jit(solution)/shard_map/all_to_all | solution.py:24
  92.0 4.1 %geometry.1 = (f32[3,128,8,128]{3,2,1,0:T(8,128)S(1)}, f32[4,8,32,8,128]{4,3,2,1,0:T(8,128)}) custom-call(s32[4]{0:T(128)S(1)} %copy-done.6, f32[3,1000]{1,0:T(4,128)S(1)} %copy-done.2, f32[3,4,256]{2,1,0:T(4,128)S(1)} %copy-done.3, f32[3,8,128]{2,1,0:T(8,128)S(1)} %bitcast.11), custom_call_target="tpu_custom_call" | custom-call | flops 20000000 | bytes 6291456 | tf_op jit(solution)/shard_map/geometry/pallas_call | solution.py:306
  96.1 4.7 %all-to-all-done.3.shares = f32[32,1,512]{2,1,0:T(1,128)S(1)} async-done(((f32[32,1,512]{2,1,0:T(1,128)}), f32[32,1,512]{2,1,0:T(1,128)S(1)}, u32[]{:S(2)}, u32[]{:S(2)}) %all-to-all-start.3) | async-done | bytes 65568 | tf_op jit(solution)/shard_map/all_to_all | solution.py:24
  100.7 7.0 %terms.1 = (f32[32,128]{1,0:T(8,128)S(1)}, bf16[32,8,32,128]{3,2,1,0:T(8,128)(2,1)S(1)}) custom-call(s32[4,16]{1,0:T(4,128)S(1)} %copy-done.4, f32[32,1,512]{2,1,0:T(1,128)S(1)} %all-to-all-done.3.shares, f32[4,256]{1,0:T(4,128)S(1)} %get-tuple-element.19.rho, f32[4,256]{1,0:T(4,128)S(1)} %copy-done.1, f32[4,256]{1,0:T(4,128)S(1)} %copy-done.5, ...), custom_call_target="tpu_custom_call" | custom-call | tf_op jit(solution)/shard_map/terms/pallas_call | solution.py:378
  107.7 31.6 %all_to_all.37.received = bf16[32,8,32,128]{3,2,1,0:T(8,128)(2,1)S(1)} all-to-all(bf16[32,8,32,128]{3,2,1,0:T(8,128)(2,1)S(1)} %get-tuple-element.22), channel_id=1, replica_groups=mesh['y4'=4,'y2'=2,'c'=2,'z4'=4,'z2'=2,'x'=4] {'y2','c','z2','x'}, dimensions={0} | all-to-all | bytes 4194304 | tf_op jit(solution)/shard_map/all_to_all | solution.py:24
  139.3 1.9 %collect.1 = bf16[16,64,128]{2,1,0:T(8,128)(2,1)S(1)} custom-call(s32[32,1,128]{2,1,0:T(1,128)S(1)} %get-tuple-element.16.asked, bf16[32,8,32,128]{3,2,1,0:T(8,128)(2,1)S(1)} %all_to_all.37.received), custom_call_target="tpu_custom_call" | custom-call | tf_op jit(solution)/shard_map/collect/pallas_call | solution.py:409
  141.1 16.0 %all_to_all.38 = bf16[16,64,128]{2,1,0:T(8,128)(2,1)S(1)} all-to-all(bf16[16,64,128]{2,1,0:T(8,128)(2,1)S(1)} %collect.1), channel_id=1, replica_groups=mesh['y4'=4,'y2'=2,'c'=2,'z4'=4,'z2'=2,'x'=4] {'y4','z4'}, dimensions={0} | all-to-all | bytes 524288 | tf_op jit(solution)/shard_map/all_to_all | solution.py:24
  157.2 0.8 broadcast_in_dim.2
  158.0 6.5 %all-to-all-start.6 = ((bf16[16,64,128]{2,1,0:T(8,128)(2,1)}), bf16[16,64,128]{2,1,0:T(8,128)(2,1)S(1)}, u32[]{:S(2)}, u32[]{:S(2)}) async-start(bf16[16,64,128]{2,1,0:T(8,128)(2,1)} %broadcast_in_dim.2), calls=%async_computation.6 | async-start | bytes 524288 | tf_op jit(solution)/shard_map/all_to_all | solution.py:24
  164.5 0.6 reshape.22
  165.1 11.1 %all-to-all-done.6 = bf16[16,64,128]{2,1,0:T(8,128)(2,1)S(1)} async-done(((bf16[16,64,128]{2,1,0:T(8,128)(2,1)}), bf16[16,64,128]{2,1,0:T(8,128)(2,1)S(1)}, u32[]{:S(2)}, u32[]{:S(2)}) %all-to-all-start.6) | async-done | bytes 262176 | tf_op jit(solution)/shard_map/all_to_all | solution.py:24
  176.2 0.8 copy.12
  (11 shorter events, 0.1 us)
Async XLA Ops:
  2.1 29.3 %all-to-all-start = ((s32[32,1,1024]{2,1,0:T(1,128)}), s32[32,1,1024]{2,1,0:T(1,128)S(1)}, u32[]{:S(2)}, u32[]{:S(2)}) async-start(s32[32,1,1024]{2,1,0:T(1,128)} %get-tuple-element.14), calls=%async_computation | async-start | bytes 262144 | tf_op jit(solution)/shard_map/all_to_all | solution.py:24
  12.5 14.3 %collective-permute-start.2 = (bf16[8,32,128]{2,1,0:T(8,128)(2,1)S(1)}, bf16[8,32,128]{2,1,0:T(8,128)(2,1)S(1)}, u32[]{:S(2)}, u32[]{:S(2)}) collective-permute-start(bf16[8,32,128]{2,1,0:T(8,128)(2,1)S(1)} %get-tuple-element.15.own), channel_id=1, source_target_pairs={{0,24},{8,0},{16,8},{24,16},{1,25},{9,1},{17,9},{25,17},{2,26},{10... | collective-permute-start | bytes 196616 | tf_op jit(solution)/shard_map/ppermute | solution.py:340
  20.6 10.7 %collective-permute-start.1 = (bf16[8,32,128]{2,1,0:T(8,128)(2,1)S(1)}, bf16[8,32,128]{2,1,0:T(8,128)(2,1)S(1)}, u32[]{:S(2)}, u32[]{:S(2)}) collective-permute-start(bf16[8,32,128]{2,1,0:T(8,128)(2,1)S(1)} %get-tuple-element.15.own), channel_id=1, source_target_pairs={{0,16},{8,24},{16,0},{24,8},{1,17},{9,25},{17,1},{25,9},{2,18},{10... | collective-permute-start | bytes 196616 | tf_op jit(solution)/shard_map/ppermute | solution.py:340
  22.6 8.8 %collective-permute-start = (bf16[8,32,128]{2,1,0:T(8,128)(2,1)S(1)}, bf16[8,32,128]{2,1,0:T(8,128)(2,1)S(1)}, u32[]{:S(2)}, u32[]{:S(2)}) collective-permute-start(bf16[8,32,128]{2,1,0:T(8,128)(2,1)S(1)} %get-tuple-element.15.own), channel_id=1, source_target_pairs={{0,8},{8,16},{16,24},{24,0},{1,9},{9,17},{17,25},{25,1},{2,10},{10... | collective-permute-start | bytes 196616 | tf_op jit(solution)/shard_map/ppermute | solution.py:340
  32.7 35.6 %copy-start = (bf16[4,256,512]{2,1,0:T(8,128)(2,1)S(1)}, bf16[4,256,512]{2,1,0:T(8,128)(2,1)}, u32[]{:S(2)}) copy-start(bf16[4,256,512]{2,1,0:T(8,128)(2,1)} %phi.3) | copy-start | bytes 3145732
  32.7 35.6 %copy-start.1 = (f32[4,256]{1,0:T(4,128)S(1)}, f32[4,256]{1,0:T(4,128)}, u32[]{:S(2)}) copy-start(f32[4,256]{1,0:T(4,128)} %weight.3) | copy-start | bytes 12292
  32.7 35.5 %copy-start.3 = (f32[3,4,256]{2,1,0:T(4,128)S(1)}, f32[3,4,256]{2,1,0:T(4,128)}, u32[]{:S(2)}) copy-start(f32[3,4,256]{2,1,0:T(4,128)} %offset.3) | copy-start | bytes 36868
  32.7 35.5 %copy-start.4 = (s32[4,16]{1,0:T(4,128)S(1)}, s32[4,16]{1,0:T(4,128)}, u32[]{:S(2)}) copy-start(s32[4,16]{1,0:T(4,128)} %needed.3) | copy-start | bytes 772
  32.7 35.5 %copy-start.6 = (s32[4]{0:T(128)S(1)}, s32[4]{0:T(128)}, u32[]{:S(2)}) copy-start(s32[4]{0:T(128)} %atom.3) | copy-start | bytes 52
  68.3 23.6 %copy-start.2 = (f32[3,1000]{1,0:T(4,128)S(1)}, f32[3,1000]{1,0:T(4,128)}, u32[]{:S(2)}) copy-start(f32[3,1000]{1,0:T(4,128)} %places.1) | copy-start | bytes 36004
  68.3 32.5 %copy-start.5 = (f32[4,256]{1,0:T(4,128)S(1)}, f32[4,256]{1,0:T(4,128)}, u32[]{:S(2)}) copy-start(f32[4,256]{1,0:T(4,128)} %exchange_part.1) | copy-start | bytes 12292
  85.4 15.4 %all-to-all-start.3 = ((f32[32,1,512]{2,1,0:T(1,128)}), f32[32,1,512]{2,1,0:T(1,128)S(1)}, u32[]{:S(2)}, u32[]{:S(2)}) async-start(f32[32,1,512]{2,1,0:T(1,128)} %relay.1), calls=%async_computation.3 | async-start | bytes 131072 | tf_op jit(solution)/shard_map/all_to_all | solution.py:24
  158.0 18.3 %all-to-all-start.6 = ((bf16[16,64,128]{2,1,0:T(8,128)(2,1)}), bf16[16,64,128]{2,1,0:T(8,128)(2,1)S(1)}, u32[]{:S(2)}, u32[]{:S(2)}) async-start(bf16[16,64,128]{2,1,0:T(8,128)(2,1)} %broadcast_in_dim.2), calls=%async_computation.6 | async-start | bytes 524288 | tf_op jit(solution)/shard_map/all_to_all | solution.py:24

commit v5 on v4

--- a/solution.py
+++ b/solution.py
@@ -76,29 +76,42 @@
             out[n, k] = held[k // 2, asked_at(asked, n, w, k)]
 
 
-def geometry_kernel(atom, places, offset, xyz, points_out, inverse_far, inverse, sems):
+def three_parts(value):
+    parts = []
+    for _ in range(3):
+        parts.append(value.astype(BF16).astype(F32))
+        value = value - parts[-1]
+    return parts
+
+
+def geometry_kernel(atom, places, offset, xyz, phi, left_out, turned_out, inverse_far, inverse, spots, sems):
     batches, points = offset.shape[1], offset.shape[2]
     chunks = xyz.shape[1]
-    rows = points // 8
-    filler = jnp.zeros((128 - 3 * batches, points), F32)
-    features = jnp.concatenate([offset[0], offset[1], offset[2], filler], axis=0).T
+    ones = jnp.ones((1, points), F32)
+    filler = jnp.zeros((128 - 24, points), F32)
     copies = []
     for b in range(batches):
+        spot = [offset[k, b : b + 1] + places[k, atom[b]] for k in range(3)] + [ones]
+        spot = jnp.concatenate(spot, axis=0)
+        high, middle, low = three_parts(spot)
+        stacked = jnp.concatenate([high, high, middle, high, low, middle, filler], axis=0)
+        left_out[b] = stacked.T.astype(BF16)
+        turned_out[b] = phi[b].T
+        columns = jnp.concatenate([spot, jnp.zeros((124, points), F32)], axis=0).T
         for k in range(3):
-            spot = features[:, k * batches + b : k * batches + b + 1] + places[k, atom[b]]
-            points_out[k, b * rows : (b + 1) * rows] = jnp.broadcast_to(spot, (points, 128)).reshape(rows, 8, 128)
+            spots[k] = jnp.broadcast_to(columns[:, k : k + 1], (points, 128))
 
         def inverse_of(step, _, b=b):
-            at = pl.ds(step * 8, 8)
-            px, py, pz = (points_out[k, pl.ds(b * rows + step * 8, 8)] for k in range(3))
+            at = pl.ds(step * 64, 64)
+            px, py, pz = (spots[k, at] for k in range(3))
             for h in range(chunks):
-                gx = px - xyz[0, h : h + 1][None]
-                gy = py - xyz[1, h : h + 1][None]
-                gz = pz - xyz[2, h : h + 1][None]
+                gx = px - xyz[0, h : h + 1]
+                gy = py - xyz[1, h : h + 1]
+                gz = pz - xyz[2, h : h + 1]
                 inverse[b, h, at] = lax.rsqrt(gx * gx + gy * gy + gz * gz + 1.0)
             return 0
 
-        lax.fori_loop(0, rows // 8, inverse_of, 0)
+        lax.fori_loop(0, points // 64, inverse_of, 0)
         copies.append(pltpu.make_async_copy(inverse.at[b], inverse_far.at[b], sems.at[b]))
         copies[-1].start()
     for copy in copies:
@@ -158,27 +171,28 @@
     weight,
     exchange_part,
     xyz,
-    points_at,
+    left,
+    turned_phi,
     phi,
     inverse_far,
     multipoles_out,
     out,
     inverse,
     rows,
-    spread,
-    potential,
+    right,
     total,
     load_sems,
 ):
-    loads = [pltpu.make_async_copy(inverse_far.at[b], inverse.at[b], load_sems.at[b]) for b in range(phi.shape[0])]
+    batches, points, width = phi.shape
+    loads = [pltpu.make_async_copy(inverse_far.at[b], inverse.at[b], load_sems.at[b]) for b in range(batches)]
     for load in loads:
         load.start()
-    batches, points, width = phi.shape
     rel = width // 128
     devices = rows.shape[0]
     sources = shares.shape[0]
     each = batches * VALUES
     chunks = xyz.shape[1]
+    atoms = multipoles_out.shape[1]
 
     rows[...] = jnp.zeros_like(rows)
     near = shares[...].reshape(sources, shares.shape[2])
@@ -192,12 +206,9 @@
     for b in range(batches):
         low = jnp.where(table[:, b * VALUES + 4 : b * VALUES + 5] == low_at, 1.0, 0.0).astype(BF16)
         high = jnp.where(turned[b * VALUES + 5 : b * VALUES + 6] == high_at, 1.0, 0.0)
-        rest = turned[b * VALUES : (b + 1) * VALUES]
         stacked = []
-        for _ in range(3):
-            part = rest.astype(BF16).astype(F32)
-            rest = rest - part
-            stacked += [high * part[k : k + 1] for k in range(4)]
+        for piece in three_parts(turned[b * VALUES : (b + 1) * VALUES]):
+            stacked += [high * piece[k : k + 1] for k in range(4)]
         stacked = jnp.concatenate(stacked, axis=0).astype(BF16)
         summed = summed + jnp.dot(stacked, low, preferred_element_type=F32)
     multipoles = [
@@ -206,47 +217,31 @@
         for k in range(4)
     ]
     for k in range(4):
-        multipoles_out[k * chunks : (k + 1) * chunks] = multipoles[k]
+        for h in range(chunks):
+            count = min(128, atoms - h * 128)
+            multipoles_out[k : k + 1, h * 128 : h * 128 + count] = multipoles[k][h : h + 1, :count]
+
     shift = multipoles[1] * xyz[0] + multipoles[2] * xyz[1] + multipoles[3] * xyz[2]
-    for k, value in enumerate(multipoles + [shift]):
+    parts = [three_parts(value) for value in (multipoles[1], multipoles[2], multipoles[3], -shift)]
+    right[...] = jnp.zeros_like(right)
+    for h in range(chunks):
+        stacked = [parts[k][n][h : h + 1] for n in (0, 1, 0, 2, 0, 1) for k in range(4)]
+        stacked = jnp.concatenate(stacked + [jnp.zeros((8, 128), F32)], axis=0)
+        right[:32, h * 128 : (h + 1) * 128] = stacked.astype(BF16)
+
+    total[...] = jnp.zeros_like(total)
+    for b in range(batches):
+        dipole = jnp.dot(left[b], right[...], preferred_element_type=F32)
+        loads[b].wait()
+        acc = jnp.zeros((points, 128), F32)
         for h in range(chunks):
-            spread[k * chunks + h] = jnp.broadcast_to(value[h : h + 1], (8, 128))
-
-    filler = jnp.zeros((128 - 2 * batches, points), F32)
-    features = jnp.concatenate([weight[...], exchange_part[...] * rho[...], filler], axis=0).T
-    total[...] = jnp.zeros_like(total)
-    rows_each = points // 8
-    for b in range(batches):
-        loads[b].wait()
-
-        def potential_of(step, _, b=b):
-            at = pl.ds(step * 8, 8)
-            px, py, pz = (points_at[k, pl.ds(b * rows_each + step * 8, 8)] for k in range(3))
-            acc = jnp.zeros((8, 8, 128), F32)
-            for h in range(chunks):
-                dipole = (
-                    spread[chunks + h][None] * px
-                    + spread[2 * chunks + h][None] * py
-                    + spread[3 * chunks + h][None] * pz
-                    - spread[4 * chunks + h][None]
-                )
-                s = inverse[b, h, at]
-                acc = acc + s * (spread[h][None] + dipole * (s * s))
-            potential[at] = acc
-            return 0
-
-        lax.fori_loop(0, rows_each // 8, potential_of, 0)
-        hartree = jnp.sum(potential[...].reshape(points, 128), axis=1, keepdims=True)
-        factor = features[:, b : b + 1] * (features[:, batches + b : batches + b + 1] + hartree)
-        values = phi[b]
-        scaled = (values.astype(F32) * factor).astype(BF16)
+            s = inverse[b, h]
+            acc = acc + s * (multipoles[0][h : h + 1] + dipole[:, h * 128 : (h + 1) * 128] * (s * s))
+        hartree = jnp.sum(acc.T, axis=0, keepdims=True)
+        factor = weight[b : b + 1] * (exchange_part[b : b + 1] * rho[b : b + 1] + hartree)
+        scaled = (turned_phi[b].astype(F32) * factor).astype(BF16)
         for i in range(rel):
-            term = lax.dot_general(
-                scaled[:, i * 128 : (i + 1) * 128],
-                values,
-                (((0,), (0,)), ((), ())),
-                preferred_element_type=F32,
-            )
+            term = jnp.dot(scaled[i * 128 : (i + 1) * 128], phi[b], preferred_element_type=F32)
             for j in range(rel):
                 q = needed[b, i * rel + j]
                 total[q] += term[:, j * 128 : (j + 1) * 128]
@@ -277,6 +272,15 @@
             for y4 in range(4):
                 pair = jnp.concatenate([value[y4 * 8 : (y4 + 1) * 8] for value in two], axis=0)
                 out[y4 * 4 + z4, h * 16 : (h + 1) * 16] = pair.astype(BF16)
+
+
+def settle_kernel(received, out):
+    summed = received[0].astype(F32)
+    for n in range(1, received.shape[0]):
+        summed = summed + received[n].astype(F32)
+    summed = summed.astype(BF16)
+    for n in range(out.shape[0]):
+        out[n] = summed
 
 
 def on_device(
@@ -297,28 +301,29 @@
     part = tile // 4
     chunks = padded // 128
     each = batches * VALUES
-    groups = batches * points // 8
     params = pltpu.CompilerParams(vmem_limit_bytes=32 * MIB)
     hbm = pl.BlockSpec(memory_space=pltpu.HBM)
-    far_away = pl.BlockSpec(memory_space=pl.ANY)
+    anywhere = pl.BlockSpec(memory_space=pl.ANY)
 
     far = jnp.pad(atom_xyz, ((0, 0), (0, padded - atoms))).reshape(3, chunks, 128)
-    points_at, inverse = pl.pallas_call(
+    left, turned_phi, inverse = pl.pallas_call(
         geometry_kernel,
         name="geometry",
         out_shape=(
-            pltpu.VMEM((3, groups, 8, 128), F32),
-            pltpu.HBM((batches, chunks, points // 8, 8, 128), F32),
+            jax.ShapeDtypeStruct((batches, points, 128), BF16),
+            jax.ShapeDtypeStruct((batches, width, points), BF16),
+            pltpu.HBM((batches, chunks, points, 128), F32),
         ),
-        in_specs=smem(2) + vmem(2),
-        out_specs=(vmem(1)[0], hbm),
+        in_specs=smem(2) + vmem(3),
+        out_specs=tuple(vmem(2)) + (hbm,),
         scratch_shapes=[
-            pltpu.VMEM((batches, chunks, points // 8, 8, 128), F32),
+            pltpu.VMEM((batches, chunks, points, 128), F32),
+            pltpu.VMEM((3, points, 128), F32),
             pltpu.SemaphoreType.DMA((batches,)),
         ],
         compiler_params=params,
         cost_estimate=pl.CostEstimate(flops=2 * 10**7, bytes_accessed=6 * MIB, transcendentals=10**6),
-    )(batch_atom, atom_xyz, point_offset, far)
+    )(batch_atom, atom_xyz, point_offset, far, basis_values)
 
     message, slab = pl.pallas_call(
         prepare_kernel,
@@ -342,7 +347,7 @@
         serve_kernel,
         name="serve",
         out_shape=(jax.ShapeDtypeStruct((32, 8, part, tile), BF16), jax.ShapeDtypeStruct((32, 1, 128), jnp.int32)),
-        in_specs=[far_away] + vmem(4),
+        in_specs=[anywhere] + vmem(4),
         out_specs=tuple(vmem(2)),
         scratch_shapes=[
             pltpu.SMEM((32, 1, 128), jnp.int32),
@@ -379,16 +384,15 @@
         term_kernel,
         name="terms",
         out_shape=(
-            jax.ShapeDtypeStruct((4 * chunks, 128), F32),
+            jax.ShapeDtypeStruct((4, atoms), F32),
             jax.ShapeDtypeStruct((32, 8, 32, tile), BF16),
         ),
-        in_specs=smem(1) + vmem(7) + [hbm],
+        in_specs=smem(1) + vmem(8) + [hbm],
         out_specs=tuple(vmem(2)),
         scratch_shapes=[
             pltpu.VMEM(inverse.shape, F32),
             pltpu.VMEM((512, 128), F32),
-            pltpu.VMEM((5 * chunks, 8, 128), F32),
-            pltpu.VMEM((points // 8, 8, 128), F32),
+            pltpu.VMEM((128, padded), BF16),
             pltpu.VMEM((64, tile, tile), F32),
             pltpu.SemaphoreType.DMA((batches,)),
         ],
@@ -400,7 +404,8 @@
         point_weight,
         exchange_kernel,
         far,
-        pltpu.with_memory_space_constraint(points_at, pltpu.VMEM),
+        left,
+        turned_phi,
         basis_values,
         pltpu.with_memory_space_constraint(inverse, pltpu.HBM),
     )
@@ -415,10 +420,17 @@
         scratch_shapes=[pltpu.VMEM((own, 32, tile), F32)] * 8,
         compiler_params=params,
     )(asked, received)
-    settled = exchange(partial, SETTLE).astype(F32).sum(axis=0).astype(BF16)
-    rows = exchange(jnp.broadcast_to(settled[None], (16, own * 8, tile)), GRP)
+    settled = pl.pallas_call(
+        settle_kernel,
+        name="settle",
+        out_shape=jax.ShapeDtypeStruct((16, own * 8, tile), BF16),
+        in_specs=vmem(1),
+        out_specs=vmem(1)[0],
+        compiler_params=params,
+    )(exchange(partial, SETTLE))
+    rows = exchange(settled, GRP)
     rows = rows.reshape(4, 2, 2, own, 8, tile).transpose(3, 2, 1, 0, 4, 5)
-    return (rows.reshape(own, tile, tile), density, multipoles.reshape(4, padded)[:, :atoms])
+    return (rows.reshape(own, tile, tile), density, multipoles)
 
 
 def solution(mesh):

time: 178 us -> 175 us (0.983)
  blocking collectives: 97.1 us -> 116 us
  waiting for transfers between devices: 20.3 us -> 8.4 us
  starting transfers between devices: 37.8 us -> 31.3 us
    all_to_all x4 -> x5, blocking collectives: 97.1 us -> 116 us  [exchange(): return lax.all_to_all(value, axes, split_axis=0, concat_axis=0, tiled=True)]
    all_to_all x3 -> x2, waiting for transfers between devices: 15.8 us -> 3.89 us  [exchange(): return lax.all_to_all(value, axes, split_axis=0, concat_axis=0, tiled=True)]
    all_to_all x3 -> x2, starting transfers between devices: 23.6 us -> 17 us  [exchange(): return lax.all_to_all(value, axes, split_axis=0, concat_axis=0, tiled=True)]
    pallas_call x1 -> x2, Pallas kernels: 4.1 us -> 4.93 us  [the longest x1 4.89 us: on_device(): pl.pallas_call(geometry_kernel, name='geometry', out_shape=(jax.ShapeDtyp...]
  transfers between devices with their start and end apart: 6 -> 5, of which waited for: 3 -> 2; matrix products, arithmetic and copies ran while one was open for 0% -> 0% of each run, Pallas kernels for 2% -> 3%
where the time goes in v5:
time: 175 us
  blocking collectives  116 us (66%)
  starting transfers between devices  31.3 us (18%)
  Pallas kernels  17.8 us (10%)
  waiting for transfers between devices  8.4 us (5%)
    all_to_all x5, blocking collectives, exchange(): return lax.all_to_all(value, axes, split_axis=0, concat_axis=0, tiled=True)  116 us
    all_to_all x2, starting transfers between devices, exchange(): return lax.all_to_all(value, axes, split_axis=0, concat_axis=0, tiled=True)  17 us
    ppermute x3, starting transfers between devices, on_device(): lax.ppermute(slab, 'z4', [(i, (i + s) % 4) for i in range(4)])  14.3 us
    pallas_call x1, Pallas kernels, on_device(): pl.pallas_call(term_kernel, name='terms', out_shape=(jax.ShapeDtypeStruct...  5.2 us
    pallas_call x1, Pallas kernels, on_device(): pl.pallas_call(geometry_kernel, name='geometry', out_shape=(jax.ShapeDtyp...  4.89 us
    ppermute x3, waiting for transfers between devices, on_device(): lax.ppermute(slab, 'z4', [(i, (i + s) % 4) for i in range(4)])  4.5 us
    all_to_all x2, waiting for transfers between devices, exchange(): return lax.all_to_all(value, axes, split_axis=0, concat_axis=0, tiled=True)  3.89 us
  transfers between devices with their start and end apart: 5, of which 2 were waited for; matrix products, arithmetic and copies ran while one was open for 0% of the time, Pallas kernels for 3%

profile of v5, /device:TPU:1, one launch (start us, length us, event | category | flops | bytes accessed | tf_op | source)
XLA Modules:
  0.0 174.9 jit_solution(17033170732405299983)
XLA Ops:
  0.6 1.4 prepare.1
  2.1 10.4 %all-to-all-start = ((s32[32,1,1024]{2,1,0:T(1,128)}), s32[32,1,1024]{2,1,0:T(1,128)S(1)}, u32[]{:S(2)}, u32[]{:S(2)}) async-start(s32[32,1,1024]{2,1,0:T(1,128)} %get-tuple-element.15), calls=%async_computation | async-start | bytes 262144 | tf_op jit(solution)/shard_map/all_to_all | solution.py:24
  12.5 8.1 %collective-permute-start.2 = (bf16[8,32,128]{2,1,0:T(8,128)(2,1)S(1)}, bf16[8,32,128]{2,1,0:T(8,128)(2,1)S(1)}, u32[]{:S(2)}, u32[]{:S(2)}) collective-permute-start(bf16[8,32,128]{2,1,0:T(8,128)(2,1)S(1)} %get-tuple-element.16.own), channel_id=1, source_target_pairs={{0,24},{8,0},{16,8},{24,16},{1,25},{9,1},{17,9},{25,17},{2,26},{10... | collective-permute-start | bytes 196616 | tf_op jit(solution)/shard_map/ppermute | solution.py:345
  20.6 1.9 %collective-permute-start.1 = (bf16[8,32,128]{2,1,0:T(8,128)(2,1)S(1)}, bf16[8,32,128]{2,1,0:T(8,128)(2,1)S(1)}, u32[]{:S(2)}, u32[]{:S(2)}) collective-permute-start(bf16[8,32,128]{2,1,0:T(8,128)(2,1)S(1)} %get-tuple-element.16.own), channel_id=1, source_target_pairs={{0,16},{8,24},{16,0},{24,8},{1,17},{9,25},{17,1},{25,9},{2,18},{10... | collective-permute-start | bytes 196616 | tf_op jit(solution)/shard_map/ppermute | solution.py:345
  22.6 4.2 %collective-permute-start = (bf16[8,32,128]{2,1,0:T(8,128)(2,1)S(1)}, bf16[8,32,128]{2,1,0:T(8,128)(2,1)S(1)}, u32[]{:S(2)}, u32[]{:S(2)}) collective-permute-start(bf16[8,32,128]{2,1,0:T(8,128)(2,1)S(1)} %get-tuple-element.16.own), channel_id=1, source_target_pairs={{0,8},{8,16},{16,24},{24,0},{1,9},{9,17},{17,25},{25,1},{2,10},{10... | collective-permute-start | bytes 196616 | tf_op jit(solution)/shard_map/ppermute | solution.py:345
  26.8 0.0 collective-permute-done.2.three
  26.8 4.5 %collective-permute-done.1.two = bf16[8,32,128]{2,1,0:T(8,128)(2,1)S(1)} collective-permute-done((bf16[8,32,128]{2,1,0:T(8,128)(2,1)S(1)}, bf16[8,32,128]{2,1,0:T(8,128)(2,1)S(1)}, u32[]{:S(2)}, u32[]{:S(2)}) %collective-permute-start.1) | collective-permute-done | bytes 65568 | tf_op jit(solution)/shard_map/ppermute | solution.py:345
  31.3 0.0 collective-permute-done.one
  31.3 0.0 all-to-all-done.message
  31.3 1.3 serve.1
  32.7 0.0 copy-start
  32.7 0.0 copy-start.1
  32.7 0.0 copy-start.3
  32.7 0.0 copy-start.4
  32.7 0.0 copy-start.6
  32.7 35.5 %all_to_all.35.blocks = bf16[32,8,32,128]{3,2,1,0:T(8,128)(2,1)S(1)} all-to-all(bf16[32,8,32,128]{3,2,1,0:T(8,128)(2,1)S(1)} %get-tuple-element.18), channel_id=1, replica_groups=mesh['y4'=4,'y2'=2,'c'=2,'z4'=4,'z2'=2,'x'=4] {'y2','c','z2','x'}, dimensions={0} | all-to-all | bytes 4194304 | tf_op jit(solution)/shard_map/all_to_all | solution.py:24
  68.2 0.0 copy-done
  68.3 0.0 copy-done.3
  68.3 0.0 copy-start.2
  68.3 0.0 copy-start.5
  68.3 2.3 %density.1 = (f32[4,256]{1,0:T(4,128)}, f32[4,256]{1,0:T(4,128)S(1)}, f32[16,1,32]{2,1,0:T(1,128)S(1)}) custom-call(s32[4,16]{1,0:T(4,128)S(1)} %copy-done.4, s32[4]{0:T(128)S(1)} %copy-done.6, bf16[4,256,512]{2,1,0:T(8,128)(2,1)S(1)} %copy-done, bf16[32,8,32,128]{3,2,1,0:T(8,128)(2,1)S(1)} %all_to_all.35.blocks, f32[4,256]{1,0:T(4,128)S(1)} %copy-done.1, ...), custom_call_target="tpu_custom_call" | custom-call | tf_op jit(solution)/shard_map/density/pallas_call | solution.py:361
  70.6 14.0 %all_to_all.36.near = f32[16,1,32]{2,1,0:T(1,128)S(1)} all-to-all(f32[16,1,32]{2,1,0:T(1,128)S(1)} %get-tuple-element.19), channel_id=1, replica_groups=mesh['y4'=4,'y2'=2,'c'=2,'z4'=4,'z2'=2,'x'=4] {'y4','y2','c'}, dimensions={0} | all-to-all | bytes 4096 | tf_op jit(solution)/shard_map/all_to_all | solution.py:24
  84.6 0.7 relay.1
  85.4 6.6 %all-to-all-start.3 = ((f32[32,1,512]{2,1,0:T(1,128)}), f32[32,1,512]{2,1,0:T(1,128)S(1)}, u32[]{:S(2)}, u32[]{:S(2)}) async-start(f32[32,1,512]{2,1,0:T(1,128)} %relay.1), calls=%async_computation.3 | async-start | bytes 131072 | tf_op jit(solution)/shard_map/all_to_all | solution.py:24
  92.0 4.9 %geometry.1 = (bf16[4,256,128]{2,1,0:T(8,128)(2,1)S(1)}, bf16[4,512,256]{2,1,0:T(8,128)(2,1)S(1)}, f32[4,8,256,128]{3,2,1,0:T(8,128)}) custom-call(s32[4]{0:T(128)S(1)} %copy-done.6, f32[3,1000]{1,0:T(4,128)S(1)} %copy-done.2, f32[3,4,256]{2,1,0:T(4,128)S(1)} %copy-done.3, f32[3,8,128]{2,1,0:T(8,128)S(1)} %bitcast.10, bf16[4,256,512]{2,1,0:T(8,128)(2,1)S(1)} %copy-done), custom_call_target="tpu_custom_call" | custom-call | flops 20000000 | bytes 6291456 | tf_op jit(solution)/shard_map/geometry/pallas_call | solution.py:309
  96.8 3.9 %all-to-all-done.3.shares = f32[32,1,512]{2,1,0:T(1,128)S(1)} async-done(((f32[32,1,512]{2,1,0:T(1,128)}), f32[32,1,512]{2,1,0:T(1,128)S(1)}, u32[]{:S(2)}, u32[]{:S(2)}) %all-to-all-start.3) | async-done | bytes 65568 | tf_op jit(solution)/shard_map/all_to_all | solution.py:24
  100.7 5.2 %terms.1 = (f32[4,1000]{1,0:T(4,128)}, bf16[32,8,32,128]{3,2,1,0:T(8,128)(2,1)S(1)}) custom-call(s32[4,16]{1,0:T(4,128)S(1)} %copy-done.4, f32[32,1,512]{2,1,0:T(1,128)S(1)} %all-to-all-done.3.shares, f32[4,256]{1,0:T(4,128)S(1)} %get-tuple-element.20.rho, f32[4,256]{1,0:T(4,128)S(1)} %copy-done.1, f32[4,256]{1,0:T(4,128)S(1)} %copy-done.5, ...), custom_call_target="tpu_custom_call" | custom-call | tf_op jit(solution)/shard_map/terms/pallas_call | solution.py:383
  106.0 31.6 %all_to_all.37.received = bf16[32,8,32,128]{3,2,1,0:T(8,128)(2,1)S(1)} all-to-all(bf16[32,8,32,128]{3,2,1,0:T(8,128)(2,1)S(1)} %get-tuple-element.24), channel_id=1, replica_groups=mesh['y4'=4,'y2'=2,'c'=2,'z4'=4,'z2'=2,'x'=4] {'y2','c','z2','x'}, dimensions={0} | all-to-all | bytes 4194304 | tf_op jit(solution)/shard_map/all_to_all | solution.py:24
  137.5 1.9 %collect.1 = bf16[16,64,128]{2,1,0:T(8,128)(2,1)S(1)} custom-call(s32[32,1,128]{2,1,0:T(1,128)S(1)} %get-tuple-element.17.asked, bf16[32,8,32,128]{3,2,1,0:T(8,128)(2,1)S(1)} %all_to_all.37.received), custom_call_target="tpu_custom_call" | custom-call | tf_op jit(solution)/shard_map/collect/pallas_call | solution.py:414
  139.4 16.6 %all_to_all.38.received = bf16[16,64,128]{2,1,0:T(8,128)(2,1)S(1)} all-to-all(bf16[16,64,128]{2,1,0:T(8,128)(2,1)S(1)} %collect.1), channel_id=1, replica_groups=mesh['y4'=4,'y2'=2,'c'=2,'z4'=4,'z2'=2,'x'=4] {'y4','z4'}, dimensions={0} | all-to-all | bytes 524288 | tf_op jit(solution)/shard_map/all_to_all | solution.py:24
  156.1 18.0 %all_to_all.39 = bf16[16,64,128]{2,1,0:T(8,128)(2,1)S(1)} all-to-all(bf16[16,64,128]{2,1,0:T(8,128)(2,1)S(1)} %settle.1), channel_id=1, replica_groups=mesh['y4'=4,'y2'=2,'c'=2,'z4'=4,'z2'=2,'x'=4] {'y4','y2','c'}, dimensions={0} | all-to-all | bytes 524288 | tf_op jit(solution)/shard_map/all_to_all | solution.py:24
  174.1 0.8 copy.12
  (8 shorter events, 0.1 us)
Async XLA Ops:
  2.1 29.3 %all-to-all-start = ((s32[32,1,1024]{2,1,0:T(1,128)}), s32[32,1,1024]{2,1,0:T(1,128)S(1)}, u32[]{:S(2)}, u32[]{:S(2)}) async-start(s32[32,1,1024]{2,1,0:T(1,128)} %get-tuple-element.15), calls=%async_computation | async-start | bytes 262144 | tf_op jit(solution)/shard_map/all_to_all | solution.py:24
  12.5 14.3 %collective-permute-start.2 = (bf16[8,32,128]{2,1,0:T(8,128)(2,1)S(1)}, bf16[8,32,128]{2,1,0:T(8,128)(2,1)S(1)}, u32[]{:S(2)}, u32[]{:S(2)}) collective-permute-start(bf16[8,32,128]{2,1,0:T(8,128)(2,1)S(1)} %get-tuple-element.16.own), channel_id=1, source_target_pairs={{0,24},{8,0},{16,8},{24,16},{1,25},{9,1},{17,9},{25,17},{2,26},{10... | collective-permute-start | bytes 196616 | tf_op jit(solution)/shard_map/ppermute | solution.py:345
  20.6 10.7 %collective-permute-start.1 = (bf16[8,32,128]{2,1,0:T(8,128)(2,1)S(1)}, bf16[8,32,128]{2,1,0:T(8,128)(2,1)S(1)}, u32[]{:S(2)}, u32[]{:S(2)}) collective-permute-start(bf16[8,32,128]{2,1,0:T(8,128)(2,1)S(1)} %get-tuple-element.16.own), channel_id=1, source_target_pairs={{0,16},{8,24},{16,0},{24,8},{1,17},{9,25},{17,1},{25,9},{2,18},{10... | collective-permute-start | bytes 196616 | tf_op jit(solution)/shard_map/ppermute | solution.py:345
  22.6 8.8 %collective-permute-start = (bf16[8,32,128]{2,1,0:T(8,128)(2,1)S(1)}, bf16[8,32,128]{2,1,0:T(8,128)(2,1)S(1)}, u32[]{:S(2)}, u32[]{:S(2)}) collective-permute-start(bf16[8,32,128]{2,1,0:T(8,128)(2,1)S(1)} %get-tuple-element.16.own), channel_id=1, source_target_pairs={{0,8},{8,16},{16,24},{24,0},{1,9},{9,17},{17,25},{25,1},{2,10},{10... | collective-permute-start | bytes 196616 | tf_op jit(solution)/shard_map/ppermute | solution.py:345
  32.7 35.6 %copy-start = (bf16[4,256,512]{2,1,0:T(8,128)(2,1)S(1)}, bf16[4,256,512]{2,1,0:T(8,128)(2,1)}, u32[]{:S(2)}) copy-start(bf16[4,256,512]{2,1,0:T(8,128)(2,1)} %phi.5) | copy-start | bytes 3145732
  32.7 35.6 %copy-start.1 = (f32[4,256]{1,0:T(4,128)S(1)}, f32[4,256]{1,0:T(4,128)}, u32[]{:S(2)}) copy-start(f32[4,256]{1,0:T(4,128)} %weight.3) | copy-start | bytes 12292
  32.7 35.5 %copy-start.3 = (f32[3,4,256]{2,1,0:T(4,128)S(1)}, f32[3,4,256]{2,1,0:T(4,128)}, u32[]{:S(2)}) copy-start(f32[3,4,256]{2,1,0:T(4,128)} %offset.3) | copy-start | bytes 36868
  32.7 35.5 %copy-start.4 = (s32[4,16]{1,0:T(4,128)S(1)}, s32[4,16]{1,0:T(4,128)}, u32[]{:S(2)}) copy-start(s32[4,16]{1,0:T(4,128)} %needed.3) | copy-start | bytes 772
  32.7 35.5 %copy-start.6 = (s32[4]{0:T(128)S(1)}, s32[4]{0:T(128)}, u32[]{:S(2)}) copy-start(s32[4]{0:T(128)} %atom.3) | copy-start | bytes 52
  68.3 23.6 %copy-start.2 = (f32[3,1000]{1,0:T(4,128)S(1)}, f32[3,1000]{1,0:T(4,128)}, u32[]{:S(2)}) copy-start(f32[3,1000]{1,0:T(4,128)} %places.1) | copy-start | bytes 36004
  68.3 32.5 %copy-start.5 = (f32[4,256]{1,0:T(4,128)S(1)}, f32[4,256]{1,0:T(4,128)}, u32[]{:S(2)}) copy-start(f32[4,256]{1,0:T(4,128)} %exchange_part.1) | copy-start | bytes 12292
  85.4 15.4 %all-to-all-start.3 = ((f32[32,1,512]{2,1,0:T(1,128)}), f32[32,1,512]{2,1,0:T(1,128)S(1)}, u32[]{:S(2)}, u32[]{:S(2)}) async-start(f32[32,1,512]{2,1,0:T(1,128)} %relay.1), calls=%async_computation.3 | async-start | bytes 131072 | tf_op jit(solution)/shard_map/all_to_all | solution.py:24

commit v6 on v5

--- a/solution.py
+++ b/solution.py
@@ -60,20 +60,17 @@
     return jnp.maximum(asked[n, 0, (k % 2) * 32 + (k // 2) * 8 + w], 0)
 
 
-def serve_kernel(message, own, one, two, three, out, kept, asked, held, load_sems):
+def serve_kernel(message, held, out, kept, asked, load_sems):
     few = message.at[:, :, pl.ds(0, 128)]
     loads = [pltpu.make_async_copy(few, target, load_sems.at[n]) for n, target in enumerate((asked, kept))]
     for load in loads:
         load.start()
-    z4 = lax.axis_index("z4")
     w = lax.axis_index("z2") * 4 + lax.axis_index("x")
-    for shift, piece in enumerate((own, one, two, three)):
-        held[(z4 - shift) & 3] = piece[...]
     for load in loads:
         load.wait()
     for n in range(out.shape[0]):
         for k in range(8):
-            out[n, k] = held[k // 2, asked_at(asked, n, w, k)]
+            out[n, k] = held[(k // 2) * 8 + asked_at(asked, n, w, k)]
 
 
 def three_parts(value):
@@ -328,12 +325,12 @@
     message, slab = pl.pallas_call(
         prepare_kernel,
         name="prepare",
-        out_shape=(pltpu.HBM((32, 1, 1024), jnp.int32), jax.ShapeDtypeStruct((own, part, tile), BF16)),
+        out_shape=(pltpu.HBM((32, 1, 128), jnp.int32), jax.ShapeDtypeStruct((own, part, tile), BF16)),
         in_specs=[hbm, hbm],
         out_specs=(hbm, vmem(1)[0]),
         scratch_shapes=[
             pltpu.VMEM((1, 2, 32), jnp.int32),
-            pltpu.VMEM((32, 1, 1024), jnp.int32),
+            pltpu.VMEM((32, 1, 128), jnp.int32),
             pltpu.SemaphoreType.DMA((3,)),
         ],
         compiler_params=params,
@@ -342,20 +339,19 @@
         pltpu.with_memory_space_constraint(stored_density_blocks, pltpu.HBM),
     )
     message = exchange(message, COLLECT)
-    pieces = [slab] + [lax.ppermute(slab, "z4", [(i, (i + s) % 4) for i in range(4)]) for s in (1, 2, 3)]
+    pieces = lax.all_gather(slab, "z4", tiled=True)
     served, asked = pl.pallas_call(
         serve_kernel,
         name="serve",
         out_shape=(jax.ShapeDtypeStruct((32, 8, part, tile), BF16), jax.ShapeDtypeStruct((32, 1, 128), jnp.int32)),
-        in_specs=[anywhere] + vmem(4),
+        in_specs=[anywhere] + vmem(1),
         out_specs=tuple(vmem(2)),
         scratch_shapes=[
             pltpu.SMEM((32, 1, 128), jnp.int32),
-            pltpu.VMEM((4, own, part, tile), BF16),
             pltpu.SemaphoreType.DMA((2,)),
         ],
         compiler_params=params,
-    )(message, *pieces)
+    )(message, pieces)
     blocks = exchange(served, COLLECT)
 
     density, density_again, share = pl.pallas_call(

time: 175 us -> 172 us (0.983)
  blocking collectives: 116 us -> 131 us
  starting transfers between devices: 31.3 us -> 16.6 us
  waiting for transfers between devices: 8.4 us -> 3.89 us
    all_gather x0 -> x1, blocking collectives: none -> 15.3 us  [on_device(): pieces = lax.all_gather(slab, 'z4', tiled=True)]
    ppermute x3 -> x0, starting transfers between devices: 14.3 us -> none  [on_device(): lax.ppermute(slab, 'z4', [(i, (i + s) % 4) for i in range(4)])]
    ppermute x3 -> x0, waiting for transfers between devices: 4.5 us -> none  [on_device(): lax.ppermute(slab, 'z4', [(i, (i + s) % 4) for i in range(4)])]
  transfers between devices with their start and end apart: 5 -> 2, of which waited for: 2 -> 1; matrix products, arithmetic and copies ran while one was open for 0% -> 0% of each run, Pallas kernels for 3% -> 3%
where the time goes in v6:
time: 172 us; the launch traced here: 171 us
  blocking collectives  131 us (76%)
  Pallas kernels  17.8 us (10%)
  starting transfers between devices  16.6 us (10%)
  waiting for transfers between devices  3.89 us (2%)
    all_to_all x5, blocking collectives, exchange(): return lax.all_to_all(value, axes, split_axis=0, concat_axis=0, tiled=True)  116 us
    all_to_all x2, starting transfers between devices, exchange(): return lax.all_to_all(value, axes, split_axis=0, concat_axis=0, tiled=True)  16.6 us
    all_gather x1, blocking collectives, on_device(): pieces = lax.all_gather(slab, 'z4', tiled=True)  15.3 us
    pallas_call x1, Pallas kernels, on_device(): pl.pallas_call(term_kernel, name='terms', out_shape=(jax.ShapeDtypeStruct...  5.19 us
    pallas_call x1, Pallas kernels, on_device(): pl.pallas_call(geometry_kernel, name='geometry', out_shape=(jax.ShapeDtyp...  4.89 us
    all_to_all x2, waiting for transfers between devices, exchange(): return lax.all_to_all(value, axes, split_axis=0, concat_axis=0, tiled=True)  3.89 us
  transfers between devices with their start and end apart: 2, of which 1 were waited for; matrix products, arithmetic and copies ran while one was open for 0% of the time, Pallas kernels for 3%

profile of v6, /device:TPU:1, one launch (start us, length us, event | category | flops | bytes accessed | tf_op | source)
XLA Modules:
  0.0 171.1 jit_solution(1681339272489192968)
XLA Ops:
  0.6 1.4 prepare.1
  2.0 10.4 %all-to-all-start = ((s32[32,1,128]{2,1,0:T(1,128)}), s32[32,1,128]{2,1,0:T(1,128)S(1)}, u32[]{:S(2)}, u32[]{:S(2)}) async-start(s32[32,1,128]{2,1,0:T(1,128)} %get-tuple-element.15), calls=%async_computation | async-start | bytes 32768 | tf_op jit(solution)/shard_map/all_to_all | solution.py:24
  12.4 15.3 %all_gather.3.held = bf16[32,32,128]{2,1,0:T(8,128)(2,1)S(1)} all-gather(bf16[8,32,128]{2,1,0:T(8,128)(2,1)S(1)} %get-tuple-element.16), channel_id=1, replica_groups=mesh['y4'=4,'y2'=2,'c'=2,'z4'=4,'z2'=2,'x'=4] {'z4'}, dimensions={0}, use_global_device_ids=true | all-gather | bytes 327680 | tf_op jit(solution)/shard_map/all_gather | solution.py:342
  27.7 0.0 all-to-all-done.message
  27.7 1.3 serve.1
  29.1 0.0 copy-start
  29.1 0.0 copy-start.1
  29.1 0.0 copy-start.3
  29.1 0.0 copy-start.4
  29.1 0.0 copy-start.6
  29.2 35.7 %all_to_all.35.blocks = bf16[32,8,32,128]{3,2,1,0:T(8,128)(2,1)S(1)} all-to-all(bf16[32,8,32,128]{3,2,1,0:T(8,128)(2,1)S(1)} %get-tuple-element.18), channel_id=1, replica_groups=mesh['y4'=4,'y2'=2,'c'=2,'z4'=4,'z2'=2,'x'=4] {'y2','c','z2','x'}, dimensions={0} | all-to-all | bytes 4194304 | tf_op jit(solution)/shard_map/all_to_all | solution.py:24
  64.9 0.0 copy-done
  64.9 0.0 copy-done.1
  64.9 0.0 copy-done.3
  64.9 0.0 copy-done.4
  64.9 0.0 copy-done.6
  64.9 0.0 copy-start.2
  64.9 0.0 copy-start.5
  64.9 2.3 %density.1 = (f32[4,256]{1,0:T(4,128)}, f32[4,256]{1,0:T(4,128)S(1)}, f32[16,1,32]{2,1,0:T(1,128)S(1)}) custom-call(s32[4,16]{1,0:T(4,128)S(1)} %copy-done.4, s32[4]{0:T(128)S(1)} %copy-done.6, bf16[4,256,512]{2,1,0:T(8,128)(2,1)S(1)} %copy-done, bf16[32,8,32,128]{3,2,1,0:T(8,128)(2,1)S(1)} %all_to_all.35.blocks, f32[4,256]{1,0:T(4,128)S(1)} %copy-done.1, ...), custom_call_target="tpu_custom_call" | custom-call | tf_op jit(solution)/shard_map/density/pallas_call | solution.py:357
  67.2 14.0 %all_to_all.36.near = f32[16,1,32]{2,1,0:T(1,128)S(1)} all-to-all(f32[16,1,32]{2,1,0:T(1,128)S(1)} %get-tuple-element.19), channel_id=1, replica_groups=mesh['y4'=4,'y2'=2,'c'=2,'z4'=4,'z2'=2,'x'=4] {'y4','y2','c'}, dimensions={0} | all-to-all | bytes 4096 | tf_op jit(solution)/shard_map/all_to_all | solution.py:24
  81.3 0.7 relay.1
  82.0 6.2 %all-to-all-start.3 = ((f32[32,1,512]{2,1,0:T(1,128)}), f32[32,1,512]{2,1,0:T(1,128)S(1)}, u32[]{:S(2)}, u32[]{:S(2)}) async-start(f32[32,1,512]{2,1,0:T(1,128)} %relay.1), calls=%async_computation.3 | async-start | bytes 131072 | tf_op jit(solution)/shard_map/all_to_all | solution.py:24
  88.2 0.0 copy-done.2
  88.2 4.9 %geometry.1 = (bf16[4,256,128]{2,1,0:T(8,128)(2,1)S(1)}, bf16[4,512,256]{2,1,0:T(8,128)(2,1)S(1)}, f32[4,8,256,128]{3,2,1,0:T(8,128)}) custom-call(s32[4]{0:T(128)S(1)} %copy-done.6, f32[3,1000]{1,0:T(4,128)S(1)} %copy-done.2, f32[3,4,256]{2,1,0:T(4,128)S(1)} %copy-done.3, f32[3,8,128]{2,1,0:T(8,128)S(1)} %bitcast.10, bf16[4,256,512]{2,1,0:T(8,128)(2,1)S(1)} %copy-done), custom_call_target="tpu_custom_call" | custom-call | flops 20000000 | bytes 6291456 | tf_op jit(solution)/shard_map/geometry/pallas_call | solution.py:306
  93.1 3.9 %all-to-all-done.3.shares = f32[32,1,512]{2,1,0:T(1,128)S(1)} async-done(((f32[32,1,512]{2,1,0:T(1,128)}), f32[32,1,512]{2,1,0:T(1,128)S(1)}, u32[]{:S(2)}, u32[]{:S(2)}) %all-to-all-start.3) | async-done | bytes 65568 | tf_op jit(solution)/shard_map/all_to_all | solution.py:24
  97.0 0.0 copy-done.5
  97.0 5.2 %terms.1 = (f32[4,1000]{1,0:T(4,128)}, bf16[32,8,32,128]{3,2,1,0:T(8,128)(2,1)S(1)}) custom-call(s32[4,16]{1,0:T(4,128)S(1)} %copy-done.4, f32[32,1,512]{2,1,0:T(1,128)S(1)} %all-to-all-done.3.shares, f32[4,256]{1,0:T(4,128)S(1)} %get-tuple-element.20.rho, f32[4,256]{1,0:T(4,128)S(1)} %copy-done.1, f32[4,256]{1,0:T(4,128)S(1)} %copy-done.5, ...), custom_call_target="tpu_custom_call" | custom-call | tf_op jit(solution)/shard_map/terms/pallas_call | solution.py:379
  102.2 31.6 %all_to_all.37.received = bf16[32,8,32,128]{3,2,1,0:T(8,128)(2,1)S(1)} all-to-all(bf16[32,8,32,128]{3,2,1,0:T(8,128)(2,1)S(1)} %get-tuple-element.24), channel_id=1, replica_groups=mesh['y4'=4,'y2'=2,'c'=2,'z4'=4,'z2'=2,'x'=4] {'y2','c','z2','x'}, dimensions={0} | all-to-all | bytes 4194304 | tf_op jit(solution)/shard_map/all_to_all | solution.py:24
  133.8 1.9 %collect.1 = bf16[16,64,128]{2,1,0:T(8,128)(2,1)S(1)} custom-call(s32[32,1,128]{2,1,0:T(1,128)S(1)} %get-tuple-element.17.asked, bf16[32,8,32,128]{3,2,1,0:T(8,128)(2,1)S(1)} %all_to_all.37.received), custom_call_target="tpu_custom_call" | custom-call | tf_op jit(solution)/shard_map/collect/pallas_call | solution.py:410
  135.6 16.6 %all_to_all.38.received = bf16[16,64,128]{2,1,0:T(8,128)(2,1)S(1)} all-to-all(bf16[16,64,128]{2,1,0:T(8,128)(2,1)S(1)} %collect.1), channel_id=1, replica_groups=mesh['y4'=4,'y2'=2,'c'=2,'z4'=4,'z2'=2,'x'=4] {'y4','z4'}, dimensions={0} | all-to-all | bytes 524288 | tf_op jit(solution)/shard_map/all_to_all | solution.py:24
  152.3 18.0 %all_to_all.39 = bf16[16,64,128]{2,1,0:T(8,128)(2,1)S(1)} all-to-all(bf16[16,64,128]{2,1,0:T(8,128)(2,1)S(1)} %settle.1), channel_id=1, replica_groups=mesh['y4'=4,'y2'=2,'c'=2,'z4'=4,'z2'=2,'x'=4] {'y4','y2','c'}, dimensions={0} | all-to-all | bytes 524288 | tf_op jit(solution)/shard_map/all_to_all | solution.py:24
  170.4 0.8 copy.13
  (3 shorter events, 0.1 us)
Async XLA Ops:
  2.0 25.7 %all-to-all-start = ((s32[32,1,128]{2,1,0:T(1,128)}), s32[32,1,128]{2,1,0:T(1,128)S(1)}, u32[]{:S(2)}, u32[]{:S(2)}) async-start(s32[32,1,128]{2,1,0:T(1,128)} %get-tuple-element.15), calls=%async_computation | async-start | bytes 32768 | tf_op jit(solution)/shard_map/all_to_all | solution.py:24
  29.1 35.8 %copy-start = (bf16[4,256,512]{2,1,0:T(8,128)(2,1)S(1)}, bf16[4,256,512]{2,1,0:T(8,128)(2,1)}, u32[]{:S(2)}) copy-start(bf16[4,256,512]{2,1,0:T(8,128)(2,1)} %phi.5) | copy-start | bytes 3145732
  29.1 35.8 %copy-start.1 = (f32[4,256]{1,0:T(4,128)S(1)}, f32[4,256]{1,0:T(4,128)}, u32[]{:S(2)}) copy-start(f32[4,256]{1,0:T(4,128)} %weight.3) | copy-start | bytes 12292
  29.1 35.8 %copy-start.3 = (f32[3,4,256]{2,1,0:T(4,128)S(1)}, f32[3,4,256]{2,1,0:T(4,128)}, u32[]{:S(2)}) copy-start(f32[3,4,256]{2,1,0:T(4,128)} %offset.3) | copy-start | bytes 36868
  29.1 35.8 %copy-start.4 = (s32[4,16]{1,0:T(4,128)S(1)}, s32[4,16]{1,0:T(4,128)}, u32[]{:S(2)}) copy-start(s32[4,16]{1,0:T(4,128)} %needed.3) | copy-start | bytes 772
  29.1 35.8 %copy-start.6 = (s32[4]{0:T(128)S(1)}, s32[4]{0:T(128)}, u32[]{:S(2)}) copy-start(s32[4]{0:T(128)} %atom.3) | copy-start | bytes 52
  64.9 23.3 %copy-start.2 = (f32[3,1000]{1,0:T(4,128)S(1)}, f32[3,1000]{1,0:T(4,128)}, u32[]{:S(2)}) copy-start(f32[3,1000]{1,0:T(4,128)} %places.1) | copy-start | bytes 36004
  64.9 32.1 %copy-start.5 = (f32[4,256]{1,0:T(4,128)S(1)}, f32[4,256]{1,0:T(4,128)}, u32[]{:S(2)}) copy-start(f32[4,256]{1,0:T(4,128)} %exchange_part.1) | copy-start | bytes 12292
  82.0 15.0 %all-to-all-start.3 = ((f32[32,1,512]{2,1,0:T(1,128)}), f32[32,1,512]{2,1,0:T(1,128)S(1)}, u32[]{:S(2)}, u32[]{:S(2)}) async-start(f32[32,1,512]{2,1,0:T(1,128)} %relay.1), calls=%async_computation.3 | async-start | bytes 131072 | tf_op jit(solution)/shard_map/all_to_all | solution.py:24

commit v7 on v6

--- a/solution.py
+++ b/solution.py
@@ -13,6 +13,8 @@
 GRP_DEV = GRP + DEV
 COLLECT = ("y2", "c", "z2", "x")
 SETTLE = ("y4", "z4")
+NEAR = ("c", "x")
+FAR = ("y4", "y2", "z4", "z2")
 
 F32 = jnp.float32
 BF16 = jnp.bfloat16
@@ -360,7 +362,7 @@
         out_shape=(
             jax.ShapeDtypeStruct((batches, points), F32),
             jax.ShapeDtypeStruct((batches, points), F32),
-            jax.ShapeDtypeStruct((16, 1, each), F32),
+            jax.ShapeDtypeStruct((8, 1, each), F32),
         ),
         in_specs=smem(2) + vmem(4),
         out_specs=tuple(vmem(3)),
@@ -371,11 +373,11 @@
     shares = pl.pallas_call(
         relay_kernel,
         name="relay",
-        out_shape=jax.ShapeDtypeStruct((32, 1, 16 * each), F32),
+        out_shape=jax.ShapeDtypeStruct((64, 1, 8 * each), F32),
         in_specs=vmem(1),
         out_specs=vmem(1)[0],
         compiler_params=params,
-    )(exchange(share, GRP))
+    )(exchange(share, NEAR))
     multipoles, outgoing = pl.pallas_call(
         term_kernel,
         name="terms",
@@ -395,7 +397,7 @@
         compiler_params=params,
     )(
         batch_blocks,
-        exchange(shares, DEV),
+        exchange(shares, FAR),
         density_again,
         point_weight,
         exchange_kernel,

time: 172 us -> 172 us (level)
  blocking collectives: 131 us -> 125 us
  starting transfers between devices: 16.6 us -> 20.9 us
  waiting for transfers between devices: 3.89 us -> 6.19 us
    all_to_all x5, blocking collectives: 116 us -> 110 us  [exchange(): return lax.all_to_all(value, axes, split_axis=0, concat_axis=0, tiled=True)]
    all_to_all x2, starting transfers between devices: 16.6 us -> 20.9 us  [exchange(): return lax.all_to_all(value, axes, split_axis=0, concat_axis=0, tiled=True)]
    all_to_all x2, waiting for transfers between devices: 3.89 us -> 6.19 us  [exchange(): return lax.all_to_all(value, axes, split_axis=0, concat_axis=0, tiled=True)]
where the time goes in v7:
time: 172 us
  blocking collectives  125 us (73%)
  starting transfers between devices  20.9 us (12%)
  Pallas kernels  17.8 us (10%)
  waiting for transfers between devices  6.19 us (4%)
    all_to_all x5, blocking collectives, exchange(): return lax.all_to_all(value, axes, split_axis=0, concat_axis=0, tiled=True)  110 us
    all_to_all x2, starting transfers between devices, exchange(): return lax.all_to_all(value, axes, split_axis=0, concat_axis=0, tiled=True)  20.9 us
    all_gather x1, blocking collectives, on_device(): pieces = lax.all_gather(slab, 'z4', tiled=True)  15.3 us
    all_to_all x2, waiting for transfers between devices, exchange(): return lax.all_to_all(value, axes, split_axis=0, concat_axis=0, tiled=True)  6.19 us
    pallas_call x1, Pallas kernels, on_device(): pl.pallas_call(term_kernel, name='terms', out_shape=(jax.ShapeDtypeStruct...  5.27 us
    pallas_call x1, Pallas kernels, on_device(): pl.pallas_call(geometry_kernel, name='geometry', out_shape=(jax.ShapeDtyp...  4.89 us
  transfers between devices with their start and end apart: 2, of which 1 were waited for; matrix products, arithmetic and copies ran while one was open for 0% of the time, Pallas kernels for 3%

profile of v7, /device:TPU:1, one launch (start us, length us, event | category | flops | bytes accessed | tf_op | source)
XLA Modules:
  0.0 171.7 jit_solution(7943536342704722220)
XLA Ops:
  0.6 1.4 prepare.1
  2.0 10.4 %all-to-all-start = ((s32[32,1,128]{2,1,0:T(1,128)}), s32[32,1,128]{2,1,0:T(1,128)S(1)}, u32[]{:S(2)}, u32[]{:S(2)}) async-start(s32[32,1,128]{2,1,0:T(1,128)} %get-tuple-element.15), calls=%async_computation | async-start | bytes 32768 | tf_op jit(solution)/shard_map/all_to_all | solution.py:26
  12.4 15.3 %all_gather.3.held = bf16[32,32,128]{2,1,0:T(8,128)(2,1)S(1)} all-gather(bf16[8,32,128]{2,1,0:T(8,128)(2,1)S(1)} %get-tuple-element.16), channel_id=1, replica_groups=mesh['y4'=4,'y2'=2,'c'=2,'z4'=4,'z2'=2,'x'=4] {'z4'}, dimensions={0}, use_global_device_ids=true | all-gather | bytes 327680 | tf_op jit(solution)/shard_map/all_gather | solution.py:344
  27.7 0.0 all-to-all-done.message
  27.7 1.3 serve.1
  29.1 0.0 copy-start
  29.1 0.0 copy-start.1
  29.1 0.0 copy-start.3
  29.1 0.0 copy-start.4
  29.1 0.0 copy-start.6
  29.2 35.7 %all_to_all.35.blocks = bf16[32,8,32,128]{3,2,1,0:T(8,128)(2,1)S(1)} all-to-all(bf16[32,8,32,128]{3,2,1,0:T(8,128)(2,1)S(1)} %get-tuple-element.18), channel_id=1, replica_groups=mesh['y4'=4,'y2'=2,'c'=2,'z4'=4,'z2'=2,'x'=4] {'y2','c','z2','x'}, dimensions={0} | all-to-all | bytes 4194304 | tf_op jit(solution)/shard_map/all_to_all | solution.py:26
  64.9 0.0 copy-done
  64.9 0.0 copy-done.1
  64.9 0.0 copy-done.3
  64.9 0.0 copy-done.4
  64.9 0.0 copy-done.6
  64.9 0.0 copy-start.2
  64.9 0.0 copy-start.5
  64.9 2.3 %density.1 = (f32[4,256]{1,0:T(4,128)}, f32[4,256]{1,0:T(4,128)S(1)}, f32[8,1,32]{2,1,0:T(1,128)S(1)}) custom-call(s32[4,16]{1,0:T(4,128)S(1)} %copy-done.4, s32[4]{0:T(128)S(1)} %copy-done.6, bf16[4,256,512]{2,1,0:T(8,128)(2,1)S(1)} %copy-done, bf16[32,8,32,128]{3,2,1,0:T(8,128)(2,1)S(1)} %all_to_all.35.blocks, f32[4,256]{1,0:T(4,128)S(1)} %copy-done.1, ...), custom_call_target="tpu_custom_call" | custom-call | tf_op jit(solution)/shard_map/density/pallas_call | solution.py:359
  67.2 7.9 %all_to_all.36.near = f32[8,1,32]{2,1,0:T(1,128)S(1)} all-to-all(f32[8,1,32]{2,1,0:T(1,128)S(1)} %get-tuple-element.19), channel_id=1, replica_groups=mesh['y4'=4,'y2'=2,'c'=2,'z4'=4,'z2'=2,'x'=4] {'c','x'}, dimensions={0} | all-to-all | bytes 2048 | tf_op jit(solution)/shard_map/all_to_all | solution.py:26
  75.1 0.7 relay.1
  75.9 10.4 %all-to-all-start.3 = ((f32[64,1,256]{2,1,0:T(1,128)}), f32[64,1,256]{2,1,0:T(1,128)S(1)}, u32[]{:S(2)}, u32[]{:S(2)}) async-start(f32[64,1,256]{2,1,0:T(1,128)} %relay.1), calls=%async_computation.3 | async-start | bytes 131072 | tf_op jit(solution)/shard_map/all_to_all | solution.py:26
  86.3 0.0 copy-done.2
  86.4 4.9 %geometry.1 = (bf16[4,256,128]{2,1,0:T(8,128)(2,1)S(1)}, bf16[4,512,256]{2,1,0:T(8,128)(2,1)S(1)}, f32[4,8,256,128]{3,2,1,0:T(8,128)}) custom-call(s32[4]{0:T(128)S(1)} %copy-done.6, f32[3,1000]{1,0:T(4,128)S(1)} %copy-done.2, f32[3,4,256]{2,1,0:T(4,128)S(1)} %copy-done.3, f32[3,8,128]{2,1,0:T(8,128)S(1)} %bitcast.10, bf16[4,256,512]{2,1,0:T(8,128)(2,1)S(1)} %copy-done), custom_call_target="tpu_custom_call" | custom-call | flops 20000000 | bytes 6291456 | tf_op jit(solution)/shard_map/geometry/pallas_call | solution.py:308
  91.2 6.2 %all-to-all-done.3.shares = f32[64,1,256]{2,1,0:T(1,128)S(1)} async-done(((f32[64,1,256]{2,1,0:T(1,128)}), f32[64,1,256]{2,1,0:T(1,128)S(1)}, u32[]{:S(2)}, u32[]{:S(2)}) %all-to-all-start.3) | async-done | bytes 65568 | tf_op jit(solution)/shard_map/all_to_all | solution.py:26
  97.4 0.0 copy-done.5
  97.4 5.3 %terms.1 = (f32[4,1000]{1,0:T(4,128)}, bf16[32,8,32,128]{3,2,1,0:T(8,128)(2,1)S(1)}) custom-call(s32[4,16]{1,0:T(4,128)S(1)} %copy-done.4, f32[64,1,256]{2,1,0:T(1,128)S(1)} %all-to-all-done.3.shares, f32[4,256]{1,0:T(4,128)S(1)} %get-tuple-element.20.rho, f32[4,256]{1,0:T(4,128)S(1)} %copy-done.1, f32[4,256]{1,0:T(4,128)S(1)} %copy-done.5, ...), custom_call_target="tpu_custom_call" | custom-call | tf_op jit(solution)/shard_map/terms/pallas_call | solution.py:381
  102.7 31.6 %all_to_all.37.received = bf16[32,8,32,128]{3,2,1,0:T(8,128)(2,1)S(1)} all-to-all(bf16[32,8,32,128]{3,2,1,0:T(8,128)(2,1)S(1)} %get-tuple-element.24), channel_id=1, replica_groups=mesh['y4'=4,'y2'=2,'c'=2,'z4'=4,'z2'=2,'x'=4] {'y2','c','z2','x'}, dimensions={0} | all-to-all | bytes 4194304 | tf_op jit(solution)/shard_map/all_to_all | solution.py:26
  134.3 1.9 %collect.1 = bf16[16,64,128]{2,1,0:T(8,128)(2,1)S(1)} custom-call(s32[32,1,128]{2,1,0:T(1,128)S(1)} %get-tuple-element.17.asked, bf16[32,8,32,128]{3,2,1,0:T(8,128)(2,1)S(1)} %all_to_all.37.received), custom_call_target="tpu_custom_call" | custom-call | tf_op jit(solution)/shard_map/collect/pallas_call | solution.py:412
  136.2 17.1 %all_to_all.38.received = bf16[16,64,128]{2,1,0:T(8,128)(2,1)S(1)} all-to-all(bf16[16,64,128]{2,1,0:T(8,128)(2,1)S(1)} %collect.1), channel_id=1, replica_groups=mesh['y4'=4,'y2'=2,'c'=2,'z4'=4,'z2'=2,'x'=4] {'y4','z4'}, dimensions={0} | all-to-all | bytes 524288 | tf_op jit(solution)/shard_map/all_to_all | solution.py:26
  153.3 17.6 %all_to_all.39 = bf16[16,64,128]{2,1,0:T(8,128)(2,1)S(1)} all-to-all(bf16[16,64,128]{2,1,0:T(8,128)(2,1)S(1)} %settle.1), channel_id=1, replica_groups=mesh['y4'=4,'y2'=2,'c'=2,'z4'=4,'z2'=2,'x'=4] {'y4','y2','c'}, dimensions={0} | all-to-all | bytes 524288 | tf_op jit(solution)/shard_map/all_to_all | solution.py:26
  170.9 0.8 copy.13
  (3 shorter events, 0.1 us)
Async XLA Ops:
  2.0 25.7 %all-to-all-start = ((s32[32,1,128]{2,1,0:T(1,128)}), s32[32,1,128]{2,1,0:T(1,128)S(1)}, u32[]{:S(2)}, u32[]{:S(2)}) async-start(s32[32,1,128]{2,1,0:T(1,128)} %get-tuple-element.15), calls=%async_computation | async-start | bytes 32768 | tf_op jit(solution)/shard_map/all_to_all | solution.py:26
  29.1 35.8 %copy-start = (bf16[4,256,512]{2,1,0:T(8,128)(2,1)S(1)}, bf16[4,256,512]{2,1,0:T(8,128)(2,1)}, u32[]{:S(2)}) copy-start(bf16[4,256,512]{2,1,0:T(8,128)(2,1)} %phi.5) | copy-start | bytes 3145732
  29.1 35.8 %copy-start.1 = (f32[4,256]{1,0:T(4,128)S(1)}, f32[4,256]{1,0:T(4,128)}, u32[]{:S(2)}) copy-start(f32[4,256]{1,0:T(4,128)} %weight.3) | copy-start | bytes 12292
  29.1 35.8 %copy-start.3 = (f32[3,4,256]{2,1,0:T(4,128)S(1)}, f32[3,4,256]{2,1,0:T(4,128)}, u32[]{:S(2)}) copy-start(f32[3,4,256]{2,1,0:T(4,128)} %offset.3) | copy-start | bytes 36868
  29.1 35.8 %copy-start.4 = (s32[4,16]{1,0:T(4,128)S(1)}, s32[4,16]{1,0:T(4,128)}, u32[]{:S(2)}) copy-start(s32[4,16]{1,0:T(4,128)} %needed.3) | copy-start | bytes 772
  29.1 35.8 %copy-start.6 = (s32[4]{0:T(128)S(1)}, s32[4]{0:T(128)}, u32[]{:S(2)}) copy-start(s32[4]{0:T(128)} %atom.3) | copy-start | bytes 52
  64.9 21.4 %copy-start.2 = (f32[3,1000]{1,0:T(4,128)S(1)}, f32[3,1000]{1,0:T(4,128)}, u32[]{:S(2)}) copy-start(f32[3,1000]{1,0:T(4,128)} %places.1) | copy-start | bytes 36004
  64.9 32.5 %copy-start.5 = (f32[4,256]{1,0:T(4,128)S(1)}, f32[4,256]{1,0:T(4,128)}, u32[]{:S(2)}) copy-start(f32[4,256]{1,0:T(4,128)} %exchange_part.1) | copy-start | bytes 12292
  75.9 21.6 %all-to-all-start.3 = ((f32[64,1,256]{2,1,0:T(1,128)}), f32[64,1,256]{2,1,0:T(1,128)S(1)}, u32[]{:S(2)}, u32[]{:S(2)}) async-start(f32[64,1,256]{2,1,0:T(1,128)} %relay.1), calls=%async_computation.3 | async-start | bytes 131072 | tf_op jit(solution)/shard_map/all_to_all | solution.py:26

commit v8 on v7

--- a/solution.py
+++ b/solution.py
@@ -11,6 +11,7 @@
 GRP = ("y4", "y2", "c")
 DEV = ("z4", "z2", "x")
 GRP_DEV = GRP + DEV
+SERVE = ("c", "z2", "x")
 COLLECT = ("y2", "c", "z2", "x")
 SETTLE = ("y4", "z4")
 NEAR = ("c", "x")
@@ -42,7 +43,7 @@
     ask = pltpu.make_async_copy(request_far, request, sems.at[2])
     ask.start()
     part = slab.shape[1]
-    at = (lax.axis_index("c") * 2 + lax.axis_index("y2")) * part
+    at = lax.axis_index("c") * part
     own = stored.at[:, pl.ds(pl.multiple_of(at, part), part)]
     load = pltpu.make_async_copy(own, slab, sems.at[0])
     load.start()
@@ -62,17 +63,12 @@
     return jnp.maximum(asked[n, 0, (k % 2) * 32 + (k // 2) * 8 + w], 0)
 
 
-def serve_kernel(message, held, out, kept, asked, load_sems):
-    few = message.at[:, :, pl.ds(0, 128)]
-    loads = [pltpu.make_async_copy(few, target, load_sems.at[n]) for n, target in enumerate((asked, kept))]
-    for load in loads:
-        load.start()
+def serve_kernel(asked, held, out):
     w = lax.axis_index("z2") * 4 + lax.axis_index("x")
-    for load in loads:
-        load.wait()
+    first = lax.axis_index("y2") * out.shape[0]
     for n in range(out.shape[0]):
         for k in range(8):
-            out[n, k] = held[(k // 2) * 8 + asked_at(asked, n, w, k)]
+            out[n, k] = held[(k // 2) * 8 + asked_at(asked, first + n, w, k)]
 
 
 def three_parts(value):
@@ -128,9 +124,8 @@
             w, k = place_of(needed[b, p])
             i, j = p // rel, p % rel
             for c in range(2):
-                for y2 in range(2):
-                    at = i * 128 + (c * 2 + y2) * part
-                    wide[b % 2, pl.ds(at, part), pl.ds(j * 128, 128)] = blocks[(y2 * 2 + c) * 8 + w, k]
+                at = i * 128 + c * part
+                wide[b % 2, pl.ds(at, part), pl.ds(j * 128, 128)] = blocks[c * 8 + w, k]
         values = phi[b]
         product = jnp.dot(values, wide[b % 2], preferred_element_type=F32) * values.astype(F32)
         folded = product[:, :128]
@@ -297,12 +292,11 @@
     own, tile = stored_density_blocks.shape[0], stored_density_blocks.shape[1]
     atoms = atom_xyz.shape[1]
     padded = -(-atoms // 128) * 128
-    part = tile // 4
+    part = tile // 2
     chunks = padded // 128
     each = batches * VALUES
     params = pltpu.CompilerParams(vmem_limit_bytes=32 * MIB)
     hbm = pl.BlockSpec(memory_space=pltpu.HBM)
-    anywhere = pl.BlockSpec(memory_space=pl.ANY)
 
     far = jnp.pad(atom_xyz, ((0, 0), (0, padded - atoms))).reshape(3, chunks, 128)
     left, turned_phi, inverse = pl.pallas_call(
@@ -340,21 +334,17 @@
         pltpu.with_memory_space_constraint(device_request.transpose(0, 2, 1), pltpu.HBM),
         pltpu.with_memory_space_constraint(stored_density_blocks, pltpu.HBM),
     )
-    message = exchange(message, COLLECT)
+    asked = exchange(message, COLLECT)
     pieces = lax.all_gather(slab, "z4", tiled=True)
-    served, asked = pl.pallas_call(
+    served = pl.pallas_call(
         serve_kernel,
         name="serve",
-        out_shape=(jax.ShapeDtypeStruct((32, 8, part, tile), BF16), jax.ShapeDtypeStruct((32, 1, 128), jnp.int32)),
-        in_specs=[anywhere] + vmem(1),
-        out_specs=tuple(vmem(2)),
-        scratch_shapes=[
-            pltpu.SMEM((32, 1, 128), jnp.int32),
-            pltpu.SemaphoreType.DMA((2,)),
-        ],
-        compiler_params=params,
-    )(message, pieces)
-    blocks = exchange(served, COLLECT)
+        out_shape=jax.ShapeDtypeStruct((16, 8, part, tile), BF16),
+        in_specs=smem(1) + vmem(1),
+        out_specs=vmem(1)[0],
+        compiler_params=params,
+    )(asked, pieces)
+    blocks = exchange(served, SERVE)
 
     density, density_again, share = pl.pallas_call(
         density_kernel,

time: 172 us -> 172 us (level)
  blocking collectives: 125 us -> 127 us
    all_gather x1, blocking collectives: 15.3 us -> 18.3 us  [on_device(): pieces = lax.all_gather(slab, 'z4', tiled=True)]
where the time goes in v8:
time: 172 us
  blocking collectives  127 us (74%)
  starting transfers between devices  19.6 us (11%)
  Pallas kernels  17.6 us (10%)
  waiting for transfers between devices  6.21 us (4%)
    all_to_all x5, blocking collectives, exchange(): return lax.all_to_all(value, axes, split_axis=0, concat_axis=0, tiled=True)  108 us
    all_to_all x2, starting transfers between devices, exchange(): return lax.all_to_all(value, axes, split_axis=0, concat_axis=0, tiled=True)  19.6 us
    all_gather x1, blocking collectives, on_device(): pieces = lax.all_gather(slab, 'z4', tiled=True)  18.3 us
    all_to_all x2, waiting for transfers between devices, exchange(): return lax.all_to_all(value, axes, split_axis=0, concat_axis=0, tiled=True)  6.21 us
    pallas_call x1, Pallas kernels, on_device(): pl.pallas_call(term_kernel, name='terms', out_shape=(jax.ShapeDtypeStruct...  5.27 us
    pallas_call x1, Pallas kernels, on_device(): pl.pallas_call(geometry_kernel, name='geometry', out_shape=(jax.ShapeDtyp...  4.87 us
  transfers between devices with their start and end apart: 2, of which 1 were waited for; matrix products, arithmetic and copies ran while one was open for 0% of the time, Pallas kernels for 3%

profile of v8, /device:TPU:1, one launch (start us, length us, event | category | flops | bytes accessed | tf_op | source)
XLA Modules:
  0.0 171.6 jit_solution(3426882822412950037)
XLA Ops:
  0.6 1.4 prepare.1
  2.0 10.4 %all-to-all-start = ((s32[32,1,128]{2,1,0:T(1,128)}), s32[32,1,128]{2,1,0:T(1,128)S(1)}, u32[]{:S(2)}, u32[]{:S(2)}) async-start(s32[32,1,128]{2,1,0:T(1,128)} %get-tuple-element.13), calls=%async_computation | async-start | bytes 32768 | tf_op jit(solution)/shard_map/all_to_all | solution.py:27
  12.4 18.3 %all_gather.3.held = bf16[32,64,128]{2,1,0:T(8,128)(2,1)S(1)} all-gather(bf16[8,64,128]{2,1,0:T(8,128)(2,1)S(1)} %get-tuple-element.14), channel_id=1, replica_groups=mesh['y4'=4,'y2'=2,'c'=2,'z4'=4,'z2'=2,'x'=4] {'z4'}, dimensions={0}, use_global_device_ids=true | all-gather | bytes 655360 | tf_op jit(solution)/shard_map/all_gather | solution.py:338
  30.8 0.0 all-to-all-done.asked
  30.8 1.1 serve.1
  31.9 0.0 copy-start
  31.9 0.0 copy-start.1
  32.0 0.0 copy-start.3
  32.0 0.0 copy-start.4
  32.0 0.0 copy-start.6
  32.0 34.8 %all_to_all.35.blocks = bf16[16,8,64,128]{3,2,1,0:T(8,128)(2,1)S(1)} all-to-all(bf16[16,8,64,128]{3,2,1,0:T(8,128)(2,1)S(1)} %serve.1), channel_id=1, replica_groups=mesh['y4'=4,'y2'=2,'c'=2,'z4'=4,'z2'=2,'x'=4] {'c','z2','x'}, dimensions={0} | all-to-all | bytes 4194304 | tf_op jit(solution)/shard_map/all_to_all | solution.py:27
  66.8 0.0 copy-done
  66.8 0.0 copy-done.1
  66.8 0.0 copy-done.3
  66.8 0.0 copy-done.4
  66.8 0.0 copy-done.6
  66.8 0.0 copy-start.2
  66.8 0.0 copy-start.5
  66.8 2.3 %density.1 = (f32[4,256]{1,0:T(4,128)}, f32[4,256]{1,0:T(4,128)S(1)}, f32[8,1,32]{2,1,0:T(1,128)S(1)}) custom-call(s32[4,16]{1,0:T(4,128)S(1)} %copy-done.4, s32[4]{0:T(128)S(1)} %copy-done.6, bf16[4,256,512]{2,1,0:T(8,128)(2,1)S(1)} %copy-done, bf16[16,8,64,128]{3,2,1,0:T(8,128)(2,1)S(1)} %all_to_all.35.blocks, f32[4,256]{1,0:T(4,128)S(1)} %copy-done.1, ...), custom_call_target="tpu_custom_call" | custom-call | tf_op jit(solution)/shard_map/density/pallas_call | solution.py:349
  69.1 7.1 %all_to_all.36.near = f32[8,1,32]{2,1,0:T(1,128)S(1)} all-to-all(f32[8,1,32]{2,1,0:T(1,128)S(1)} %get-tuple-element.15), channel_id=1, replica_groups=mesh['y4'=4,'y2'=2,'c'=2,'z4'=4,'z2'=2,'x'=4] {'c','x'}, dimensions={0} | all-to-all | bytes 2048 | tf_op jit(solution)/shard_map/all_to_all | solution.py:27
  76.3 0.7 relay.1
  77.0 9.2 %all-to-all-start.3 = ((f32[64,1,256]{2,1,0:T(1,128)}), f32[64,1,256]{2,1,0:T(1,128)S(1)}, u32[]{:S(2)}, u32[]{:S(2)}) async-start(f32[64,1,256]{2,1,0:T(1,128)} %relay.1), calls=%async_computation.3 | async-start | bytes 131072 | tf_op jit(solution)/shard_map/all_to_all | solution.py:27
  86.2 0.0 copy-done.2
  86.3 4.9 %geometry.1 = (bf16[4,256,128]{2,1,0:T(8,128)(2,1)S(1)}, bf16[4,512,256]{2,1,0:T(8,128)(2,1)S(1)}, f32[4,8,256,128]{3,2,1,0:T(8,128)}) custom-call(s32[4]{0:T(128)S(1)} %copy-done.6, f32[3,1000]{1,0:T(4,128)S(1)} %copy-done.2, f32[3,4,256]{2,1,0:T(4,128)S(1)} %copy-done.3, f32[3,8,128]{2,1,0:T(8,128)S(1)} %bitcast.10, bf16[4,256,512]{2,1,0:T(8,128)(2,1)S(1)} %copy-done), custom_call_target="tpu_custom_call" | custom-call | flops 20000000 | bytes 6291456 | tf_op jit(solution)/shard_map/geometry/pallas_call | solution.py:302
  91.1 6.2 %all-to-all-done.3.shares = f32[64,1,256]{2,1,0:T(1,128)S(1)} async-done(((f32[64,1,256]{2,1,0:T(1,128)}), f32[64,1,256]{2,1,0:T(1,128)S(1)}, u32[]{:S(2)}, u32[]{:S(2)}) %all-to-all-start.3) | async-done | bytes 65568 | tf_op jit(solution)/shard_map/all_to_all | solution.py:27
  97.3 0.0 copy-done.5
  97.3 5.3 %terms.1 = (f32[4,1000]{1,0:T(4,128)}, bf16[32,8,32,128]{3,2,1,0:T(8,128)(2,1)S(1)}) custom-call(s32[4,16]{1,0:T(4,128)S(1)} %copy-done.4, f32[64,1,256]{2,1,0:T(1,128)S(1)} %all-to-all-done.3.shares, f32[4,256]{1,0:T(4,128)S(1)} %get-tuple-element.16.rho, f32[4,256]{1,0:T(4,128)S(1)} %copy-done.1, f32[4,256]{1,0:T(4,128)S(1)} %copy-done.5, ...), custom_call_target="tpu_custom_call" | custom-call | tf_op jit(solution)/shard_map/terms/pallas_call | solution.py:371
  102.6 31.6 %all_to_all.37.received = bf16[32,8,32,128]{3,2,1,0:T(8,128)(2,1)S(1)} all-to-all(bf16[32,8,32,128]{3,2,1,0:T(8,128)(2,1)S(1)} %get-tuple-element.20), channel_id=1, replica_groups=mesh['y4'=4,'y2'=2,'c'=2,'z4'=4,'z2'=2,'x'=4] {'y2','c','z2','x'}, dimensions={0} | all-to-all | bytes 4194304 | tf_op jit(solution)/shard_map/all_to_all | solution.py:27
  134.2 1.9 %collect.1 = bf16[16,64,128]{2,1,0:T(8,128)(2,1)S(1)} custom-call(s32[32,1,128]{2,1,0:T(1,128)S(1)} %all-to-all-done.asked, bf16[32,8,32,128]{3,2,1,0:T(8,128)(2,1)S(1)} %all_to_all.37.received), custom_call_target="tpu_custom_call" | custom-call | tf_op jit(solution)/shard_map/collect/pallas_call | solution.py:402
  136.1 17.1 %all_to_all.38.received = bf16[16,64,128]{2,1,0:T(8,128)(2,1)S(1)} all-to-all(bf16[16,64,128]{2,1,0:T(8,128)(2,1)S(1)} %collect.1), channel_id=1, replica_groups=mesh['y4'=4,'y2'=2,'c'=2,'z4'=4,'z2'=2,'x'=4] {'y4','z4'}, dimensions={0} | all-to-all | bytes 524288 | tf_op jit(solution)/shard_map/all_to_all | solution.py:27
  153.2 17.6 %all_to_all.39 = bf16[16,64,128]{2,1,0:T(8,128)(2,1)S(1)} all-to-all(bf16[16,64,128]{2,1,0:T(8,128)(2,1)S(1)} %settle.1), channel_id=1, replica_groups=mesh['y4'=4,'y2'=2,'c'=2,'z4'=4,'z2'=2,'x'=4] {'y4','y2','c'}, dimensions={0} | all-to-all | bytes 524288 | tf_op jit(solution)/shard_map/all_to_all | solution.py:27
  170.8 0.8 copy.13
  (3 shorter events, 0.1 us)
Async XLA Ops:
  2.0 28.8 %all-to-all-start = ((s32[32,1,128]{2,1,0:T(1,128)}), s32[32,1,128]{2,1,0:T(1,128)S(1)}, u32[]{:S(2)}, u32[]{:S(2)}) async-start(s32[32,1,128]{2,1,0:T(1,128)} %get-tuple-element.13), calls=%async_computation | async-start | bytes 32768 | tf_op jit(solution)/shard_map/all_to_all | solution.py:27
  31.9 34.9 %copy-start = (bf16[4,256,512]{2,1,0:T(8,128)(2,1)S(1)}, bf16[4,256,512]{2,1,0:T(8,128)(2,1)}, u32[]{:S(2)}) copy-start(bf16[4,256,512]{2,1,0:T(8,128)(2,1)} %phi.5) | copy-start | bytes 3145732
  31.9 34.9 %copy-start.1 = (f32[4,256]{1,0:T(4,128)S(1)}, f32[4,256]{1,0:T(4,128)}, u32[]{:S(2)}) copy-start(f32[4,256]{1,0:T(4,128)} %weight.3) | copy-start | bytes 12292
  32.0 34.8 %copy-start.3 = (f32[3,4,256]{2,1,0:T(4,128)S(1)}, f32[3,4,256]{2,1,0:T(4,128)}, u32[]{:S(2)}) copy-start(f32[3,4,256]{2,1,0:T(4,128)} %offset.3) | copy-start | bytes 36868
  32.0 34.8 %copy-start.4 = (s32[4,16]{1,0:T(4,128)S(1)}, s32[4,16]{1,0:T(4,128)}, u32[]{:S(2)}) copy-start(s32[4,16]{1,0:T(4,128)} %needed.3) | copy-start | bytes 772
  32.0 34.8 %copy-start.6 = (s32[4]{0:T(128)S(1)}, s32[4]{0:T(128)}, u32[]{:S(2)}) copy-start(s32[4]{0:T(128)} %atom.3) | copy-start | bytes 52
  66.8 19.4 %copy-start.2 = (f32[3,1000]{1,0:T(4,128)S(1)}, f32[3,1000]{1,0:T(4,128)}, u32[]{:S(2)}) copy-start(f32[3,1000]{1,0:T(4,128)} %places.1) | copy-start | bytes 36004
  66.8 30.5 %copy-start.5 = (f32[4,256]{1,0:T(4,128)S(1)}, f32[4,256]{1,0:T(4,128)}, u32[]{:S(2)}) copy-start(f32[4,256]{1,0:T(4,128)} %exchange_part.1) | copy-start | bytes 12292
  77.0 20.3 %all-to-all-start.3 = ((f32[64,1,256]{2,1,0:T(1,128)}), f32[64,1,256]{2,1,0:T(1,128)S(1)}, u32[]{:S(2)}, u32[]{:S(2)}) async-start(f32[64,1,256]{2,1,0:T(1,128)} %relay.1), calls=%async_computation.3 | async-start | bytes 131072 | tf_op jit(solution)/shard_map/all_to_all | solution.py:27

commit v9 on v8

--- a/solution.py
+++ b/solution.py
@@ -11,7 +11,6 @@
 GRP = ("y4", "y2", "c")
 DEV = ("z4", "z2", "x")
 GRP_DEV = GRP + DEV
-SERVE = ("c", "z2", "x")
 COLLECT = ("y2", "c", "z2", "x")
 SETTLE = ("y4", "z4")
 NEAR = ("c", "x")
@@ -43,7 +42,7 @@
     ask = pltpu.make_async_copy(request_far, request, sems.at[2])
     ask.start()
     part = slab.shape[1]
-    at = lax.axis_index("c") * part
+    at = (lax.axis_index("c") * 2 + lax.axis_index("y2")) * part
     own = stored.at[:, pl.ds(pl.multiple_of(at, part), part)]
     load = pltpu.make_async_copy(own, slab, sems.at[0])
     load.start()
@@ -65,10 +64,9 @@
 
 def serve_kernel(asked, held, out):
     w = lax.axis_index("z2") * 4 + lax.axis_index("x")
-    first = lax.axis_index("y2") * out.shape[0]
     for n in range(out.shape[0]):
         for k in range(8):
-            out[n, k] = held[(k // 2) * 8 + asked_at(asked, first + n, w, k)]
+            out[n, k] = held[(k // 2) * 8 + asked_at(asked, n, w, k)]
 
 
 def three_parts(value):
@@ -124,8 +122,9 @@
             w, k = place_of(needed[b, p])
             i, j = p // rel, p % rel
             for c in range(2):
-                at = i * 128 + c * part
-                wide[b % 2, pl.ds(at, part), pl.ds(j * 128, 128)] = blocks[c * 8 + w, k]
+                for y2 in range(2):
+                    at = i * 128 + (c * 2 + y2) * part
+                    wide[b % 2, pl.ds(at, part), pl.ds(j * 128, 128)] = blocks[(y2 * 2 + c) * 8 + w, k]
         values = phi[b]
         product = jnp.dot(values, wide[b % 2], preferred_element_type=F32) * values.astype(F32)
         folded = product[:, :128]
@@ -292,7 +291,7 @@
     own, tile = stored_density_blocks.shape[0], stored_density_blocks.shape[1]
     atoms = atom_xyz.shape[1]
     padded = -(-atoms // 128) * 128
-    part = tile // 2
+    part = tile // 4
     chunks = padded // 128
     each = batches * VALUES
     params = pltpu.CompilerParams(vmem_limit_bytes=32 * MIB)
@@ -339,12 +338,12 @@
     served = pl.pallas_call(
         serve_kernel,
         name="serve",
-        out_shape=jax.ShapeDtypeStruct((16, 8, part, tile), BF16),
+        out_shape=jax.ShapeDtypeStruct((32, 8, part, tile), BF16),
         in_specs=smem(1) + vmem(1),
         out_specs=vmem(1)[0],
         compiler_params=params,
     )(asked, pieces)
-    blocks = exchange(served, SERVE)
+    blocks = exchange(served, COLLECT)
 
     density, density_again, share = pl.pallas_call(
         density_kernel,

time: 172 us -> 172 us (level)
  blocking collectives: 127 us -> 125 us
    all_gather x1, blocking collectives: 18.3 us -> 15.3 us  [on_device(): pieces = lax.all_gather(slab, 'z4', tiled=True)]
where the time goes in v9:
time: 172 us
  blocking collectives  125 us (73%)
  starting transfers between devices  20.9 us (12%)
  Pallas kernels  17.8 us (10%)
  waiting for transfers between devices  6.21 us (4%)
    all_to_all x5, blocking collectives, exchange(): return lax.all_to_all(value, axes, split_axis=0, concat_axis=0, tiled=True)  110 us
    all_to_all x2, starting transfers between devices, exchange(): return lax.all_to_all(value, axes, split_axis=0, concat_axis=0, tiled=True)  20.9 us
    all_gather x1, blocking collectives, on_device(): pieces = lax.all_gather(slab, 'z4', tiled=True)  15.3 us
    all_to_all x2, waiting for transfers between devices, exchange(): return lax.all_to_all(value, axes, split_axis=0, concat_axis=0, tiled=True)  6.21 us
    pallas_call x1, Pallas kernels, on_device(): pl.pallas_call(term_kernel, name='terms', out_shape=(jax.ShapeDtypeStruct...  5.26 us
    pallas_call x1, Pallas kernels, on_device(): pl.pallas_call(geometry_kernel, name='geometry', out_shape=(jax.ShapeDtyp...  4.87 us
  transfers between devices with their start and end apart: 2, of which 1 were waited for; matrix products, arithmetic and copies ran while one was open for 0% of the time, Pallas kernels for 3%

profile of v9, /device:TPU:1, one launch (start us, length us, event | category | flops | bytes accessed | tf_op | source)
XLA Modules:
  0.0 171.7 jit_solution(6148797668177986479)
XLA Ops:
  0.6 1.4 prepare.1
  2.0 10.4 %all-to-all-start = ((s32[32,1,128]{2,1,0:T(1,128)}), s32[32,1,128]{2,1,0:T(1,128)S(1)}, u32[]{:S(2)}, u32[]{:S(2)}) async-start(s32[32,1,128]{2,1,0:T(1,128)} %get-tuple-element.13), calls=%async_computation | async-start | bytes 32768 | tf_op jit(solution)/shard_map/all_to_all | solution.py:26
  12.4 15.3 %all_gather.3.held = bf16[32,32,128]{2,1,0:T(8,128)(2,1)S(1)} all-gather(bf16[8,32,128]{2,1,0:T(8,128)(2,1)S(1)} %get-tuple-element.14), channel_id=1, replica_groups=mesh['y4'=4,'y2'=2,'c'=2,'z4'=4,'z2'=2,'x'=4] {'z4'}, dimensions={0}, use_global_device_ids=true | all-gather | bytes 327680 | tf_op jit(solution)/shard_map/all_gather | solution.py:337
  27.7 0.0 all-to-all-done.asked
  27.7 1.4 serve.1
  29.1 0.0 copy-start
  29.1 0.0 copy-start.1
  29.1 0.0 copy-start.3
  29.1 0.0 copy-start.4
  29.2 0.0 copy-start.6
  29.2 35.7 %all_to_all.35.blocks = bf16[32,8,32,128]{3,2,1,0:T(8,128)(2,1)S(1)} all-to-all(bf16[32,8,32,128]{3,2,1,0:T(8,128)(2,1)S(1)} %serve.1), channel_id=1, replica_groups=mesh['y4'=4,'y2'=2,'c'=2,'z4'=4,'z2'=2,'x'=4] {'y2','c','z2','x'}, dimensions={0} | all-to-all | bytes 4194304 | tf_op jit(solution)/shard_map/all_to_all | solution.py:26
  64.9 0.0 copy-done
  64.9 0.0 copy-done.1
  64.9 0.0 copy-done.3
  64.9 0.0 copy-done.4
  64.9 0.0 copy-done.6
  64.9 0.0 copy-start.2
  64.9 0.0 copy-start.5
  64.9 2.3 %density.1 = (f32[4,256]{1,0:T(4,128)}, f32[4,256]{1,0:T(4,128)S(1)}, f32[8,1,32]{2,1,0:T(1,128)S(1)}) custom-call(s32[4,16]{1,0:T(4,128)S(1)} %copy-done.4, s32[4]{0:T(128)S(1)} %copy-done.6, bf16[4,256,512]{2,1,0:T(8,128)(2,1)S(1)} %copy-done, bf16[32,8,32,128]{3,2,1,0:T(8,128)(2,1)S(1)} %all_to_all.35.blocks, f32[4,256]{1,0:T(4,128)S(1)} %copy-done.1, ...), custom_call_target="tpu_custom_call" | custom-call | tf_op jit(solution)/shard_map/density/pallas_call | solution.py:348
  67.3 7.9 %all_to_all.36.near = f32[8,1,32]{2,1,0:T(1,128)S(1)} all-to-all(f32[8,1,32]{2,1,0:T(1,128)S(1)} %get-tuple-element.15), channel_id=1, replica_groups=mesh['y4'=4,'y2'=2,'c'=2,'z4'=4,'z2'=2,'x'=4] {'c','x'}, dimensions={0} | all-to-all | bytes 2048 | tf_op jit(solution)/shard_map/all_to_all | solution.py:26
  75.2 0.7 relay.1
  75.9 10.4 %all-to-all-start.3 = ((f32[64,1,256]{2,1,0:T(1,128)}), f32[64,1,256]{2,1,0:T(1,128)S(1)}, u32[]{:S(2)}, u32[]{:S(2)}) async-start(f32[64,1,256]{2,1,0:T(1,128)} %relay.1), calls=%async_computation.3 | async-start | bytes 131072 | tf_op jit(solution)/shard_map/all_to_all | solution.py:26
  86.3 0.0 copy-done.2
  86.4 4.9 %geometry.1 = (bf16[4,256,128]{2,1,0:T(8,128)(2,1)S(1)}, bf16[4,512,256]{2,1,0:T(8,128)(2,1)S(1)}, f32[4,8,256,128]{3,2,1,0:T(8,128)}) custom-call(s32[4]{0:T(128)S(1)} %copy-done.6, f32[3,1000]{1,0:T(4,128)S(1)} %copy-done.2, f32[3,4,256]{2,1,0:T(4,128)S(1)} %copy-done.3, f32[3,8,128]{2,1,0:T(8,128)S(1)} %bitcast.10, bf16[4,256,512]{2,1,0:T(8,128)(2,1)S(1)} %copy-done), custom_call_target="tpu_custom_call" | custom-call | flops 20000000 | bytes 6291456 | tf_op jit(solution)/shard_map/geometry/pallas_call | solution.py:301
  91.2 6.2 %all-to-all-done.3.shares = f32[64,1,256]{2,1,0:T(1,128)S(1)} async-done(((f32[64,1,256]{2,1,0:T(1,128)}), f32[64,1,256]{2,1,0:T(1,128)S(1)}, u32[]{:S(2)}, u32[]{:S(2)}) %all-to-all-start.3) | async-done | bytes 65568 | tf_op jit(solution)/shard_map/all_to_all | solution.py:26
  97.5 0.0 copy-done.5
  97.5 5.3 %terms.1 = (f32[4,1000]{1,0:T(4,128)}, bf16[32,8,32,128]{3,2,1,0:T(8,128)(2,1)S(1)}) custom-call(s32[4,16]{1,0:T(4,128)S(1)} %copy-done.4, f32[64,1,256]{2,1,0:T(1,128)S(1)} %all-to-all-done.3.shares, f32[4,256]{1,0:T(4,128)S(1)} %get-tuple-element.16.rho, f32[4,256]{1,0:T(4,128)S(1)} %copy-done.1, f32[4,256]{1,0:T(4,128)S(1)} %copy-done.5, ...), custom_call_target="tpu_custom_call" | custom-call | tf_op jit(solution)/shard_map/terms/pallas_call | solution.py:370
  102.7 31.6 %all_to_all.37.received = bf16[32,8,32,128]{3,2,1,0:T(8,128)(2,1)S(1)} all-to-all(bf16[32,8,32,128]{3,2,1,0:T(8,128)(2,1)S(1)} %get-tuple-element.20), channel_id=1, replica_groups=mesh['y4'=4,'y2'=2,'c'=2,'z4'=4,'z2'=2,'x'=4] {'y2','c','z2','x'}, dimensions={0} | all-to-all | bytes 4194304 | tf_op jit(solution)/shard_map/all_to_all | solution.py:26
  134.3 1.9 %collect.1 = bf16[16,64,128]{2,1,0:T(8,128)(2,1)S(1)} custom-call(s32[32,1,128]{2,1,0:T(1,128)S(1)} %all-to-all-done.asked, bf16[32,8,32,128]{3,2,1,0:T(8,128)(2,1)S(1)} %all_to_all.37.received), custom_call_target="tpu_custom_call" | custom-call | tf_op jit(solution)/shard_map/collect/pallas_call | solution.py:401
  136.2 17.1 %all_to_all.38.received = bf16[16,64,128]{2,1,0:T(8,128)(2,1)S(1)} all-to-all(bf16[16,64,128]{2,1,0:T(8,128)(2,1)S(1)} %collect.1), channel_id=1, replica_groups=mesh['y4'=4,'y2'=2,'c'=2,'z4'=4,'z2'=2,'x'=4] {'y4','z4'}, dimensions={0} | all-to-all | bytes 524288 | tf_op jit(solution)/shard_map/all_to_all | solution.py:26
  153.3 17.6 %all_to_all.39 = bf16[16,64,128]{2,1,0:T(8,128)(2,1)S(1)} all-to-all(bf16[16,64,128]{2,1,0:T(8,128)(2,1)S(1)} %settle.1), channel_id=1, replica_groups=mesh['y4'=4,'y2'=2,'c'=2,'z4'=4,'z2'=2,'x'=4] {'y4','y2','c'}, dimensions={0} | all-to-all | bytes 524288 | tf_op jit(solution)/shard_map/all_to_all | solution.py:26
  170.9 0.8 copy.13
  (3 shorter events, 0.1 us)
Async XLA Ops:
  2.0 25.7 %all-to-all-start = ((s32[32,1,128]{2,1,0:T(1,128)}), s32[32,1,128]{2,1,0:T(1,128)S(1)}, u32[]{:S(2)}, u32[]{:S(2)}) async-start(s32[32,1,128]{2,1,0:T(1,128)} %get-tuple-element.13), calls=%async_computation | async-start | bytes 32768 | tf_op jit(solution)/shard_map/all_to_all | solution.py:26
  29.1 35.8 %copy-start = (bf16[4,256,512]{2,1,0:T(8,128)(2,1)S(1)}, bf16[4,256,512]{2,1,0:T(8,128)(2,1)}, u32[]{:S(2)}) copy-start(bf16[4,256,512]{2,1,0:T(8,128)(2,1)} %phi.5) | copy-start | bytes 3145732
  29.1 35.8 %copy-start.1 = (f32[4,256]{1,0:T(4,128)S(1)}, f32[4,256]{1,0:T(4,128)}, u32[]{:S(2)}) copy-start(f32[4,256]{1,0:T(4,128)} %weight.3) | copy-start | bytes 12292
  29.1 35.8 %copy-start.3 = (f32[3,4,256]{2,1,0:T(4,128)S(1)}, f32[3,4,256]{2,1,0:T(4,128)}, u32[]{:S(2)}) copy-start(f32[3,4,256]{2,1,0:T(4,128)} %offset.3) | copy-start | bytes 36868
  29.1 35.8 %copy-start.4 = (s32[4,16]{1,0:T(4,128)S(1)}, s32[4,16]{1,0:T(4,128)}, u32[]{:S(2)}) copy-start(s32[4,16]{1,0:T(4,128)} %needed.3) | copy-start | bytes 772
  29.2 35.8 %copy-start.6 = (s32[4]{0:T(128)S(1)}, s32[4]{0:T(128)}, u32[]{:S(2)}) copy-start(s32[4]{0:T(128)} %atom.3) | copy-start | bytes 52
  64.9 21.4 %copy-start.2 = (f32[3,1000]{1,0:T(4,128)S(1)}, f32[3,1000]{1,0:T(4,128)}, u32[]{:S(2)}) copy-start(f32[3,1000]{1,0:T(4,128)} %places.1) | copy-start | bytes 36004
  64.9 32.5 %copy-start.5 = (f32[4,256]{1,0:T(4,128)S(1)}, f32[4,256]{1,0:T(4,128)}, u32[]{:S(2)}) copy-start(f32[4,256]{1,0:T(4,128)} %exchange_part.1) | copy-start | bytes 12292
  75.9 21.6 %all-to-all-start.3 = ((f32[64,1,256]{2,1,0:T(1,128)}), f32[64,1,256]{2,1,0:T(1,128)S(1)}, u32[]{:S(2)}, u32[]{:S(2)}) async-start(f32[64,1,256]{2,1,0:T(1,128)} %relay.1), calls=%async_computation.3 | async-start | bytes 131072 | tf_op jit(solution)/shard_map/all_to_all | solution.py:26

commit v10 on v9

--- a/solution.py
+++ b/solution.py
@@ -13,8 +13,6 @@
 GRP_DEV = GRP + DEV
 COLLECT = ("y2", "c", "z2", "x")
 SETTLE = ("y4", "z4")
-NEAR = ("c", "x")
-FAR = ("y4", "y2", "z4", "z2")
 
 F32 = jnp.float32
 BF16 = jnp.bfloat16
@@ -258,7 +256,7 @@
             total[asked_at(asked, n, w, k)] += received[n, k].astype(F32)
         return 0
 
-    lax.fori_loop(0, received.shape[0], add_one, 0)
+    lax.fori_loop(0, received.shape[0], add_one, 0, unroll=4)
     for z4 in range(4):
         for h in range(4):
             two = [totals[2 * z4][2 * h + e] + totals[2 * z4 + 1][2 * h + e] for e in range(2)]
@@ -351,7 +349,7 @@
         out_shape=(
             jax.ShapeDtypeStruct((batches, points), F32),
             jax.ShapeDtypeStruct((batches, points), F32),
-            jax.ShapeDtypeStruct((8, 1, each), F32),
+            jax.ShapeDtypeStruct((16, 1, each), F32),
         ),
         in_specs=smem(2) + vmem(4),
         out_specs=tuple(vmem(3)),
@@ -362,11 +360,11 @@
     shares = pl.pallas_call(
         relay_kernel,
         name="relay",
-        out_shape=jax.ShapeDtypeStruct((64, 1, 8 * each), F32),
+        out_shape=jax.ShapeDtypeStruct((32, 1, 16 * each), F32),
         in_specs=vmem(1),
         out_specs=vmem(1)[0],
         compiler_params=params,
-    )(exchange(share, NEAR))
+    )(exchange(share, GRP))
     multipoles, outgoing = pl.pallas_call(
         term_kernel,
         name="terms",
@@ -386,7 +384,7 @@
         compiler_params=params,
     )(
         batch_blocks,
-        exchange(shares, FAR),
+        exchange(shares, DEV),
         density_again,
         point_weight,
         exchange_kernel,

time: 172 us -> 171 us (level)
  blocking collectives: 125 us -> 131 us
  starting transfers between devices: 20.9 us -> 16.6 us
  waiting for transfers between devices: 6.21 us -> 3.91 us
    all_to_all x5, blocking collectives: 110 us -> 116 us  [exchange(): return lax.all_to_all(value, axes, split_axis=0, concat_axis=0, tiled=True)]
    all_to_all x2, starting transfers between devices: 20.9 us -> 16.6 us  [exchange(): return lax.all_to_all(value, axes, split_axis=0, concat_axis=0, tiled=True)]
    all_to_all x2, waiting for transfers between devices: 6.21 us -> 3.91 us  [exchange(): return lax.all_to_all(value, axes, split_axis=0, concat_axis=0, tiled=True)]
where the time goes in v10:
time: 171 us
  blocking collectives  131 us (77%)
  Pallas kernels  17.5 us (10%)
  starting transfers between devices  16.6 us (10%)
  waiting for transfers between devices  3.91 us (2%)
    all_to_all x5, blocking collectives, exchange(): return lax.all_to_all(value, axes, split_axis=0, concat_axis=0, tiled=True)  116 us
    all_to_all x2, starting transfers between devices, exchange(): return lax.all_to_all(value, axes, split_axis=0, concat_axis=0, tiled=True)  16.6 us
    all_gather x1, blocking collectives, on_device(): pieces = lax.all_gather(slab, 'z4', tiled=True)  15.3 us
    pallas_call x1, Pallas kernels, on_device(): pl.pallas_call(term_kernel, name='terms', out_shape=(jax.ShapeDtypeStruct...  5.2 us
    pallas_call x1, Pallas kernels, on_device(): pl.pallas_call(geometry_kernel, name='geometry', out_shape=(jax.ShapeDtyp...  4.87 us
    all_to_all x2, waiting for transfers between devices, exchange(): return lax.all_to_all(value, axes, split_axis=0, concat_axis=0, tiled=True)  3.91 us
  transfers between devices with their start and end apart: 2, of which 1 were waited for; matrix products, arithmetic and copies ran while one was open for 0% of the time, Pallas kernels for 3%

profile of v10, /device:TPU:1, one launch (start us, length us, event | category | flops | bytes accessed | tf_op | source)
XLA Modules:
  0.0 170.9 jit_solution(10779378261737471989)
XLA Ops:
  0.6 1.4 prepare.1
  2.0 10.4 %all-to-all-start = ((s32[32,1,128]{2,1,0:T(1,128)}), s32[32,1,128]{2,1,0:T(1,128)S(1)}, u32[]{:S(2)}, u32[]{:S(2)}) async-start(s32[32,1,128]{2,1,0:T(1,128)} %get-tuple-element.13), calls=%async_computation | async-start | bytes 32768 | tf_op jit(solution)/shard_map/all_to_all | solution.py:24
  12.4 15.3 %all_gather.3.held = bf16[32,32,128]{2,1,0:T(8,128)(2,1)S(1)} all-gather(bf16[8,32,128]{2,1,0:T(8,128)(2,1)S(1)} %get-tuple-element.14), channel_id=1, replica_groups=mesh['y4'=4,'y2'=2,'c'=2,'z4'=4,'z2'=2,'x'=4] {'z4'}, dimensions={0}, use_global_device_ids=true | all-gather | bytes 327680 | tf_op jit(solution)/shard_map/all_gather | solution.py:335
  27.7 0.0 all-to-all-done.asked
  27.7 1.4 serve.1
  29.1 0.0 copy-start
  29.1 0.0 copy-start.1
  29.1 0.0 copy-start.3
  29.1 0.0 copy-start.4
  29.2 0.0 copy-start.6
  29.2 35.7 %all_to_all.35.blocks = bf16[32,8,32,128]{3,2,1,0:T(8,128)(2,1)S(1)} all-to-all(bf16[32,8,32,128]{3,2,1,0:T(8,128)(2,1)S(1)} %serve.1), channel_id=1, replica_groups=mesh['y4'=4,'y2'=2,'c'=2,'z4'=4,'z2'=2,'x'=4] {'y2','c','z2','x'}, dimensions={0} | all-to-all | bytes 4194304 | tf_op jit(solution)/shard_map/all_to_all | solution.py:24
  64.9 0.0 copy-done
  64.9 0.0 copy-done.1
  64.9 0.0 copy-done.3
  64.9 0.0 copy-done.4
  64.9 0.0 copy-done.6
  64.9 0.0 copy-start.2
  64.9 0.0 copy-start.5
  64.9 2.3 %density.1 = (f32[4,256]{1,0:T(4,128)}, f32[4,256]{1,0:T(4,128)S(1)}, f32[16,1,32]{2,1,0:T(1,128)S(1)}) custom-call(s32[4,16]{1,0:T(4,128)S(1)} %copy-done.4, s32[4]{0:T(128)S(1)} %copy-done.6, bf16[4,256,512]{2,1,0:T(8,128)(2,1)S(1)} %copy-done, bf16[32,8,32,128]{3,2,1,0:T(8,128)(2,1)S(1)} %all_to_all.35.blocks, f32[4,256]{1,0:T(4,128)S(1)} %copy-done.1, ...), custom_call_target="tpu_custom_call" | custom-call | tf_op jit(solution)/shard_map/density/pallas_call | solution.py:346
  67.3 14.0 %all_to_all.36.near = f32[16,1,32]{2,1,0:T(1,128)S(1)} all-to-all(f32[16,1,32]{2,1,0:T(1,128)S(1)} %get-tuple-element.15), channel_id=1, replica_groups=mesh['y4'=4,'y2'=2,'c'=2,'z4'=4,'z2'=2,'x'=4] {'y4','y2','c'}, dimensions={0} | all-to-all | bytes 4096 | tf_op jit(solution)/shard_map/all_to_all | solution.py:24
  81.3 0.7 relay.1
  82.0 6.2 %all-to-all-start.3 = ((f32[32,1,512]{2,1,0:T(1,128)}), f32[32,1,512]{2,1,0:T(1,128)S(1)}, u32[]{:S(2)}, u32[]{:S(2)}) async-start(f32[32,1,512]{2,1,0:T(1,128)} %relay.1), calls=%async_computation.3 | async-start | bytes 131072 | tf_op jit(solution)/shard_map/all_to_all | solution.py:24
  88.2 0.0 copy-done.2
  88.2 4.9 %geometry.1 = (bf16[4,256,128]{2,1,0:T(8,128)(2,1)S(1)}, bf16[4,512,256]{2,1,0:T(8,128)(2,1)S(1)}, f32[4,8,256,128]{3,2,1,0:T(8,128)}) custom-call(s32[4]{0:T(128)S(1)} %copy-done.6, f32[3,1000]{1,0:T(4,128)S(1)} %copy-done.2, f32[3,4,256]{2,1,0:T(4,128)S(1)} %copy-done.3, f32[3,8,128]{2,1,0:T(8,128)S(1)} %bitcast.10, bf16[4,256,512]{2,1,0:T(8,128)(2,1)S(1)} %copy-done), custom_call_target="tpu_custom_call" | custom-call | flops 20000000 | bytes 6291456 | tf_op jit(solution)/shard_map/geometry/pallas_call | solution.py:299
  93.1 3.9 %all-to-all-done.3.shares = f32[32,1,512]{2,1,0:T(1,128)S(1)} async-done(((f32[32,1,512]{2,1,0:T(1,128)}), f32[32,1,512]{2,1,0:T(1,128)S(1)}, u32[]{:S(2)}, u32[]{:S(2)}) %all-to-all-start.3) | async-done | bytes 65568 | tf_op jit(solution)/shard_map/all_to_all | solution.py:24
  97.0 0.0 copy-done.5
  97.0 5.2 %terms.1 = (f32[4,1000]{1,0:T(4,128)}, bf16[32,8,32,128]{3,2,1,0:T(8,128)(2,1)S(1)}) custom-call(s32[4,16]{1,0:T(4,128)S(1)} %copy-done.4, f32[32,1,512]{2,1,0:T(1,128)S(1)} %all-to-all-done.3.shares, f32[4,256]{1,0:T(4,128)S(1)} %get-tuple-element.16.rho, f32[4,256]{1,0:T(4,128)S(1)} %copy-done.1, f32[4,256]{1,0:T(4,128)S(1)} %copy-done.5, ...), custom_call_target="tpu_custom_call" | custom-call | tf_op jit(solution)/shard_map/terms/pallas_call | solution.py:368
  102.2 31.6 %all_to_all.37.received = bf16[32,8,32,128]{3,2,1,0:T(8,128)(2,1)S(1)} all-to-all(bf16[32,8,32,128]{3,2,1,0:T(8,128)(2,1)S(1)} %get-tuple-element.20), channel_id=1, replica_groups=mesh['y4'=4,'y2'=2,'c'=2,'z4'=4,'z2'=2,'x'=4] {'y2','c','z2','x'}, dimensions={0} | all-to-all | bytes 4194304 | tf_op jit(solution)/shard_map/all_to_all | solution.py:24
  133.8 1.6 collect.1
  135.4 16.6 %all_to_all.38.received = bf16[16,64,128]{2,1,0:T(8,128)(2,1)S(1)} all-to-all(bf16[16,64,128]{2,1,0:T(8,128)(2,1)S(1)} %collect.1), channel_id=1, replica_groups=mesh['y4'=4,'y2'=2,'c'=2,'z4'=4,'z2'=2,'x'=4] {'y4','z4'}, dimensions={0} | all-to-all | bytes 524288 | tf_op jit(solution)/shard_map/all_to_all | solution.py:24
  152.0 18.0 %all_to_all.39 = bf16[16,64,128]{2,1,0:T(8,128)(2,1)S(1)} all-to-all(bf16[16,64,128]{2,1,0:T(8,128)(2,1)S(1)} %settle.1), channel_id=1, replica_groups=mesh['y4'=4,'y2'=2,'c'=2,'z4'=4,'z2'=2,'x'=4] {'y4','y2','c'}, dimensions={0} | all-to-all | bytes 524288 | tf_op jit(solution)/shard_map/all_to_all | solution.py:24
  170.1 0.8 copy.13
  (3 shorter events, 0.1 us)
Async XLA Ops:
  2.0 25.7 %all-to-all-start = ((s32[32,1,128]{2,1,0:T(1,128)}), s32[32,1,128]{2,1,0:T(1,128)S(1)}, u32[]{:S(2)}, u32[]{:S(2)}) async-start(s32[32,1,128]{2,1,0:T(1,128)} %get-tuple-element.13), calls=%async_computation | async-start | bytes 32768 | tf_op jit(solution)/shard_map/all_to_all | solution.py:24
  29.1 35.8 %copy-start = (bf16[4,256,512]{2,1,0:T(8,128)(2,1)S(1)}, bf16[4,256,512]{2,1,0:T(8,128)(2,1)}, u32[]{:S(2)}) copy-start(bf16[4,256,512]{2,1,0:T(8,128)(2,1)} %phi.5) | copy-start | bytes 3145732
  29.1 35.8 %copy-start.1 = (f32[4,256]{1,0:T(4,128)S(1)}, f32[4,256]{1,0:T(4,128)}, u32[]{:S(2)}) copy-start(f32[4,256]{1,0:T(4,128)} %weight.3) | copy-start | bytes 12292
  29.1 35.8 %copy-start.3 = (f32[3,4,256]{2,1,0:T(4,128)S(1)}, f32[3,4,256]{2,1,0:T(4,128)}, u32[]{:S(2)}) copy-start(f32[3,4,256]{2,1,0:T(4,128)} %offset.3) | copy-start | bytes 36868
  29.1 35.8 %copy-start.4 = (s32[4,16]{1,0:T(4,128)S(1)}, s32[4,16]{1,0:T(4,128)}, u32[]{:S(2)}) copy-start(s32[4,16]{1,0:T(4,128)} %needed.3) | copy-start | bytes 772
  29.2 35.8 %copy-start.6 = (s32[4]{0:T(128)S(1)}, s32[4]{0:T(128)}, u32[]{:S(2)}) copy-start(s32[4]{0:T(128)} %atom.3) | copy-start | bytes 52
  64.9 23.3 %copy-start.2 = (f32[3,1000]{1,0:T(4,128)S(1)}, f32[3,1000]{1,0:T(4,128)}, u32[]{:S(2)}) copy-start(f32[3,1000]{1,0:T(4,128)} %places.1) | copy-start | bytes 36004
  64.9 32.1 %copy-start.5 = (f32[4,256]{1,0:T(4,128)S(1)}, f32[4,256]{1,0:T(4,128)}, u32[]{:S(2)}) copy-start(f32[4,256]{1,0:T(4,128)} %exchange_part.1) | copy-start | bytes 12292
  82.0 15.0 %all-to-all-start.3 = ((f32[32,1,512]{2,1,0:T(1,128)}), f32[32,1,512]{2,1,0:T(1,128)S(1)}, u32[]{:S(2)}, u32[]{:S(2)}) async-start(f32[32,1,512]{2,1,0:T(1,128)} %relay.1), calls=%async_computation.3 | async-start | bytes 131072 | tf_op jit(solution)/shard_map/all_to_all | solution.py:24
